TPU v7x, 256 devices: a whole 4x4x8 slice. The times are simulated.
256 devices in a mesh: scene: 32 (over x, y, core), kd: 8 (over z).
Axes of the slice: x: 4, y: 4, z: 8, core: 2. Of those that a mesh axis runs over, the one named last changes fastest.
Arguments:
- features: bfloat16 [32, 32, 512, 128], P('scene', 'kd'), may hold values from -6 to 6
- send_faces: int32 [32, 8, 3, 1], P('scene', 'kd'), may hold values from 0 to 23, as said below
- face_source: int32 [32, 32, 6], P('scene', 'kd'), may hold values from 0 to 27, as said below
- cotangent: bfloat16 [32, 32, 64, 256], P('scene', 'kd'), may hold values from -12 to 12
- conv_one: bfloat16 [7, 128, 128], replicated, may hold values from -0.1875 to 0.1875
- down_weight: bfloat16 [1024, 256], replicated, may hold values from -0.1875 to 0.1875
- conv_two: bfloat16 [7, 256, 256], replicated, may hold values from -0.125 to 0.125
Outputs:
- encoded: bfloat16 [32, 32, 64, 256], P('scene', 'kd')
- grad_conv_one: float32 [7, 128, 128], replicated
- grad_down: float32 [1024, 256], replicated
- grad_conv_two: float32 [7, 256, 256], replicated
Inputs may be any that keep to these rules, and one draw needn't show every extreme that they name: `send_faces`: entry [i, t] names face 6 b + s of the sender's own brick b; across bit i every device sends exactly one face, of side 2 (i mod 3) + 1 where its bit i is 0 and of side 2 (i mod 3) where it is 1; no face is named twice on a device. `face_source`: for brick b and direction s: a value under 6 * 4 is a local face, of the side opposite s; 24 + i + t is slot t received across bit i; 27 is no neighbour. The relation is symmetric: where direction s of brick b takes a face of brick b2, direction opposite s of b2 takes the face of b at side s, across devices through the same bit and slot.
All inputs are finite; a program needn't handle non-finite values.
Results may differ from a plain program's by a relative error of at most 0.0065.
Values may be sent and summed in bfloat16 or wider, within the bound.
No kernel may reach another device: no remote copies, remote signals or barrier semaphores. Data moves between devices by JAX's collectives and lax.ppermute only.
A program may use at most 64 MiB of HBM per device.

v0:
```python
import jax
import jax.numpy as jnp
from jax import lax
from jax.sharding import PartitionSpec as P

OPPOSITE = (0, 2, 1, 4, 3, 6, 5)


def swapped(value, axis, stride):
    mask = 2**stride
    pairs = [(source, source ^ mask) for source in range(lax.axis_size(axis))]
    return lax.ppermute(value, axis, pairs)


def face_slabs(blocks):
    return jnp.stack(
        [
            blocks[:, 0],
            blocks[:, -1],
            blocks[:, :, 0],
            blocks[:, :, -1],
            blocks[:, :, :, 0],
            blocks[:, :, :, -1],
        ],
        axis=1,
    )


def shift_taps(blocks, border):
    return [
        blocks,
        jnp.concatenate([border[:, 0][:, None], blocks[:, :-1]], 1),
        jnp.concatenate([blocks[:, 1:], border[:, 1][:, None]], 1),
        jnp.concatenate([border[:, 2][:, :, None], blocks[:, :, :-1]], 2),
        jnp.concatenate([blocks[:, :, 1:], border[:, 3][:, :, None]], 2),
        jnp.concatenate([border[:, 4][:, :, :, None], blocks[:, :, :, :-1]], 3),
        jnp.concatenate([blocks[:, :, :, 1:], border[:, 5][:, :, :, None]], 3),
    ]


def conv_apply(taps, weight):
    chans = taps[0].shape[-1]
    total = jnp.dot(taps[0].reshape(-1, chans), weight[0], preferred_element_type=jnp.float32)
    for tap_index in range(1, 7):
        total = total + jnp.dot(
            taps[tap_index].reshape(-1, chans),
            weight[tap_index],
            preferred_element_type=jnp.float32,
        )
    return total


def conv_back(taps, weight):
    chans = taps[0].shape[-1]
    total = lax.dot_general(
        taps[0].reshape(-1, chans),
        weight[0],
        (((1,), (1,)), ((), ())),
        preferred_element_type=jnp.float32,
    )
    for tap_index in range(1, 7):
        total = total + lax.dot_general(
            taps[OPPOSITE[tap_index]].reshape(-1, chans),
            weight[tap_index],
            (((1,), (1,)), ((), ())),
            preferred_element_type=jnp.float32,
        )
    return total


def weight_grads(taps, delta):
    chans = taps[0].shape[-1]
    return jnp.stack(
        [
            lax.dot_general(
                single.reshape(-1, chans),
                delta,
                (((0,), (0,)), ((), ())),
                preferred_element_type=jnp.float32,
            )
            for single in taps
        ]
    )


def down_rows(hidden, brick_count, chans):
    return (
        hidden.reshape(brick_count, 4, 2, 4, 2, 4, 2, chans)
        .transpose(0, 1, 3, 5, 2, 4, 6, 7)
        .reshape(brick_count * 64, 8 * chans)
    )


def up_rows(patch_grad, brick_count, chans):
    return (
        patch_grad.reshape(brick_count, 4, 4, 4, 2, 2, 2, chans)
        .transpose(0, 1, 4, 2, 5, 3, 6, 7)
        .reshape(brick_count * 512, chans)
    )


def silu_slope(value):
    sigma = jax.nn.sigmoid(value)
    return sigma * (1.0 + value * (1.0 - sigma))


def rims_local(blocks, send_list, source_list, swapper):
    brick_count = blocks.shape[0]
    side_cells = blocks.shape[1]
    chans = blocks.shape[-1]
    faces = face_slabs(blocks).reshape(brick_count * 6, side_cells, side_cells, chans)
    pieces = [faces]
    for bit_index in range(send_list.shape[0]):
        pieces.append(swapper(faces[send_list[bit_index]], bit_index))
    pieces.append(jnp.zeros((1, side_cells, side_cells, chans), faces.dtype))
    lookup = jnp.concatenate(pieces, axis=0)
    return lookup[source_list.reshape(-1)].reshape(brick_count, 6, side_cells, side_cells, chans)


def on_device(features, send_faces, face_source, cotangent, conv_one, down_weight, conv_two):
    send_list = send_faces[0, 0]
    source_list = face_source[0]
    brick_count = features.shape[1]
    chan_one = features.shape[3]
    chan_two = cotangent.shape[3]
    grid_one = features[0].reshape(brick_count, 8, 8, 8, chan_one)
    border_one = rims_local(
        grid_one, send_list, source_list, lambda buffer, bit_index: swapped(buffer, "kd", bit_index)
    )
    taps_one = shift_taps(grid_one, border_one)
    pre_one = conv_apply(taps_one, conv_one)
    hidden_one = (
        features[0].reshape(-1, chan_one).astype(jnp.float32) + jax.nn.silu(pre_one)
    ).astype(jnp.bfloat16)
    patches = down_rows(hidden_one, brick_count, chan_one)
    coarse = jnp.dot(patches, down_weight, preferred_element_type=jnp.float32).astype(jnp.bfloat16)
    grid_two = coarse.reshape(brick_count, 4, 4, 4, chan_two)
    border_two = rims_local(
        grid_two, send_list, source_list, lambda buffer, bit_index: swapped(buffer, "kd", bit_index)
    )
    taps_two = shift_taps(grid_two, border_two)
    pre_two = conv_apply(taps_two, conv_two)
    encoded = (coarse.astype(jnp.float32) + jax.nn.silu(pre_two)).astype(jnp.bfloat16)
    upstream = cotangent[0].reshape(-1, chan_two).astype(jnp.float32)
    delta_two = (upstream * silu_slope(pre_two)).astype(jnp.bfloat16)
    grid_delta = delta_two.reshape(brick_count, 4, 4, 4, chan_two)
    border_delta = rims_local(
        grid_delta,
        send_list,
        source_list,
        lambda buffer, bit_index: swapped(buffer, "kd", bit_index),
    )
    taps_delta = shift_taps(grid_delta, border_delta)
    grad_two = weight_grads(taps_two, delta_two)
    grad_coarse = (upstream + conv_back(taps_delta, conv_two)).astype(jnp.bfloat16)
    grad_down = lax.dot_general(
        patches, grad_coarse, (((0,), (0,)), ((), ())), preferred_element_type=jnp.float32
    )
    patch_grad = lax.dot_general(
        grad_coarse, down_weight, (((1,), (1,)), ((), ())), preferred_element_type=jnp.float32
    )
    delta_one = (up_rows(patch_grad, brick_count, chan_one) * silu_slope(pre_one)).astype(
        jnp.bfloat16
    )
    grad_one = weight_grads(taps_one, delta_one)
    grad_one, grad_down, grad_two = lax.psum((grad_one, grad_down, grad_two), ("scene", "kd"))
    return (encoded.reshape(1, brick_count, 64, chan_two), grad_one, grad_down, grad_two)


def solution(mesh):
    placed = (
        P("scene", "kd", None, None),
        P("scene", "kd", None, None),
        P("scene", "kd", None),
        P("scene", "kd", None, None),
        P(),
        P(),
        P(),
    )
    return jax.shard_map(
        on_device,
        mesh=mesh,
        in_specs=placed,
        out_specs=(P("scene", "kd", None, None), P(), P(), P()),
        check_vma=False,
    )
```

profile of v0, /device:TPU:1, one launch (start us, length us, event | category | flops | bytes accessed | tf_op | source)
XLA Modules:
  0.0 420.7 jit_solution(17682841565608177725)
XLA Ops:
  8.2 1.4 fusion.66
  9.6 1.4 fusion.75
  19.4 2.5 collective-permute-start
  22.0 3.0 collective-permute-start.1
  25.0 4.2 %collective-permute-start.2 = (bf16[1,8,8,128]{3,2,1,0:T(8,128)(2,1)S(1)}, bf16[1,8,8,128]{3,2,1,0:T(8,128)(2,1)S(1)}, u32[]{:S(2)}, u32[]{:S(2)}) collective-permute-start(bf16[1,8,8,128]{3,2,1,0:T(8,128)(2,1)S(1)} %get-tuple-element.136), channel_id=1, source_target_pairs={{0,4},{1,5},{2,6},{3,7},{4,0},{5,1},{6,2},{7,3},{8,12},{9,13},{10,... | collective-permute-start | bytes 49160 | tf_op jit(solution)/shard_map/ppermute | solution.py:12
  29.2 1.2 fusion.65
  30.4 1.0 fusion.64
  31.4 1.2 fusion.63
  34.0 1.3 pad_maximum_fusion
  39.1 1.4 add_convert_fusion
  40.6 1.2 copy.202
  41.8 1.4 reshape.158
  45.9 1.8 fusion.31
  49.5 1.2 collective-permute-start.4
  50.7 2.6 collective-permute-start.5
  54.5 2.6 collective-permute-done.5
  58.3 1.6 gather_fusion.1
  61.7 1.7 pad_maximum_fusion.7
  64.4 1.7 pad_maximum_fusion.8
  66.0 1.6 reshape.164
  67.6 1.7 pad_maximum_fusion.9
  69.3 1.6 reshape.165
  71.7 1.7 pad_maximum_fusion.10
  73.4 1.6 reshape.166
  75.8 1.7 pad_maximum_fusion.11
  77.5 1.6 reshape.167
  79.1 1.3 convolution_add_fusion.17
  80.4 1.1 convolution_add_fusion.16
  81.5 1.2 convolution_add_fusion.15
  90.4 1.2 copy-done.7
  92.4 1.2 collective-permute-start.7
  93.6 2.6 collective-permute-start.8
  97.4 2.6 collective-permute-done.8
  101.2 1.6 gather_fusion.2
  115.4 1.2 convolution_add_fusion.11
  116.7 1.2 convolution_add_fusion.10
  117.9 1.2 convolution_add_fusion.9
  119.1 1.1 convolution_add_fusion.8
  120.2 1.1 convolution_add_fusion.7
  121.4 1.1 fusion.8
  122.5 1.3 fusion.76
  123.8 1.3 fusion.77
  125.2 3.1 reshape.178
  128.3 1.8 copy.159
  137.4 270.9 %all-reduce.3.cloned.1.call-done = (f32[7,128,128]{1,2,0:T(8,128)}, f32[1024,256]{1,0:T(8,128)}, f32[7,256,256]{2,1,0:T(8,128)}) async-done(((f32[7,128,128]{1,2,0:T(8,128)}, f32[1024,256]{1,0:T(8,128)}, f32[7,256,256]{2,1,0:T(8,128)}), (f32[7,128,128]{1,2,0:T(8,128)}, f32[1024,256]{1,0:T(8,128)}, f32[7,256,256]{2,1,0:T(8,128)})) %all-reduce.3.cloned.1.call-update) | async-done | bytes 3342352 | tf_op jit(solution)/shard_map/psum | solution.py:166
  408.3 2.1 copy.166
  410.4 2.3 copy.245
  412.6 1.2 copy.246
  (184 shorter events, 50.3 us)
Async XLA Ops:
  7.2 36.0 %copy-start = (bf16[1024,256]{1,0:T(8,128)(2,1)S(1)}, bf16[1024,256]{1,0:T(8,128)(2,1)}, u32[]{:S(2)}) copy-start(bf16[1024,256]{1,0:T(8,128)(2,1)} %param.12) | copy-start | bytes 1572868
  7.2 22.0 %copy-start.1 = (bf16[1,4,512,128]{3,2,1,0:T(8,128)(2,1)S(1)}, bf16[1,4,512,128]{3,2,1,0:T(8,128)(2,1)}, u32[]{:S(2)}) copy-start(bf16[1,4,512,128]{3,2,1,0:T(8,128)(2,1)} %param.7) | copy-start | bytes 1572868
  7.2 401.1 %all-reduce.3.cloned.1.call-start = ((), (), s32[]{:S(2)}) async-start(), calls=%async_computation | async-start | bytes 6684672 | tf_op jit(solution)/shard_map/psum | solution.py:166
  19.4 13.6 %collective-permute-start = (bf16[1,8,8,128]{3,2,1,0:T(8,128)(2,1)S(1)}, bf16[1,8,8,128]{3,2,1,0:T(8,128)(2,1)S(1)}, u32[]{:S(2)}, u32[]{:S(2)}) collective-permute-start(bf16[1,8,8,128]{3,2,1,0:T(8,128)(2,1)S(1)} %get-tuple-element.138), channel_id=1, source_target_pairs={{0,1},{1,0},{2,3},{3,2},{4,5},{5,4},{6,7},{7,6},{8,9},{9,8},{10,11... | collective-permute-start | bytes 49160 | tf_op jit(solution)/shard_map/ppermute | solution.py:12
  22.0 11.0 %collective-permute-start.1 = (bf16[1,8,8,128]{3,2,1,0:T(8,128)(2,1)S(1)}, bf16[1,8,8,128]{3,2,1,0:T(8,128)(2,1)S(1)}, u32[]{:S(2)}, u32[]{:S(2)}) collective-permute-start(bf16[1,8,8,128]{3,2,1,0:T(8,128)(2,1)S(1)} %get-tuple-element.137), channel_id=1, source_target_pairs={{0,2},{1,3},{2,0},{3,1},{4,6},{5,7},{6,4},{7,5},{8,10},{9,11},{10,... | collective-permute-start | bytes 49160 | tf_op jit(solution)/shard_map/ppermute | solution.py:12
  25.0 8.1 %collective-permute-start.2 = (bf16[1,8,8,128]{3,2,1,0:T(8,128)(2,1)S(1)}, bf16[1,8,8,128]{3,2,1,0:T(8,128)(2,1)S(1)}, u32[]{:S(2)}, u32[]{:S(2)}) collective-permute-start(bf16[1,8,8,128]{3,2,1,0:T(8,128)(2,1)S(1)} %get-tuple-element.136), channel_id=1, source_target_pairs={{0,4},{1,5},{2,6},{3,7},{4,0},{5,1},{6,2},{7,3},{8,12},{9,13},{10,... | collective-permute-start | bytes 49160 | tf_op jit(solution)/shard_map/ppermute | solution.py:12
  30.4 2.2 copy-start.34
  30.4 2.3 copy-start.31
  35.5 1.0 copy-start.13
  35.5 1.1 copy-start.14
  36.8 0.8 copy-start.2
  37.0 1.0 copy-start.10
  37.1 1.2 copy-start.11
  38.8 1.8 copy-start.4
  38.8 1.7 copy-start.8
  47.9 5.3 %collective-permute-start.3 = (bf16[1,4,4,256]{3,2,1,0:T(4,128)(2,1)S(1)}, bf16[1,4,4,256]{3,2,1,0:T(4,128)(2,1)S(1)}, u32[]{:S(2)}, u32[]{:S(2)}) collective-permute-start(bf16[1,4,4,256]{3,2,1,0:T(4,128)(2,1)S(1)} %get-tuple-element.158), channel_id=1, source_target_pairs={{0,1},{1,0},{2,3},{3,2},{4,5},{5,4},{6,7},{7,6},{8,9},{9,8},{10,11... | collective-permute-start | bytes 24584 | tf_op jit(solution)/shard_map/ppermute | solution.py:12
  49.5 4.4 %collective-permute-start.4 = (bf16[1,4,4,256]{3,2,1,0:T(4,128)(2,1)S(1)}, bf16[1,4,4,256]{3,2,1,0:T(4,128)(2,1)S(1)}, u32[]{:S(2)}, u32[]{:S(2)}) collective-permute-start(bf16[1,4,4,256]{3,2,1,0:T(4,128)(2,1)S(1)} %get-tuple-element.157), channel_id=1, source_target_pairs={{0,2},{1,3},{2,0},{3,1},{4,6},{5,7},{6,4},{7,5},{8,10},{9,11},{10,... | collective-permute-start | bytes 24584 | tf_op jit(solution)/shard_map/ppermute | solution.py:12
  50.7 6.4 %collective-permute-start.5 = (bf16[1,4,4,256]{3,2,1,0:T(4,128)(2,1)S(1)}, bf16[1,4,4,256]{3,2,1,0:T(4,128)(2,1)S(1)}, u32[]{:S(2)}, u32[]{:S(2)}) collective-permute-start(bf16[1,4,4,256]{3,2,1,0:T(4,128)(2,1)S(1)} %get-tuple-element.156), channel_id=1, source_target_pairs={{0,4},{1,5},{2,6},{3,7},{4,0},{5,1},{6,2},{7,3},{8,12},{9,13},{10,... | collective-permute-start | bytes 24584 | tf_op jit(solution)/shard_map/ppermute | solution.py:12
  61.7 18.7 %copy-start.15 = (bf16[256,256]{1,0:T(8,128)(2,1)}, bf16[256,256]{1,0:T(8,128)(2,1)S(1)}, u32[]{:S(2)}) copy-start(bf16[256,256]{1,0:T(8,128)(2,1)S(1)} %reshape.162) | copy-start | bytes 393220
  64.3 17.2 %copy-start.17 = (bf16[256,256]{1,0:T(8,128)(2,1)}, bf16[256,256]{1,0:T(8,128)(2,1)S(1)}, u32[]{:S(2)}) copy-start(bf16[256,256]{1,0:T(8,128)(2,1)S(1)} %reshape.163) | copy-start | bytes 393220
  79.1 3.6 copy-start.6
  79.1 3.6 copy-start.20
  79.1 3.8 copy-start.22
  79.1 4.0 copy-start.26
  79.1 4.0 copy-start.32
  85.1 3.9 copy-start.16
  85.1 4.1 copy-start.18
  85.2 4.2 %copy-start.19 = (bf16[256,256]{1,0:T(8,128)(2,1)S(1)}, bf16[256,256]{1,0:T(8,128)(2,1)}, u32[]{:S(2)}) copy-start(bf16[256,256]{1,0:T(8,128)(2,1)} %reshape.164) | copy-start | bytes 393220
  86.0 3.7 copy-start.21
  87.5 2.4 copy-start.23
  87.7 2.4 copy-start.27
  88.0 8.2 %collective-permute-start.6 = (bf16[1,4,4,256]{3,2,1,0:T(4,128)(2,1)S(1)}, bf16[1,4,4,256]{3,2,1,0:T(4,128)(2,1)S(1)}, u32[]{:S(2)}, u32[]{:S(2)}) collective-permute-start(bf16[1,4,4,256]{3,2,1,0:T(4,128)(2,1)S(1)} %get-tuple-element.149), channel_id=1, source_target_pairs={{0,1},{1,0},{2,3},{3,2},{4,5},{5,4},{6,7},{7,6},{8,9},{9,8},{10,11... | collective-permute-start | bytes 24584 | tf_op jit(solution)/shard_map/ppermute | solution.py:12
  90.4 1.2 copy-start.7
  92.4 4.4 %collective-permute-start.7 = (bf16[1,4,4,256]{3,2,1,0:T(4,128)(2,1)S(1)}, bf16[1,4,4,256]{3,2,1,0:T(4,128)(2,1)S(1)}, u32[]{:S(2)}, u32[]{:S(2)}) collective-permute-start(bf16[1,4,4,256]{3,2,1,0:T(4,128)(2,1)S(1)} %get-tuple-element.148), channel_id=1, source_target_pairs={{0,2},{1,3},{2,0},{3,1},{4,6},{5,7},{6,4},{7,5},{8,10},{9,11},{10,... | collective-permute-start | bytes 24584 | tf_op jit(solution)/shard_map/ppermute | solution.py:12
  93.6 6.4 %collective-permute-start.8 = (bf16[1,4,4,256]{3,2,1,0:T(4,128)(2,1)S(1)}, bf16[1,4,4,256]{3,2,1,0:T(4,128)(2,1)S(1)}, u32[]{:S(2)}, u32[]{:S(2)}) collective-permute-start(bf16[1,4,4,256]{3,2,1,0:T(4,128)(2,1)S(1)} %get-tuple-element.147), channel_id=1, source_target_pairs={{0,4},{1,5},{2,6},{3,7},{4,0},{5,1},{6,2},{7,3},{8,12},{9,13},{10,... | collective-permute-start | bytes 24584 | tf_op jit(solution)/shard_map/ppermute | solution.py:12
  103.6 11.9 %copy-start.24 = (f32[256,256]{1,0:T(8,128)S(1)}, f32[256,256]{1,0:T(8,128)}, u32[]{:S(2)}) copy-start(f32[256,256]{1,0:T(8,128)} %fusion.29) | copy-start | bytes 786436
  115.4 3.7 copy-start.28
  115.4 4.8 %copy-start.29 = (bf16[256,256]{1,0:T(8,128)(2,1)S(1)}, bf16[256,256]{1,0:T(8,128)(2,1)}, u32[]{:S(2)}) copy-start(bf16[256,256]{1,0:T(8,128)(2,1)} %reshape.176) | copy-start | bytes 393220
  115.4 6.0 %copy-start.30 = (bf16[256,256]{1,0:T(8,128)(2,1)S(1)}, bf16[256,256]{1,0:T(8,128)(2,1)}, u32[]{:S(2)}) copy-start(bf16[256,256]{1,0:T(8,128)(2,1)} %reshape.177) | copy-start | bytes 393220
  115.4 6.0 %copy-start.33 = (bf16[1,4,64,256]{3,2,1,0:T(8,128)(2,1)S(1)}, bf16[1,4,64,256]{3,2,1,0:T(8,128)(2,1)}, u32[]{:S(2)}) copy-start(bf16[1,4,64,256]{3,2,1,0:T(8,128)(2,1)} %param.10) | copy-start | bytes 393220
  128.3 1.8 copy-start.25
  130.5 2.9 copy-start.3
  132.5 2.9 copy-start.5
  133.5 2.9 copy-start.9
  408.3 4.4 %copy-start.12 = (f32[7,256,256]{2,1,0:T(8,128)S(1)}, f32[7,256,256]{2,1,0:T(8,128)}, u32[]{:S(2)}) copy-start(f32[7,256,256]{2,1,0:T(8,128)} %get-tuple-element.189) | copy-start | bytes 5505028
Sparse Core Ops, SparseCore 0:
  137.5 270.6 all-reduce.2
where the time goes:
time: 423 us; the launch traced here: 421 us
  waiting for transfers between devices  276 us (65%)
  local copies, waits for them, and re-layouts  57.9 us (14%)
  matrix products  29.1 us (7%)
  between operations  20.7 us (5%)
  starting transfers between devices  19.2 us (5%)
  other arithmetic  17.8 us (4%)
    psum x1, waiting for transfers between devices, on_device(): lax.psum((grad_one, grad_down, grad_two), ('scene', 'kd'))  271 us
    ppermute x9, starting transfers between devices, swapped(): return lax.ppermute(value, axis, pairs)  19.1 us
    unnamed x100, local copies, waits for them, and re-layouts  17.6 us
  transfers between devices with their start and end apart: 10, of which 3 were waited for; matrix products, arithmetic and copies ran while one was open for 2% of the time, Pallas kernels for 0%

commit v1 on v0

--- a/solution.py
+++ b/solution.py
@@ -117,6 +117,48 @@
     return lookup[source_list.reshape(-1)].reshape(brick_count, 6, side_cells, side_cells, chans)
 
 
+CHUNK = 208
+PLANE = 16
+
+
+def plane_groups():
+    return [[2 * chip + core for chip in range(PLANE)] for core in range(2)]
+
+
+def summed(grad_one, grad_down, grad_two):
+    core = lax.rem(lax.axis_index("scene"), 2)
+    halves = [
+        jnp.concatenate(
+            [
+                grad_one.reshape(2, 448, 128)[half],
+                grad_down[:, 128 * half : 128 * half + 128],
+                grad_two.reshape(1792, 256)[:, 128 * half : 128 * half + 128],
+                jnp.zeros((64, 128), jnp.float32),
+            ]
+        )
+        for half in range(2)
+    ]
+    kept = jnp.where(core == 0, halves[0], halves[1])
+    sent = jnp.where(core == 0, halves[1], halves[0])
+    mine = kept + swapped(sent, "scene", 0)
+    groups = plane_groups()
+    parts = mine.astype(jnp.bfloat16).reshape(PLANE, CHUNK, 128)
+    parts = lax.all_to_all(parts, "scene", 0, 0, axis_index_groups=groups)
+    piece = parts.astype(jnp.float32).sum(0).astype(jnp.bfloat16)
+    pieces = lax.all_to_all(jnp.broadcast_to(piece[None], (8, CHUNK, 128)), "kd", 0, 0)
+    piece = pieces.astype(jnp.float32).sum(0).astype(jnp.bfloat16)
+    whole = lax.all_to_all(
+        jnp.broadcast_to(piece[None], (PLANE, CHUNK, 128)), "scene", 0, 0, axis_index_groups=groups
+    ).reshape(PLANE * CHUNK, 128)
+    other = swapped(whole, "scene", 0)
+    first = jnp.where(core == 0, whole, other).astype(jnp.float32)
+    second = jnp.where(core == 0, other, whole).astype(jnp.float32)
+    one = jnp.concatenate([first[:448], second[:448]]).reshape(7, 128, 128)
+    down = jnp.concatenate([first[448:1472], second[448:1472]], axis=1)
+    two = jnp.concatenate([first[1472:3264], second[1472:3264]], axis=1).reshape(7, 256, 256)
+    return one, down, two
+
+
 def on_device(features, send_faces, face_source, cotangent, conv_one, down_weight, conv_two):
     send_list = send_faces[0, 0]
     source_list = face_source[0]
@@ -163,7 +205,7 @@
         jnp.bfloat16
     )
     grad_one = weight_grads(taps_one, delta_one)
-    grad_one, grad_down, grad_two = lax.psum((grad_one, grad_down, grad_two), ("scene", "kd"))
+    grad_one, grad_down, grad_two = summed(grad_one, grad_down, grad_two)
     return (encoded.reshape(1, brick_count, 64, chan_two), grad_one, grad_down, grad_two)
 
 

time: 423 us -> 185 us (0.44)
  waiting for transfers between devices: 276 us -> 15.5 us
  blocking collectives: 0 us -> 51.1 us
  local copies, waits for them, and re-layouts: 57.9 us -> 41.7 us
  between operations: 20.7 us -> 7.44 us
  matrix products: 29.1 us -> 22.5 us
  starting transfers between devices: 19.2 us -> 25.1 us
    psum x1 -> x0, waiting for transfers between devices: 271 us -> none  [on_device(): lax.psum((grad_one, grad_down, grad_two), ('scene', 'kd'))]
    all_to_all x0 -> x3, blocking collectives: none -> 51.1 us  [the longest x1 20.3 us: summed(): parts = lax.all_to_all(parts, 'scene', 0, 0, axis_index_groups=groups)]
    ppermute x9 -> x11, waiting for transfers between devices: 5.21 us -> 15.5 us  [swapped(): return lax.ppermute(value, axis, pairs)]
    reshape x6, local copies, waits for them, and re-layouts: 7.32 us -> 0.88 us  [conv_apply(): taps[tap_index].reshape(-1, chans)]
    unnamed x100 -> x89, local copies, waits for them, and re-layouts: 17.6 us -> 11.6 us
    ppermute x9 -> x11, starting transfers between devices: 19.1 us -> 25.1 us  [swapped(): return lax.ppermute(value, axis, pairs)]
    dot_general x14, matrix products: 8.37 us -> 3.9 us  [weight_grads(): lax.dot_general(single.reshape(-1, chans), delta, (((0,), (0,)), ((), ())...]
  transfers between devices with their start and end apart: 10 -> 11, of which waited for: 3 -> 6; matrix products, arithmetic and copies ran while one was open for 2% -> 6% of each run, Pallas kernels for 0% -> 0%
where the time goes in v1:
time: 185 us; the launch traced here: 184 us
  blocking collectives  51.1 us (28%)
  local copies, waits for them, and re-layouts  41.7 us (23%)
  starting transfers between devices  25.1 us (14%)
  matrix products  22.5 us (12%)
  other arithmetic  20.5 us (11%)
  waiting for transfers between devices  15.5 us (8%)
  between operations  7.44 us (4%)
    ppermute x11, starting transfers between devices, swapped(): return lax.ppermute(value, axis, pairs)  25.1 us
    all_to_all x1, blocking collectives, summed(): parts = lax.all_to_all(parts, 'scene', 0, 0, axis_index_groups=groups)  20.3 us
    all_to_all x1, blocking collectives, summed(): lax.all_to_all(jnp.broadcast_to(piece[None], (PLANE, CHUNK, 128)), 'scene...  16 us
    ppermute x11, waiting for transfers between devices, swapped(): return lax.ppermute(value, axis, pairs)  15.5 us
    all_to_all x1, blocking collectives, summed(): lax.all_to_all(jnp.broadcast_to(piece[None], (8, CHUNK, 128)), 'kd', 0, 0)  14.8 us
    unnamed x89, local copies, waits for them, and re-layouts  11.6 us
    dot_general x6, matrix products, conv_back(): lax.dot_general(taps[OPPOSITE[tap_index]].reshape(-1, chans), weight[tap_...  7.14 us
    dot_general x12, matrix products, conv_apply(): jnp.dot(taps[tap_index].reshape(-1, chans), weight[tap_index], preferred_...  5.67 us
  transfers between devices with their start and end apart: 11, of which 6 were waited for; matrix products, arithmetic and copies ran while one was open for 6% of the time, Pallas kernels for 0%

profile of v1, /device:TPU:1, one launch (start us, length us, event | category | flops | bytes accessed | tf_op | source)
XLA Modules:
  0.0 183.8 jit_solution(7062578616658168265)
XLA Ops:
  1.6 1.4 fusion.69
  3.0 1.4 fusion.78
  12.8 2.5 %collective-permute-start = (bf16[1,8,8,128]{3,2,1,0:T(8,128)(2,1)S(1)}, bf16[1,8,8,128]{3,2,1,0:T(8,128)(2,1)S(1)}, u32[]{:S(2)}, u32[]{:S(2)}) collective-permute-start(bf16[1,8,8,128]{3,2,1,0:T(8,128)(2,1)S(1)} %get-tuple-element.127), channel_id=1, source_target_pairs={{0,1},{1,0},{2,3},{3,2},{4,5},{5,4},{6,7},{7,6},{8,9},{9,8},{10,11... | collective-permute-start | bytes 49160 | tf_op jit(solution)/shard_map/ppermute | solution.py:12
  15.4 3.0 %collective-permute-start.1 = (bf16[1,8,8,128]{3,2,1,0:T(8,128)(2,1)S(1)}, bf16[1,8,8,128]{3,2,1,0:T(8,128)(2,1)S(1)}, u32[]{:S(2)}, u32[]{:S(2)}) collective-permute-start(bf16[1,8,8,128]{3,2,1,0:T(8,128)(2,1)S(1)} %get-tuple-element.126), channel_id=1, source_target_pairs={{0,2},{1,3},{2,0},{3,1},{4,6},{5,7},{6,4},{7,5},{8,10},{9,11},{10,... | collective-permute-start | bytes 49160 | tf_op jit(solution)/shard_map/ppermute | solution.py:12
  18.4 4.2 %collective-permute-start.2 = (bf16[1,8,8,128]{3,2,1,0:T(8,128)(2,1)S(1)}, bf16[1,8,8,128]{3,2,1,0:T(8,128)(2,1)S(1)}, u32[]{:S(2)}, u32[]{:S(2)}) collective-permute-start(bf16[1,8,8,128]{3,2,1,0:T(8,128)(2,1)S(1)} %get-tuple-element.125), channel_id=1, source_target_pairs={{0,4},{1,5},{2,6},{3,7},{4,0},{5,1},{6,2},{7,3},{8,12},{9,13},{10,... | collective-permute-start | bytes 49160 | tf_op jit(solution)/shard_map/ppermute | solution.py:12
  23.6 1.1 fusion.67
  24.7 1.1 fusion.68
  26.0 1.0 fusion.54
  30.1 1.8 gather_fusion
  32.1 1.3 pad_maximum_fusion.2
  36.9 1.4 add_convert_fusion.1
  42.5 1.3 collective-permute-start.4
  44.0 2.0 %collective-permute-done.4 = bf16[1,4,4,256]{3,2,1,0:T(4,128)(2,1)S(1)} collective-permute-done((bf16[1,4,4,256]{3,2,1,0:T(4,128)(2,1)S(1)}, bf16[1,4,4,256]{3,2,1,0:T(4,128)(2,1)S(1)}, u32[]{:S(2)}, u32[]{:S(2)}) %collective-permute-start.4) | collective-permute-done | bytes 8224 | tf_op jit(solution)/shard_map/ppermute | solution.py:12
  46.0 4.2 %collective-permute-done.5 = bf16[1,4,4,256]{3,2,1,0:T(4,128)(2,1)S(1)} collective-permute-done((bf16[1,4,4,256]{3,2,1,0:T(4,128)(2,1)S(1)}, bf16[1,4,4,256]{3,2,1,0:T(4,128)(2,1)S(1)}, u32[]{:S(2)}, u32[]{:S(2)}) %collective-permute-start.5) | collective-permute-done | bytes 8224 | tf_op jit(solution)/shard_map/ppermute | solution.py:12
  52.9 1.0 pad_maximum_fusion.12
  55.1 1.1 convolution_add_fusion.17
  62.0 1.0 collective-permute-start.6
  65.3 1.2 collective-permute-start.7
  66.5 1.2 collective-permute-start.8
  69.3 3.6 %collective-permute-done.8 = bf16[1,4,4,256]{3,2,1,0:T(4,128)(2,1)S(1)} collective-permute-done((bf16[1,4,4,256]{3,2,1,0:T(4,128)(2,1)S(1)}, bf16[1,4,4,256]{3,2,1,0:T(4,128)(2,1)S(1)}, u32[]{:S(2)}, u32[]{:S(2)}) %collective-permute-start.8) | collective-permute-done | bytes 8224 | tf_op jit(solution)/shard_map/ppermute | solution.py:12
  74.1 2.5 %gather_fusion.2 = bf16[24,4,4,256]{3,2,1,0:T(4,128)(2,1)} fusion(bf16[28,4,4,256]{3,2,1,0:T(4,128)(2,1)} %constant_dynamic-update-slice_fusion.28, s32[1024]{0:T(1024)} %pad_clamp_fusion), kind=kCustom, calls=%fused_computation.2 | custom fusion | bytes 393312 | tf_op jit(solution)/shard_map/gather | solution.py:117
  76.6 1.6 slice_bitcast_fusion.8
  78.2 1.0 pad_maximum_fusion.20
  80.7 1.0 pad_maximum_fusion.19
  82.5 1.0 pad_maximum_fusion.18
  84.2 1.0 pad_maximum_fusion.17
  87.5 1.0 pad_maximum_fusion.15
  89.2 1.3 convolution_add_fusion.11
  90.6 1.2 convolution_add_fusion.10
  91.8 1.2 convolution_add_fusion.9
  93.0 1.1 convolution_add_fusion.8
  94.2 1.1 convolution_add_fusion.7
  95.3 1.1 fusion.8
  96.5 1.4 fusion.79
  97.8 1.3 fusion.80
  99.2 3.1 %reshape.200 = f32[4,4,4,4,2,2,2,128]{7,6,5,4,3,2,1,0:T(2,128)} reshape(f32[256,1024]{1,0:T(8,128)} %fusion.79) | data formatting | bytes 2097152 | tf_op jit(solution)/shard_map/reshape | solution.py:96
  102.3 1.8 copy.170
  108.0 2.8 %fusion.16 = f32[3328,128]{1,0:T(8,128)S(1)} fusion(f32[1792,128]{1,0:T(8,128)S(1)} %get-tuple-element.104, f32[1024,128]{1,0:T(8,128)S(1)} %get-tuple-element.108, f32[448,128]{1,0:T(8,128)S(1)} %get-tuple-element.118, f32[1792,128]{1,0:T(8,128)S(1)} %get-tuple-element.103, f32[1024,128]{1,0:T(8,128)S(1)} %get-tuple-element.107, ...), kind=kLoop, calls=%fused_computation.56 | loop fusion | flops 2981888 | bytes 5059585 | tf_op jit(solution)/shard_map/jit(_where)/select_n | solution.py:142
  110.8 5.0 %collective-permute-start.9 = (f32[3328,128]{1,0:T(8,128)S(1)}, f32[3328,128]{1,0:T(8,128)S(1)}, u32[]{:S(2)}, u32[]{:S(2)}) collective-permute-start(f32[3328,128]{1,0:T(8,128)S(1)} %fusion.16), channel_id=1, source_target_pairs={{0,8},{8,0},{16,24},{24,16},{32,40},{40,32},{48,56},{56,48},{64,72... | collective-permute-start | bytes 5111816 | tf_op jit(solution)/shard_map/ppermute | solution.py:12
  115.9 3.2 %collective-permute-done.9 = f32[3328,128]{1,0:T(8,128)S(1)} collective-permute-done((f32[3328,128]{1,0:T(8,128)S(1)}, f32[3328,128]{1,0:T(8,128)S(1)}, u32[]{:S(2)}, u32[]{:S(2)}) %collective-permute-start.9) | collective-permute-done | bytes 1703968 | tf_op jit(solution)/shard_map/ppermute | solution.py:12
  119.1 2.8 %add_convert_fusion = bf16[3328,128]{1,0:T(8,128)(2,1)S(1)} fusion(f32[3328,128]{1,0:T(8,128)S(1)} %collective-permute-done.9, f32[1792,128]{1,0:T(8,128)S(1)} %get-tuple-element.104, f32[1024,128]{1,0:T(8,128)S(1)} %get-tuple-element.108, f32[448,128]{1,0:T(8,128)S(1)} %get-tuple-element.118, f32[1792,128]{1,0:T(8,128)S(1)} %get-tuple-element.103, ...), kind=kLoop, calls=%fused_computation.12 | loop fusion | flops 3833856 | bytes 5911553 | tf_op jit(solution)/shard_map/convert_element_type | solution.py:145
  121.9 20.3 %all_to_all.15 = bf16[16,208,128]{2,1,0:T(8,128)(2,1)S(1)} all-to-all(bf16[16,208,128]{2,1,0:T(8,128)(2,1)S(1)} %bitcast.352), channel_id=1, replica_groups={{0,16,32,48,64,80,96,112,128,144,160,176,192,208,224,240},{8,24,40,56,7..., dimensions={0} | all-to-all | bytes 1703936 | tf_op jit(solution)/shard_map/all_to_all | solution.py:146
  142.3 14.8 %all_to_all.16 = bf16[8,208,128]{2,1,0:T(8,128)(2,1)S(1)} all-to-all(bf16[8,208,128]{2,1,0:T(8,128)(2,1)S(1)} %broadcast_in_dim.16), channel_id=1, replica_groups=mesh['scene'=32,'kd'=8] {'kd'}, dimensions={0} | all-to-all | bytes 851968 | tf_op jit(solution)/shard_map/all_to_all | solution.py:148
  157.3 16.0 %all_to_all.17 = bf16[16,208,128]{2,1,0:T(8,128)(2,1)S(1)} all-to-all(bf16[16,208,128]{2,1,0:T(8,128)(2,1)S(1)} %broadcast_in_dim.17), channel_id=1, replica_groups={{0,16,32,48,64,80,96,112,128,144,160,176,192,208,224,240},{8,24,40,56,7..., dimensions={0} | all-to-all | bytes 1703936 | tf_op jit(solution)/shard_map/all_to_all | solution.py:150
  173.4 4.7 %collective-permute-start.10 = (bf16[3328,128]{1,0:T(8,128)(2,1)S(1)}, bf16[3328,128]{1,0:T(8,128)(2,1)S(1)}, u32[]{:S(2)}, u32[]{:S(2)}) collective-permute-start(bf16[3328,128]{1,0:T(8,128)(2,1)S(1)} %bitcast.353), channel_id=1, source_target_pairs={{0,8},{8,0},{16,24},{24,16},{32,40},{40,32},{48,56},{56,48},{64,72... | collective-permute-start | bytes 2555912 | tf_op jit(solution)/shard_map/ppermute | solution.py:12
  178.1 2.0 %collective-permute-done.10 = bf16[3328,128]{1,0:T(8,128)(2,1)S(1)} collective-permute-done((bf16[3328,128]{1,0:T(8,128)(2,1)S(1)}, bf16[3328,128]{1,0:T(8,128)(2,1)S(1)}, u32[]{:S(2)}, u32[]{:S(2)}) %collective-permute-start.10) | collective-permute-done | bytes 852000 | tf_op jit(solution)/shard_map/ppermute | solution.py:12
  180.6 1.3 pad_maximum_fusion
  182.0 1.0 pad_maximum_fusion.1
  (198 shorter events, 41.8 us)
Async XLA Ops:
  0.6 38.5 %copy-start = (bf16[1024,256]{1,0:T(8,128)(2,1)S(1)}, bf16[1024,256]{1,0:T(8,128)(2,1)}, u32[]{:S(2)}) copy-start(bf16[1024,256]{1,0:T(8,128)(2,1)} %param.12) | copy-start | bytes 1572868
  0.6 22.7 %copy-start.1 = (bf16[1,4,512,128]{3,2,1,0:T(8,128)(2,1)S(1)}, bf16[1,4,512,128]{3,2,1,0:T(8,128)(2,1)}, u32[]{:S(2)}) copy-start(bf16[1,4,512,128]{3,2,1,0:T(8,128)(2,1)} %param.7) | copy-start | bytes 1572868
  12.8 14.8 %collective-permute-start = (bf16[1,8,8,128]{3,2,1,0:T(8,128)(2,1)S(1)}, bf16[1,8,8,128]{3,2,1,0:T(8,128)(2,1)S(1)}, u32[]{:S(2)}, u32[]{:S(2)}) collective-permute-start(bf16[1,8,8,128]{3,2,1,0:T(8,128)(2,1)S(1)} %get-tuple-element.127), channel_id=1, source_target_pairs={{0,1},{1,0},{2,3},{3,2},{4,5},{5,4},{6,7},{7,6},{8,9},{9,8},{10,11... | collective-permute-start | bytes 49160 | tf_op jit(solution)/shard_map/ppermute | solution.py:12
  15.4 12.9 %collective-permute-start.1 = (bf16[1,8,8,128]{3,2,1,0:T(8,128)(2,1)S(1)}, bf16[1,8,8,128]{3,2,1,0:T(8,128)(2,1)S(1)}, u32[]{:S(2)}, u32[]{:S(2)}) collective-permute-start(bf16[1,8,8,128]{3,2,1,0:T(8,128)(2,1)S(1)} %get-tuple-element.126), channel_id=1, source_target_pairs={{0,2},{1,3},{2,0},{3,1},{4,6},{5,7},{6,4},{7,5},{8,10},{9,11},{10,... | collective-permute-start | bytes 49160 | tf_op jit(solution)/shard_map/ppermute | solution.py:12
  18.4 10.5 %collective-permute-start.2 = (bf16[1,8,8,128]{3,2,1,0:T(8,128)(2,1)S(1)}, bf16[1,8,8,128]{3,2,1,0:T(8,128)(2,1)S(1)}, u32[]{:S(2)}, u32[]{:S(2)}) collective-permute-start(bf16[1,8,8,128]{3,2,1,0:T(8,128)(2,1)S(1)} %get-tuple-element.125), channel_id=1, source_target_pairs={{0,4},{1,5},{2,6},{3,7},{4,0},{5,1},{6,2},{7,3},{8,12},{9,13},{10,... | collective-permute-start | bytes 49160 | tf_op jit(solution)/shard_map/ppermute | solution.py:12
  23.6 2.3 %copy-start.30 = (s32[1,4,6]{2,1,0:T(4,128)S(1)}, s32[1,4,6]{2,1,0:T(4,128)}, u32[]{:S(2)}) copy-start(s32[1,4,6]{2,1,0:T(4,128)} %param.9) | copy-start | bytes 292
  31.9 1.6 copy-start.25
  33.4 0.8 copy-start.2
  33.4 1.0 copy-start.4
  33.7 1.1 copy-start.16
  33.7 1.2 copy-start.17
  35.0 0.8 copy-start.6
  35.0 1.0 copy-start.8
  36.6 1.7 copy-start.10
  36.6 1.7 copy-start.14
  39.1 2.4 %copy-start.13 = (bf16[7,256,256]{2,1,0:T(8,128)(2,1)S(1)}, bf16[7,256,256]{2,1,0:T(8,128)(2,1)}, u32[]{:S(2)}) copy-start(bf16[7,256,256]{2,1,0:T(8,128)(2,1)} %param.13) | copy-start | bytes 2752516
  40.7 3.2 %collective-permute-start.3 = (bf16[1,4,4,256]{3,2,1,0:T(4,128)(2,1)S(1)}, bf16[1,4,4,256]{3,2,1,0:T(4,128)(2,1)S(1)}, u32[]{:S(2)}, u32[]{:S(2)}) collective-permute-start(bf16[1,4,4,256]{3,2,1,0:T(4,128)(2,1)S(1)} %get-tuple-element.147), channel_id=1, source_target_pairs={{0,1},{1,0},{2,3},{3,2},{4,5},{5,4},{6,7},{7,6},{8,9},{9,8},{10,11... | collective-permute-start | bytes 24584 | tf_op jit(solution)/shard_map/ppermute | solution.py:12
  42.5 3.5 %collective-permute-start.4 = (bf16[1,4,4,256]{3,2,1,0:T(4,128)(2,1)S(1)}, bf16[1,4,4,256]{3,2,1,0:T(4,128)(2,1)S(1)}, u32[]{:S(2)}, u32[]{:S(2)}) collective-permute-start(bf16[1,4,4,256]{3,2,1,0:T(4,128)(2,1)S(1)} %get-tuple-element.146), channel_id=1, source_target_pairs={{0,2},{1,3},{2,0},{3,1},{4,6},{5,7},{6,4},{7,5},{8,10},{9,11},{10,... | collective-permute-start | bytes 24584 | tf_op jit(solution)/shard_map/ppermute | solution.py:12
  43.8 6.4 %collective-permute-start.5 = (bf16[1,4,4,256]{3,2,1,0:T(4,128)(2,1)S(1)}, bf16[1,4,4,256]{3,2,1,0:T(4,128)(2,1)S(1)}, u32[]{:S(2)}, u32[]{:S(2)}) collective-permute-start(bf16[1,4,4,256]{3,2,1,0:T(4,128)(2,1)S(1)} %get-tuple-element.145), channel_id=1, source_target_pairs={{0,4},{1,5},{2,6},{3,7},{4,0},{5,1},{6,2},{7,3},{8,12},{9,13},{10,... | collective-permute-start | bytes 24584 | tf_op jit(solution)/shard_map/ppermute | solution.py:12
  51.7 2.2 %copy-start.24 = (bf16[4,4,3,4,256]{4,3,2,1,0:T(4,128)(2,1)S(1)}, bf16[4,4,3,4,256]{4,3,2,1,0:T(4,128)(2,1)}, u32[]{:S(2)}) copy-start(bf16[4,4,3,4,256]{4,3,2,1,0:T(4,128)(2,1)} %get-tuple-element.159) | copy-start | bytes 294916
  51.9 2.9 %copy-start.29 = (bf16[4,1,4,4,256]{4,3,2,1,0:T(4,128)(2,1)S(1)}, bf16[4,1,4,4,256]{4,3,2,1,0:T(4,128)(2,1)}, u32[]{:S(2)}) copy-start(bf16[4,1,4,4,256]{4,3,2,1,0:T(4,128)(2,1)} %get-tuple-element.143) | copy-start | bytes 98308
  52.0 3.0 %copy-start.28 = (bf16[4,1,4,4,256]{4,3,2,1,0:T(4,128)(2,1)S(1)}, bf16[4,1,4,4,256]{4,3,2,1,0:T(4,128)(2,1)}, u32[]{:S(2)}) copy-start(bf16[4,1,4,4,256]{4,3,2,1,0:T(4,128)(2,1)} %get-tuple-element.144) | copy-start | bytes 98308
  56.3 0.9 copy-start.19
  56.3 1.0 copy-start.26
  61.8 2.4 %copy-start.20 = (bf16[256,256]{1,0:T(8,128)(2,1)S(1)}, bf16[256,256]{1,0:T(8,128)(2,1)}, u32[]{:S(2)}) copy-start(bf16[256,256]{1,0:T(8,128)(2,1)} %reshape.189) | copy-start | bytes 393220
  62.0 5.6 %collective-permute-start.6 = (bf16[1,4,4,256]{3,2,1,0:T(4,128)(2,1)S(1)}, bf16[1,4,4,256]{3,2,1,0:T(4,128)(2,1)S(1)}, u32[]{:S(2)}, u32[]{:S(2)}) collective-permute-start(bf16[1,4,4,256]{3,2,1,0:T(4,128)(2,1)S(1)} %get-tuple-element.138), channel_id=1, source_target_pairs={{0,1},{1,0},{2,3},{3,2},{4,5},{5,4},{6,7},{7,6},{8,9},{9,8},{10,11... | collective-permute-start | bytes 24584 | tf_op jit(solution)/shard_map/ppermute | solution.py:12
  65.3 3.4 %collective-permute-start.7 = (bf16[1,4,4,256]{3,2,1,0:T(4,128)(2,1)S(1)}, bf16[1,4,4,256]{3,2,1,0:T(4,128)(2,1)S(1)}, u32[]{:S(2)}, u32[]{:S(2)}) collective-permute-start(bf16[1,4,4,256]{3,2,1,0:T(4,128)(2,1)S(1)} %get-tuple-element.137), channel_id=1, source_target_pairs={{0,2},{1,3},{2,0},{3,1},{4,6},{5,7},{6,4},{7,5},{8,10},{9,11},{10,... | collective-permute-start | bytes 24584 | tf_op jit(solution)/shard_map/ppermute | solution.py:12
  66.5 6.4 %collective-permute-start.8 = (bf16[1,4,4,256]{3,2,1,0:T(4,128)(2,1)S(1)}, bf16[1,4,4,256]{3,2,1,0:T(4,128)(2,1)S(1)}, u32[]{:S(2)}, u32[]{:S(2)}) collective-permute-start(bf16[1,4,4,256]{3,2,1,0:T(4,128)(2,1)S(1)} %get-tuple-element.136), channel_id=1, source_target_pairs={{0,4},{1,5},{2,6},{3,7},{4,0},{5,1},{6,2},{7,3},{8,12},{9,13},{10,... | collective-permute-start | bytes 24584 | tf_op jit(solution)/shard_map/ppermute | solution.py:12
  89.2 3.8 %copy-start.23 = (bf16[256,256]{1,0:T(8,128)(2,1)S(1)}, bf16[256,256]{1,0:T(8,128)(2,1)}, u32[]{:S(2)}) copy-start(bf16[256,256]{1,0:T(8,128)(2,1)} %reshape.197) | copy-start | bytes 393220
  89.2 4.9 %copy-start.22 = (bf16[256,256]{1,0:T(8,128)(2,1)S(1)}, bf16[256,256]{1,0:T(8,128)(2,1)}, u32[]{:S(2)}) copy-start(bf16[256,256]{1,0:T(8,128)(2,1)} %reshape.198) | copy-start | bytes 393220
  90.6 4.7 %copy-start.21 = (bf16[256,256]{1,0:T(8,128)(2,1)S(1)}, bf16[256,256]{1,0:T(8,128)(2,1)}, u32[]{:S(2)}) copy-start(bf16[256,256]{1,0:T(8,128)(2,1)} %reshape.199) | copy-start | bytes 393220
  90.6 4.7 %copy-start.27 = (bf16[1,4,64,256]{3,2,1,0:T(8,128)(2,1)S(1)}, bf16[1,4,64,256]{3,2,1,0:T(8,128)(2,1)}, u32[]{:S(2)}) copy-start(bf16[1,4,64,256]{3,2,1,0:T(8,128)(2,1)} %param.10) | copy-start | bytes 393220
  102.3 1.8 copy-start.18
  104.1 1.0 copy-start.5
  104.5 1.1 copy-start.3
  104.5 1.4 copy-start.9
  105.1 1.2 copy-start.7
  105.6 1.1 copy-start.11
  105.9 1.1 copy-start.15
  106.7 1.3 copy-start.12
  110.8 8.3 %collective-permute-start.9 = (f32[3328,128]{1,0:T(8,128)S(1)}, f32[3328,128]{1,0:T(8,128)S(1)}, u32[]{:S(2)}, u32[]{:S(2)}) collective-permute-start(f32[3328,128]{1,0:T(8,128)S(1)} %fusion.16), channel_id=1, source_target_pairs={{0,8},{8,0},{16,24},{24,16},{32,40},{40,32},{48,56},{56,48},{64,72... | collective-permute-start | bytes 5111816 | tf_op jit(solution)/shard_map/ppermute | solution.py:12
  173.4 6.7 %collective-permute-start.10 = (bf16[3328,128]{1,0:T(8,128)(2,1)S(1)}, bf16[3328,128]{1,0:T(8,128)(2,1)S(1)}, u32[]{:S(2)}, u32[]{:S(2)}) collective-permute-start(bf16[3328,128]{1,0:T(8,128)(2,1)S(1)} %bitcast.353), channel_id=1, source_target_pairs={{0,8},{8,0},{16,24},{24,16},{32,40},{40,32},{48,56},{56,48},{64,72... | collective-permute-start | bytes 2555912 | tf_op jit(solution)/shard_map/ppermute | solution.py:12

commit v2 on v0

v2 whole, which is shorter than its diff:
```python
import functools

import jax
import jax.numpy as jnp
from jax import lax
from jax.experimental import pallas as pl
from jax.experimental.pallas import tpu as pltpu
from jax.sharding import PartitionSpec as P

OPPOSITE = (0, 2, 1, 4, 3, 6, 5)
BRICKS = 4
C1 = 128
C2 = 256
LOCAL = 6 * BRICKS
EMPTY = LOCAL + 3
PLANE = 16
DEPTH = 8
CHUNK = 208
ONE_ROWS = 448
DOWN_ROWS = 1024
TWO_ROWS = 1792
EARLY = ONE_ROWS + DOWN_ROWS
HALF = EARLY + TWO_ROWS
F32 = jnp.float32
BF16 = jnp.bfloat16


def vmem():
    return pl.BlockSpec(memory_space=pltpu.VMEM)


def smem():
    return pl.BlockSpec(memory_space=pltpu.SMEM)


def call(body, scalars, arrays, outs, scratch=(), name=None):
    return pl.pallas_call(
        body,
        out_shape=[jax.ShapeDtypeStruct(shape, dtype) for shape, dtype in outs],
        in_specs=[smem() for _ in scalars] + [vmem() for _ in arrays],
        out_specs=[vmem() for _ in outs],
        scratch_shapes=list(scratch),
        compiler_params=pltpu.CompilerParams(vmem_limit_bytes=LIMIT),
        name=name,
    )(*scalars, *arrays)


LIMIT = 24 * 1024 * 1024


def nt_dot(left, right):
    return lax.dot_general(left, right, (((1,), (1,)), ((), ())), preferred_element_type=F32)


def tn_dot(left, right):
    return lax.dot_general(left, right, (((0,), (0,)), ((), ())), preferred_element_type=F32)


def face_value(ref, base, edge, axis, upper):
    area = edge * edge
    if axis == 0:
        return ref[pl.ds(base + upper * (edge * area - area), area), :]
    if axis == 1:
        return jnp.concatenate(
            [ref[pl.ds(base + row * area + upper * (area - edge), edge), :] for row in range(edge)]
        )
    return ref[pl.ds(base + upper * (edge - 1), area, stride=edge), :]


def write_face(ref, base, edge, axis, upper, value):
    area = edge * edge
    if axis == 0:
        ref[pl.ds(base + upper * (edge * area - area), area), :] = value
    elif axis == 1:
        for row in range(edge):
            ref[pl.ds(base + row * area + upper * (area - edge), edge), :] = value[
                row * edge : row * edge + edge
            ]
    else:
        ref[pl.ds(base + upper * (edge - 1), area, stride=edge), :] = value


def sent_face(ref, send_ref, edge, axis):
    face = send_ref[0, 0, axis, 0]
    brick = lax.div(face, 6)
    upper = lax.rem(face, 2)
    return face_value(ref, pl.multiple_of(brick * edge**3, edge**3), edge, axis, upper)


def write_tap(out, field, source_ref, received, edge, side):
    volume = edge**3
    total = BRICKS * volume
    axis, upper = side // 2, side % 2
    step = edge ** (2 - axis)
    if upper:
        out[pl.ds(0, total - step), :] = field[pl.ds(step, total - step), :]
    else:
        out[pl.ds(step, total - step), :] = field[pl.ds(0, total - step), :]
    border = received[axis][...].astype(F32)
    for brick in range(BRICKS):
        source = source_ref[0, brick, side]
        near = lax.div(jnp.minimum(source, LOCAL - 1), 6)
        slab = face_value(field, pl.multiple_of(near * volume, volume), edge, axis, 1 - upper)
        rim = jnp.where(
            source < LOCAL, slab, jnp.where(source < EMPTY, border, jnp.zeros_like(border))
        )
        write_face(out, brick * volume, edge, axis, upper, rim)


def sigmoid(value):
    return 1.0 / (1.0 + jnp.exp(-value))


def feature_faces(send_ref, features, face_0, face_1, face_2, brick_ref):
    for axis, out in enumerate((face_0, face_1, face_2)):
        face = send_ref[0, 0, axis, 0]
        base = pl.multiple_of(lax.div(face, 6) * 512, 512)
        upper = lax.rem(face, 2)
        brick_ref[axis] = features[pl.ds(base, 512), :].astype(F32)
        out[...] = face_value(brick_ref.at[axis], 0, 8, axis, upper).astype(BF16)


def level_one(
    source_ref, send_ref, features, got_0, got_1, got_2, weight, down,
    taps, slope, patches, coarse, face_0, face_1, face_2,
    field, shifted, hidden, cells,
):
    field[...] = features[...].astype(F32)
    taps[:, 0:C1] = features[...]
    for side in range(6):
        tap = shifted.at[side]
        write_tap(tap, field, source_ref, (got_0, got_1, got_2), 8, side)
        taps[:, C1 * (side + 1) : C1 * (side + 2)] = tap[...].astype(BF16)
    for brick in range(BRICKS):
        rows = pl.ds(512 * brick, 512)
        pre = jnp.dot(taps[rows, :], weight[...], preferred_element_type=F32)
        gate = sigmoid(pre)
        slope[rows, :] = gate * (1.0 + pre * (1.0 - gate))
        hidden[rows, :] = field[rows, :] + pre * gate
    low = lax.broadcasted_iota(jnp.int32, (1, 8, C1), 1) < 4
    for r in range(2):
        rows = hidden[pl.ds(r, 1024, stride=2), :].reshape(BRICKS * 4, 2, 2, 2, 8, C1)
        for a in range(2):
            left = rows[:, a, :, 0].reshape(32, 8, C1)
            right = rows[:, a, :, 1].reshape(32, 8, C1)
            first = jnp.where(low, left, pltpu.roll(right, 4, 1))
            second = jnp.where(low, pltpu.roll(left, 4, 1), right)
            for q, value in enumerate((first, second)):
                lane = ((a * 2 + q) * 2 + r) * C1
                patches[:, lane : lane + C1] = value.reshape(256, C1).astype(BF16)
    low_res = jnp.dot(patches[...], down[...], preferred_element_type=F32).astype(BF16)
    coarse[...] = low_res
    cells[0] = low_res[:, :C1].astype(F32)
    cells[1] = low_res[:, C1:].astype(F32)
    for axis, out in enumerate((face_0, face_1, face_2)):
        for part in range(2):
            out[:, C1 * part : C1 * part + C1] = sent_face(
                cells.at[part], send_ref, 4, axis
            ).astype(BF16)


def level_two_taps(source_ref, received, cells, shifted, taps):
    for side in range(6):
        for part in range(2):
            tap = shifted.at[side, part]
            lanes = pl.ds(C1 * part, C1)
            write_tap(
                tap, cells.at[part], source_ref, tuple(got.at[:, lanes] for got in received), 4, side
            )
            start = C2 * (side + 1) + C1 * part
            taps[:, start : start + C1] = tap[...].astype(BF16)


def level_two(
    source_ref, send_ref, coarse, got_0, got_1, got_2, weight, cotangent,
    taps, encoded, delta, face_0, face_1, face_2,
    cells, shifted,
):
    low_res = coarse[...]
    cells[0] = low_res[:, :C1].astype(F32)
    cells[1] = low_res[:, C1:].astype(F32)
    taps[:, 0:C2] = low_res
    level_two_taps(source_ref, (got_0, got_1, got_2), cells, shifted, taps)
    pre = jnp.dot(taps[...], weight[...], preferred_element_type=F32)
    gate = sigmoid(pre)
    encoded[...] = (low_res.astype(F32) + pre * gate).astype(BF16)
    change = (cotangent[...].astype(F32) * (gate * (1.0 + pre * (1.0 - gate)))).astype(BF16)
    delta[...] = change
    cells[0] = change[:, :C1].astype(F32)
    cells[1] = change[:, C1:].astype(F32)
    for axis, out in enumerate((face_0, face_1, face_2)):
        for part in range(2):
            out[:, C1 * part : C1 * part + C1] = sent_face(
                cells.at[part], send_ref, 4, axis
            ).astype(BF16)


def core_index():
    return lax.rem(lax.axis_index("scene"), 2)


def two_gradient(taps, delta, kept, sent, both):
    change = delta[...]
    for tap in range(7):
        grad = tn_dot(taps[:, C2 * tap : C2 * tap + C2], change)
        rows = pl.ds(C2 * tap, C2)
        both[0, rows, :] = grad[:, :C1]
        both[1, rows, :] = grad[:, C1:]
    core = core_index()
    kept[...] = both[core]
    sent[...] = both[1 - core].astype(BF16)


def backward(
    source_ref, delta, got_0, got_1, got_2, weight, cotangent, down, patches, slope, taps_one,
    kept, sent,
    cells, shifted, taps, patch_grad, spread, delta_one, both,
):
    change = delta[...]
    cells[0] = change[:, :C1].astype(F32)
    cells[1] = change[:, C1:].astype(F32)
    taps[:, 0:C2] = change
    level_two_taps(source_ref, (got_0, got_1, got_2), cells, shifted, taps)
    total = cotangent[...].astype(F32)
    for tap in range(7):
        lane = C2 * OPPOSITE[tap]
        total = total + nt_dot(taps[:, lane : lane + C2], weight[pl.ds(C2 * tap, C2), :])
    upstream = total.astype(BF16)
    grad_down = tn_dot(patches[...], upstream)
    both[0, pl.ds(ONE_ROWS, DOWN_ROWS), :] = grad_down[:, :C1]
    both[1, pl.ds(ONE_ROWS, DOWN_ROWS), :] = grad_down[:, C1:]
    patch_grad[...] = nt_dot(upstream, down[...])
    low = lax.broadcasted_iota(jnp.int32, (1, 8, C1), 1) < 4
    for r in range(2):
        halves = []
        for a in range(2):
            lane = (a * 4 + r) * C1
            first = patch_grad[:, lane : lane + C1].reshape(32, 8, C1)
            lane = lane + 2 * C1
            second = patch_grad[:, lane : lane + C1].reshape(32, 8, C1)
            left = jnp.where(low, first, pltpu.roll(second, 4, 1))
            right = jnp.where(low, pltpu.roll(first, 4, 1), second)
            halves.append(jnp.stack([left, right], axis=1).reshape(BRICKS * 4, 4, 8, C1))
        spread[pl.ds(r, 1024, stride=2), :] = jnp.stack(halves, axis=1).reshape(1024, C1)
    delta_one[...] = (spread[...] * slope[...]).astype(BF16)
    grad_one = tn_dot(delta_one[...], taps_one[...])
    for tap in range(7):
        block = grad_one[:, C1 * tap : C1 * tap + C1].T
        for start in range(0, C1, 64):
            row = C1 * tap + start
            both[row // ONE_ROWS, pl.ds(row % ONE_ROWS, 64), :] = block[start : start + 64]
    core = core_index()
    kept[...] = both[core]
    sent[...] = both[1 - core].astype(BF16)


def pair_sum(kept_a, got_a, kept_b, got_b, out):
    out[pl.ds(0, EARLY), :] = (kept_a[...] + got_a[...].astype(F32)).astype(BF16)
    out[pl.ds(EARLY, TWO_ROWS), :] = (kept_b[...] + got_b[...].astype(F32)).astype(BF16)
    out[pl.ds(HALF, PLANE * CHUNK - HALF), :] = jnp.zeros((PLANE * CHUNK - HALF, C1), BF16)


def group_sum(parts, out):
    total = parts[0].astype(F32)
    for index in range(1, parts.shape[0]):
        total = total + parts[index].astype(F32)
    total = total.astype(BF16)
    for index in range(out.shape[0]):
        out[index] = total


def unpack(own, other, one, down, two):
    def write(first, second):
        one[pl.ds(0, ONE_ROWS), :] = first[pl.ds(0, ONE_ROWS), :].astype(F32)
        one[pl.ds(ONE_ROWS, ONE_ROWS), :] = second[pl.ds(0, ONE_ROWS), :].astype(F32)
        for half, source in enumerate((first, second)):
            lanes = slice(C1 * half, C1 * half + C1)
            down[:, lanes] = source[pl.ds(ONE_ROWS, DOWN_ROWS), :].astype(F32)
            two[:, lanes] = source[pl.ds(EARLY, TWO_ROWS), :].astype(F32)

    core = core_index()

    @pl.when(core == 0)
    def _():
        write(own, other)

    @pl.when(core == 1)
    def _():
        write(other, own)


def swapped(value, axis, bit):
    mask = 2**bit
    pairs = [(source, source ^ mask) for source in range(lax.axis_size(axis))]
    return lax.ppermute(value, axis, pairs)


def exchanged(faces):
    return [swapped(face, "kd", bit) for bit, face in enumerate(faces)]


def on_device(features, send_faces, face_source, cotangent, conv_one, down_weight, conv_two):
    field = features.reshape(2048, C1)
    upstream = cotangent.reshape(256, C2)
    weight_one = conv_one.reshape(7 * C1, C1)
    weight_two = conv_two.reshape(7 * C2, C2)
    sent = call(
        feature_faces, (send_faces,), (field,), [((64, C1), BF16)] * 3,
        [pltpu.VMEM((3, 512, C1), F32)], "feature_faces",
    )
    taps_one, slope, patches, coarse, *sent = call(
        level_one, (face_source, send_faces), (field, *exchanged(sent), weight_one, down_weight),
        [((2048, 7 * C1), BF16), ((2048, C1), F32), ((256, 8 * C1), BF16), ((256, C2), BF16)]
        + [((16, C2), BF16)] * 3,
        [
            pltpu.VMEM((2048, C1), F32),
            pltpu.VMEM((6, 2048, C1), F32),
            pltpu.VMEM((2048, C1), F32),
            pltpu.VMEM((2, 256, C1), F32),
        ],
        "level_one",
    )
    taps_two, encoded, delta, *sent = call(
        level_two, (face_source, send_faces), (coarse, *exchanged(sent), weight_two, upstream),
        [((256, 7 * C2), BF16), ((256, C2), BF16), ((256, C2), BF16)] + [((16, C2), BF16)] * 3,
        [pltpu.VMEM((2, 256, C1), F32), pltpu.VMEM((6, 2, 256, C1), F32)],
        "level_two",
    )
    received = exchanged(sent)
    kept_two, sent_two = call(
        two_gradient, (), (taps_two, delta), [((TWO_ROWS, C1), F32), ((TWO_ROWS, C1), BF16)],
        [pltpu.VMEM((2, TWO_ROWS, C1), F32)], "two_gradient",
    )
    got_two = swapped(sent_two, "scene", 0)
    kept, sent = call(
        backward, (face_source,),
        (delta, *received, weight_two, upstream, down_weight, patches, slope, taps_one),
        [((EARLY, C1), F32), ((EARLY, C1), BF16)],
        [
            pltpu.VMEM((2, 256, C1), F32),
            pltpu.VMEM((6, 2, 256, C1), F32),
            pltpu.VMEM((256, 7 * C2), BF16),
            pltpu.VMEM((256, 8 * C1), F32),
            pltpu.VMEM((2048, C1), F32),
            pltpu.VMEM((2048, C1), BF16),
            pltpu.VMEM((2, EARLY, C1), F32),
        ],
        "backward",
    )
    got = swapped(sent, "scene", 0)
    groups = [[2 * chip + core for chip in range(PLANE)] for core in range(2)]
    (packed,) = call(
        pair_sum, (), (kept, got, kept_two, got_two), [((PLANE * CHUNK, C1), BF16)], (), "pair_sum"
    )
    parts = lax.all_to_all(
        packed.reshape(PLANE, CHUNK, C1), "scene", 0, 0, axis_index_groups=groups
    )
    (copies,) = call(group_sum, (), (parts,), [((DEPTH, CHUNK, C1), BF16)], (), "plane_sum")
    parts = lax.all_to_all(copies, "kd", 0, 0)
    (copies,) = call(group_sum, (), (parts,), [((PLANE, CHUNK, C1), BF16)], (), "depth_sum")
    own = lax.all_to_all(copies, "scene", 0, 0, axis_index_groups=groups)
    own = own.reshape(PLANE * CHUNK, C1)
    other = swapped(own, "scene", 0)
    one, down, two = call(
        unpack, (), (own, other),
        [((7 * C1, C1), F32), ((8 * C1, C2), F32), ((7 * C2, C2), F32)], (), "unpack",
    )
    return (
        encoded.reshape(1, BRICKS, 64, C2),
        one.reshape(7, C1, C1),
        down,
        two.reshape(7, C2, C2),
    )


def solution(mesh):
    placed = (
        P("scene", "kd", None, None),
        P("scene", "kd", None, None),
        P("scene", "kd", None),
        P("scene", "kd", None, None),
        P(),
        P(),
        P(),
    )
    return jax.shard_map(
        on_device,
        mesh=mesh,
        in_specs=placed,
        out_specs=(P("scene", "kd", None, None), P(), P(), P()),
        check_vma=False,
    )
```

time: 423 us -> 116 us (0.27)
  waiting for transfers between devices: 276 us -> 9.15 us
  blocking collectives: 0 us -> 53.8 us
  local copies, waits for them, and re-layouts: 57.9 us -> 6.62 us
  matrix products: 29.1 us -> 0 us
  between operations: 20.7 us -> 0.68 us
  other arithmetic: 17.8 us -> 0 us
  starting transfers between devices: 19.2 us -> 33.6 us
  Pallas kernels: 0 us -> 11.5 us
    psum x1 -> x0, waiting for transfers between devices: 271 us -> none  [on_device(): lax.psum((grad_one, grad_down, grad_two), ('scene', 'kd'))]
    all_to_all x0 -> x3, blocking collectives: none -> 53.8 us  [the longest x1 20.3 us: on_device(): lax.all_to_all(packed.reshape(PLANE, CHUNK, C1), 'scene', 0, 0, axis_inde...]
    dot_general x38 -> x0, matrix products: 29.1 us -> none  [the longest x14 8.37 us: weight_grads(): lax.dot_general(single.reshape(-1, chans), delta, (((0,), (0,)), ((), ())...]
    reshape x18 -> x0, local copies, waits for them, and re-layouts: 19 us -> none  [the longest x6 7.32 us: conv_apply(): taps[tap_index].reshape(-1, chans)]
    concatenate x15 -> x0, other arithmetic: 17.4 us -> none  [the longest x3 3.29 us: shift_taps(): jnp.concatenate([border[:, 4][:, :, :, None], blocks[:, :, :, :-1]], 3)]
    ppermute x9 -> x12, starting transfers between devices: 19.1 us -> 33.6 us  [swapped(): return lax.ppermute(value, axis, pairs)]
    pallas_call x0 -> x9, Pallas kernels: none -> 11.5 us  [call(): pl.pallas_call(body, out_shape=[jax.ShapeDtypeStruct(shape, dtype) for sh...]
    unnamed x100 -> x17, local copies, waits for them, and re-layouts: 17.6 us -> 6.62 us
  transfers between devices with their start and end apart: 10 -> 12, of which waited for: 3 -> 5; matrix products, arithmetic and copies ran while one was open for 2% -> 0% of each run, Pallas kernels for 0% -> 3%
where the time goes in v2:
time: 116 us; the launch traced here: 115 us
  blocking collectives  53.8 us (46%)
  starting transfers between devices  33.6 us (29%)
  Pallas kernels  11.5 us (10%)
  waiting for transfers between devices  9.15 us (8%)
  local copies, waits for them, and re-layouts  6.62 us (6%)
    ppermute x12, starting transfers between devices, swapped(): return lax.ppermute(value, axis, pairs)  33.6 us
    all_to_all x1, blocking collectives, on_device(): lax.all_to_all(packed.reshape(PLANE, CHUNK, C1), 'scene', 0, 0, axis_inde...  20.3 us
    all_to_all x1, blocking collectives, on_device(): parts = lax.all_to_all(copies, 'kd', 0, 0)  17.5 us
    all_to_all x1, blocking collectives, on_device(): own = lax.all_to_all(copies, 'scene', 0, 0, axis_index_groups=groups)  16 us
    pallas_call x9, Pallas kernels, call(): pl.pallas_call(body, out_shape=[jax.ShapeDtypeStruct(shape, dtype) for sh...  11.5 us
    ppermute x12, waiting for transfers between devices, swapped(): return lax.ppermute(value, axis, pairs)  9.15 us
    unnamed x17, local copies, waits for them, and re-layouts  6.62 us
  transfers between devices with their start and end apart: 12, of which 5 were waited for; matrix products, arithmetic and copies ran while one was open for 0% of the time, Pallas kernels for 3%

profile of v2, /device:TPU:1, one launch (start us, length us, event | category | flops | bytes accessed | tf_op | source)
XLA Modules:
  0.0 115.3 jit_solution(11463161913429972348)
XLA Ops:
  0.6 0.0 copy-start.1
  0.6 0.8 copy.13.send_ref
  1.5 0.0 copy-start.4
  1.5 1.0 copy-done.4
  2.5 0.7 feature_faces.1
  3.2 2.5 %collective-permute-start = (bf16[64,128]{1,0:T(8,128)(2,1)S(1)}, bf16[64,128]{1,0:T(8,128)(2,1)S(1)}, u32[]{:S(2)}, u32[]{:S(2)}) collective-permute-start(bf16[64,128]{1,0:T(8,128)(2,1)S(1)} %get-tuple-element.27), channel_id=1, source_target_pairs={{0,1},{1,0},{2,3},{3,2},{4,5},{5,4},{6,7},{7,6},{8,9},{9,8},{10,11... | collective-permute-start | bytes 49160 | tf_op jit(solution)/shard_map/ppermute | solution.py:295
  5.7 3.0 %collective-permute-start.1 = (bf16[64,128]{1,0:T(8,128)(2,1)S(1)}, bf16[64,128]{1,0:T(8,128)(2,1)S(1)}, u32[]{:S(2)}, u32[]{:S(2)}) collective-permute-start(bf16[64,128]{1,0:T(8,128)(2,1)S(1)} %get-tuple-element.28), channel_id=1, source_target_pairs={{0,2},{1,3},{2,0},{3,1},{4,6},{5,7},{6,4},{7,5},{8,10},{9,11},{10,... | collective-permute-start | bytes 49160 | tf_op jit(solution)/shard_map/ppermute | solution.py:295
  8.7 4.2 %collective-permute-start.2 = (bf16[64,128]{1,0:T(8,128)(2,1)S(1)}, bf16[64,128]{1,0:T(8,128)(2,1)S(1)}, u32[]{:S(2)}, u32[]{:S(2)}) collective-permute-start(bf16[64,128]{1,0:T(8,128)(2,1)S(1)} %get-tuple-element.29), channel_id=1, source_target_pairs={{0,4},{1,5},{2,6},{3,7},{4,0},{5,1},{6,2},{7,3},{8,12},{9,13},{10,... | collective-permute-start | bytes 49160 | tf_op jit(solution)/shard_map/ppermute | solution.py:295
  12.9 0.0 collective-permute-done.got_0
  12.9 0.0 collective-permute-done.1.got_1
  12.9 2.3 %collective-permute-done.2.got_2 = bf16[64,128]{1,0:T(8,128)(2,1)S(1)} collective-permute-done((bf16[64,128]{1,0:T(8,128)(2,1)S(1)}, bf16[64,128]{1,0:T(8,128)(2,1)S(1)}, u32[]{:S(2)}, u32[]{:S(2)}) %collective-permute-start.2) | collective-permute-done | bytes 16416 | tf_op jit(solution)/shard_map/ppermute | solution.py:295
  15.2 0.0 copy-start.2
  15.2 1.0 copy-done.2
  16.2 0.9 copy-done.6
  17.2 0.7 copy-done.7
  17.9 2.8 %level_one.1 = (bf16[2048,896]{1,0:T(8,128)(2,1)S(1)}, f32[2048,128]{1,0:T(8,128)S(1)}, bf16[256,1024]{1,0:T(8,128)(2,1)S(1)}, bf16[256,256]{1,0:T(8,128)(2,1)S(...) custom-call(s32[1,4,6]{2,1,0:T(4,128)S(1)} %copy-done.7, ...), custom_call_target="tpu_custom_call" | custom-call | tf_op jit(solution)/shard_map/level_one/pallas_call | solution.py:37
  20.6 0.3 collective-permute-start.3
  20.9 0.9 collective-permute-start.4
  21.8 5.1 %collective-permute-start.5 = (bf16[16,256]{1,0:T(8,128)(2,1)S(1)}, bf16[16,256]{1,0:T(8,128)(2,1)S(1)}, u32[]{:S(2)}, u32[]{:S(2)}) collective-permute-start(bf16[16,256]{1,0:T(8,128)(2,1)S(1)} %get-tuple-element.33), channel_id=1, source_target_pairs={{0,4},{1,5},{2,6},{3,7},{4,0},{5,1},{6,2},{7,3},{8,12},{9,13},{10,... | collective-permute-start | bytes 24584 | tf_op jit(solution)/shard_map/ppermute | solution.py:295
  26.8 0.0 collective-permute-done.3.got_0
  26.8 0.0 collective-permute-done.4.got_1
  26.8 1.3 %collective-permute-done.5.got_2 = bf16[16,256]{1,0:T(8,128)(2,1)S(1)} collective-permute-done((bf16[16,256]{1,0:T(8,128)(2,1)S(1)}, bf16[16,256]{1,0:T(8,128)(2,1)S(1)}, u32[]{:S(2)}, u32[]{:S(2)}) %collective-permute-start.5) | collective-permute-done | bytes 8224 | tf_op jit(solution)/shard_map/ppermute | solution.py:295
  28.2 1.2 %copy-done = bf16[7,256,256]{2,1,0:T(8,128)(2,1)S(1)} copy-done((bf16[7,256,256]{2,1,0:T(8,128)(2,1)S(1)}, bf16[7,256,256]{2,1,0:T(8,128)(2,1)}, u32[]{:S(2)}) %copy-start) | copy-done | bytes 917528
  29.3 0.9 copy-done.5
  30.2 1.9 %level_two.1 = (bf16[256,1792]{1,0:T(8,128)(2,1)S(1)}, bf16[256,256]{1,0:T(8,128)(2,1)}, bf16[256,256]{1,0:T(8,128)(2,1)S(1)}, bf16[16,256]{1,0:T(8,128)(2,1)S(1...) custom-call(s32[1,4,6]{2,1,0:T(4,128)S(1)} %copy-done.7, s32[1,1,3,1]{3,2,1,0:T(4,128)S(1)} %copy.13.send_ref, ...), custom_call_target="tpu_custom_call" | custom-call | tf_op jit(solution)/shard_map/level_two/pallas_call | solution.py:37
  32.1 0.8 two_gradient.1
  33.0 4.0 %collective-permute-start.10 = (bf16[1792,128]{1,0:T(8,128)(2,1)S(1)}, bf16[1792,128]{1,0:T(8,128)(2,1)S(1)}, u32[]{:S(2)}, u32[]{:S(2)}) collective-permute-start(bf16[1792,128]{1,0:T(8,128)(2,1)S(1)} %get-tuple-element.46), channel_id=1, source_target_pairs={{0,8},{8,0},{16,24},{24,16},{32,40},{40,32},{48,56},{56,48},{64,72... | collective-permute-start | bytes 1376264 | tf_op jit(solution)/shard_map/ppermute | solution.py:295
  37.0 0.3 collective-permute-start.6
  37.3 2.6 %collective-permute-start.7 = (bf16[16,256]{1,0:T(8,128)(2,1)S(1)}, bf16[16,256]{1,0:T(8,128)(2,1)S(1)}, u32[]{:S(2)}, u32[]{:S(2)}) collective-permute-start(bf16[16,256]{1,0:T(8,128)(2,1)S(1)} %get-tuple-element.37), channel_id=1, source_target_pairs={{0,2},{1,3},{2,0},{3,1},{4,6},{5,7},{6,4},{7,5},{8,10},{9,11},{10,... | collective-permute-start | bytes 24584 | tf_op jit(solution)/shard_map/ppermute | solution.py:295
  39.9 4.2 %collective-permute-start.8 = (bf16[16,256]{1,0:T(8,128)(2,1)S(1)}, bf16[16,256]{1,0:T(8,128)(2,1)S(1)}, u32[]{:S(2)}, u32[]{:S(2)}) collective-permute-start(bf16[16,256]{1,0:T(8,128)(2,1)S(1)} %get-tuple-element.38), channel_id=1, source_target_pairs={{0,4},{1,5},{2,6},{3,7},{4,0},{5,1},{6,2},{7,3},{8,12},{9,13},{10,... | collective-permute-start | bytes 24584 | tf_op jit(solution)/shard_map/ppermute | solution.py:295
  44.1 0.0 collective-permute-done.6.got_0
  44.1 0.0 collective-permute-done.7.got_1
  44.1 2.2 %collective-permute-done.8.got_2 = bf16[16,256]{1,0:T(8,128)(2,1)S(1)} collective-permute-done((bf16[16,256]{1,0:T(8,128)(2,1)S(1)}, bf16[16,256]{1,0:T(8,128)(2,1)S(1)}, u32[]{:S(2)}, u32[]{:S(2)}) %collective-permute-start.8) | collective-permute-done | bytes 8224 | tf_op jit(solution)/shard_map/ppermute | solution.py:295
  46.3 0.0 copy-done.1
  46.3 0.0 copy-done.3
  46.3 3.0 %backward.1 = (f32[1472,128]{1,0:T(8,128)S(1)}, bf16[1472,128]{1,0:T(8,128)(2,1)S(1)}) custom-call(s32[1,4,6]{2,1,0:T(4,128)S(1)} %copy-done.7, bf16[256,256]{1,0:T(8,128)(2,1)S(1)} %get-tuple-element.35.delta, bf16[16,256]{1,0:T(8,128)(2,1)S(1)} %collective-permute-done.6.got_0, bf16[16,256]{1,0:T(8,128)(2,1)S(1)} %collective-permute-done.7.got_1, ...), custom_call_target="tpu_custom_call" | custom-call | tf_op jit(solution)/shard_map/backward/pallas_call | solution.py:37
  49.4 1.9 %collective-permute-start.9 = (bf16[1472,128]{1,0:T(8,128)(2,1)S(1)}, bf16[1472,128]{1,0:T(8,128)(2,1)S(1)}, u32[]{:S(2)}, u32[]{:S(2)}) collective-permute-start(bf16[1472,128]{1,0:T(8,128)(2,1)S(1)} %get-tuple-element.43), channel_id=1, source_target_pairs={{0,8},{8,0},{16,24},{24,16},{32,40},{40,32},{48,56},{56,48},{64,72... | collective-permute-start | bytes 1130504 | tf_op jit(solution)/shard_map/ppermute | solution.py:295
  51.2 1.3 %collective-permute-done.9.got_a = bf16[1472,128]{1,0:T(8,128)(2,1)S(1)} collective-permute-done((bf16[1472,128]{1,0:T(8,128)(2,1)S(1)}, bf16[1472,128]{1,0:T(8,128)(2,1)S(1)}, u32[]{:S(2)}, u32[]{:S(2)}) %collective-permute-start.9) | collective-permute-done | bytes 376864 | tf_op jit(solution)/shard_map/ppermute | solution.py:295
  52.6 0.0 collective-permute-done.10.got_b
  52.6 0.2 pair_sum.1
  52.7 20.3 %all_to_all.15.parts = bf16[16,208,128]{2,1,0:T(8,128)(2,1)S(1)} all-to-all(bf16[16,208,128]{2,1,0:T(8,128)(2,1)S(1)} %bitcast.13), channel_id=1, replica_groups={{0,16,32,48,64,80,96,112,128,144,160,176,192,208,224,240},{8,24,40,56,7..., dimensions={0} | all-to-all | bytes 1703936 | tf_op jit(solution)/shard_map/all_to_all | solution.py:355
  73.0 0.1 plane_sum.1
  73.1 17.5 %all_to_all.16.parts = bf16[8,208,128]{2,1,0:T(8,128)(2,1)S(1)} all-to-all(bf16[8,208,128]{2,1,0:T(8,128)(2,1)S(1)} %plane_sum.1), channel_id=1, replica_groups=mesh['scene'=32,'kd'=8] {'kd'}, dimensions={0} | all-to-all | bytes 851968 | tf_op jit(solution)/shard_map/all_to_all | solution.py:359
  90.6 0.1 depth_sum.1
  90.6 16.0 %all_to_all.17 = bf16[16,208,128]{2,1,0:T(8,128)(2,1)S(1)} all-to-all(bf16[16,208,128]{2,1,0:T(8,128)(2,1)S(1)} %depth_sum.1), channel_id=1, replica_groups={{0,16,32,48,64,80,96,112,128,144,160,176,192,208,224,240},{8,24,40,56,7..., dimensions={0} | all-to-all | bytes 1703936 | tf_op jit(solution)/shard_map/all_to_all | solution.py:361
  106.7 4.7 %collective-permute-start.11 = (bf16[3328,128]{1,0:T(8,128)(2,1)S(1)}, bf16[3328,128]{1,0:T(8,128)(2,1)S(1)}, u32[]{:S(2)}, u32[]{:S(2)}) collective-permute-start(bf16[3328,128]{1,0:T(8,128)(2,1)S(1)} %bitcast.11), channel_id=1, source_target_pairs={{0,8},{8,0},{16,24},{24,16},{32,40},{40,32},{48,56},{56,48},{64,72... | collective-permute-start | bytes 2555912 | tf_op jit(solution)/shard_map/ppermute | solution.py:295
  111.4 2.0 %collective-permute-done.11.other = bf16[3328,128]{1,0:T(8,128)(2,1)S(1)} collective-permute-done((bf16[3328,128]{1,0:T(8,128)(2,1)S(1)}, bf16[3328,128]{1,0:T(8,128)(2,1)S(1)}, u32[]{:S(2)}, u32[]{:S(2)}) %collective-permute-start.11) | collective-permute-done | bytes 852000 | tf_op jit(solution)/shard_map/ppermute | solution.py:295
  113.4 2.0 %unpack.1 = (f32[896,128]{1,0:T(8,128)}, f32[1024,256]{1,0:T(8,128)}, f32[1792,256]{1,0:T(8,128)}) custom-call(bf16[3328,128]{1,0:T(8,128)(2,1)S(1)} %bitcast.12, bf16[3328,128]{1,0:T(8,128)(2,1)S(1)} %collective-permute-done.11.other), custom_call_target="tpu_custom_call" | custom-call | tf_op jit(solution)/shard_map/unpack/pallas_call | solution.py:37
  (5 shorter events, 0.0 us)
Async XLA Ops:
  0.6 45.7 %copy-start.1 = (bf16[7,256,256]{2,1,0:T(8,128)(2,1)S(1)}, bf16[7,256,256]{2,1,0:T(8,128)(2,1)}, u32[]{:S(2)}) copy-start(bf16[7,256,256]{2,1,0:T(8,128)(2,1)} %param.13) | copy-start | bytes 2752516
  1.5 1.0 copy-start.4
  3.2 9.7 %collective-permute-start = (bf16[64,128]{1,0:T(8,128)(2,1)S(1)}, bf16[64,128]{1,0:T(8,128)(2,1)S(1)}, u32[]{:S(2)}, u32[]{:S(2)}) collective-permute-start(bf16[64,128]{1,0:T(8,128)(2,1)S(1)} %get-tuple-element.27), channel_id=1, source_target_pairs={{0,1},{1,0},{2,3},{3,2},{4,5},{5,4},{6,7},{7,6},{8,9},{9,8},{10,11... | collective-permute-start | bytes 49160 | tf_op jit(solution)/shard_map/ppermute | solution.py:295
  5.7 7.2 %collective-permute-start.1 = (bf16[64,128]{1,0:T(8,128)(2,1)S(1)}, bf16[64,128]{1,0:T(8,128)(2,1)S(1)}, u32[]{:S(2)}, u32[]{:S(2)}) collective-permute-start(bf16[64,128]{1,0:T(8,128)(2,1)S(1)} %get-tuple-element.28), channel_id=1, source_target_pairs={{0,2},{1,3},{2,0},{3,1},{4,6},{5,7},{6,4},{7,5},{8,10},{9,11},{10,... | collective-permute-start | bytes 49160 | tf_op jit(solution)/shard_map/ppermute | solution.py:295
  8.7 6.5 %collective-permute-start.2 = (bf16[64,128]{1,0:T(8,128)(2,1)S(1)}, bf16[64,128]{1,0:T(8,128)(2,1)S(1)}, u32[]{:S(2)}, u32[]{:S(2)}) collective-permute-start(bf16[64,128]{1,0:T(8,128)(2,1)S(1)} %get-tuple-element.29), channel_id=1, source_target_pairs={{0,4},{1,5},{2,6},{3,7},{4,0},{5,1},{6,2},{7,3},{8,12},{9,13},{10,... | collective-permute-start | bytes 49160 | tf_op jit(solution)/shard_map/ppermute | solution.py:295
  15.2 1.0 copy-start.2
  16.2 0.9 copy-start.6
  17.2 0.7 copy-start.7
  17.9 28.5 %copy-start.3 = (bf16[1024,256]{1,0:T(8,128)(2,1)S(1)}, bf16[1024,256]{1,0:T(8,128)(2,1)}, u32[]{:S(2)}) copy-start(bf16[1024,256]{1,0:T(8,128)(2,1)} %down.3) | copy-start | bytes 1572868
  20.6 6.2 %collective-permute-start.3 = (bf16[16,256]{1,0:T(8,128)(2,1)S(1)}, bf16[16,256]{1,0:T(8,128)(2,1)S(1)}, u32[]{:S(2)}, u32[]{:S(2)}) collective-permute-start(bf16[16,256]{1,0:T(8,128)(2,1)S(1)} %get-tuple-element.31), channel_id=1, source_target_pairs={{0,1},{1,0},{2,3},{3,2},{4,5},{5,4},{6,7},{7,6},{8,9},{9,8},{10,11... | collective-permute-start | bytes 24584 | tf_op jit(solution)/shard_map/ppermute | solution.py:295
  20.9 5.9 %collective-permute-start.4 = (bf16[16,256]{1,0:T(8,128)(2,1)S(1)}, bf16[16,256]{1,0:T(8,128)(2,1)S(1)}, u32[]{:S(2)}, u32[]{:S(2)}) collective-permute-start(bf16[16,256]{1,0:T(8,128)(2,1)S(1)} %get-tuple-element.32), channel_id=1, source_target_pairs={{0,2},{1,3},{2,0},{3,1},{4,6},{5,7},{6,4},{7,5},{8,10},{9,11},{10,... | collective-permute-start | bytes 24584 | tf_op jit(solution)/shard_map/ppermute | solution.py:295
  21.8 6.4 %collective-permute-start.5 = (bf16[16,256]{1,0:T(8,128)(2,1)S(1)}, bf16[16,256]{1,0:T(8,128)(2,1)S(1)}, u32[]{:S(2)}, u32[]{:S(2)}) collective-permute-start(bf16[16,256]{1,0:T(8,128)(2,1)S(1)} %get-tuple-element.33), channel_id=1, source_target_pairs={{0,4},{1,5},{2,6},{3,7},{4,0},{5,1},{6,2},{7,3},{8,12},{9,13},{10,... | collective-permute-start | bytes 24584 | tf_op jit(solution)/shard_map/ppermute | solution.py:295
  28.2 1.2 %copy-start = (bf16[7,256,256]{2,1,0:T(8,128)(2,1)S(1)}, bf16[7,256,256]{2,1,0:T(8,128)(2,1)}, u32[]{:S(2)}) copy-start(bf16[7,256,256]{2,1,0:T(8,128)(2,1)} %param.13) | copy-start | bytes 2752516
  29.3 0.9 copy-start.5
  33.0 19.6 %collective-permute-start.10 = (bf16[1792,128]{1,0:T(8,128)(2,1)S(1)}, bf16[1792,128]{1,0:T(8,128)(2,1)S(1)}, u32[]{:S(2)}, u32[]{:S(2)}) collective-permute-start(bf16[1792,128]{1,0:T(8,128)(2,1)S(1)} %get-tuple-element.46), channel_id=1, source_target_pairs={{0,8},{8,0},{16,24},{24,16},{32,40},{40,32},{48,56},{56,48},{64,72... | collective-permute-start | bytes 1376264 | tf_op jit(solution)/shard_map/ppermute | solution.py:295
  37.0 7.1 %collective-permute-start.6 = (bf16[16,256]{1,0:T(8,128)(2,1)S(1)}, bf16[16,256]{1,0:T(8,128)(2,1)S(1)}, u32[]{:S(2)}, u32[]{:S(2)}) collective-permute-start(bf16[16,256]{1,0:T(8,128)(2,1)S(1)} %get-tuple-element.36), channel_id=1, source_target_pairs={{0,1},{1,0},{2,3},{3,2},{4,5},{5,4},{6,7},{7,6},{8,9},{9,8},{10,11... | collective-permute-start | bytes 24584 | tf_op jit(solution)/shard_map/ppermute | solution.py:295
  37.3 6.9 %collective-permute-start.7 = (bf16[16,256]{1,0:T(8,128)(2,1)S(1)}, bf16[16,256]{1,0:T(8,128)(2,1)S(1)}, u32[]{:S(2)}, u32[]{:S(2)}) collective-permute-start(bf16[16,256]{1,0:T(8,128)(2,1)S(1)} %get-tuple-element.37), channel_id=1, source_target_pairs={{0,2},{1,3},{2,0},{3,1},{4,6},{5,7},{6,4},{7,5},{8,10},{9,11},{10,... | collective-permute-start | bytes 24584 | tf_op jit(solution)/shard_map/ppermute | solution.py:295
  39.9 6.4 %collective-permute-start.8 = (bf16[16,256]{1,0:T(8,128)(2,1)S(1)}, bf16[16,256]{1,0:T(8,128)(2,1)S(1)}, u32[]{:S(2)}, u32[]{:S(2)}) collective-permute-start(bf16[16,256]{1,0:T(8,128)(2,1)S(1)} %get-tuple-element.38), channel_id=1, source_target_pairs={{0,4},{1,5},{2,6},{3,7},{4,0},{5,1},{6,2},{7,3},{8,12},{9,13},{10,... | collective-permute-start | bytes 24584 | tf_op jit(solution)/shard_map/ppermute | solution.py:295
  49.4 3.2 %collective-permute-start.9 = (bf16[1472,128]{1,0:T(8,128)(2,1)S(1)}, bf16[1472,128]{1,0:T(8,128)(2,1)S(1)}, u32[]{:S(2)}, u32[]{:S(2)}) collective-permute-start(bf16[1472,128]{1,0:T(8,128)(2,1)S(1)} %get-tuple-element.43), channel_id=1, source_target_pairs={{0,8},{8,0},{16,24},{24,16},{32,40},{40,32},{48,56},{56,48},{64,72... | collective-permute-start | bytes 1130504 | tf_op jit(solution)/shard_map/ppermute | solution.py:295
  106.7 6.7 %collective-permute-start.11 = (bf16[3328,128]{1,0:T(8,128)(2,1)S(1)}, bf16[3328,128]{1,0:T(8,128)(2,1)S(1)}, u32[]{:S(2)}, u32[]{:S(2)}) collective-permute-start(bf16[3328,128]{1,0:T(8,128)(2,1)S(1)} %bitcast.11), channel_id=1, source_target_pairs={{0,8},{8,0},{16,24},{24,16},{32,40},{40,32},{48,56},{56,48},{64,72... | collective-permute-start | bytes 2555912 | tf_op jit(solution)/shard_map/ppermute | solution.py:295

commit v3 on v2

--- a/solution.py
+++ b/solution.py
@@ -6,6 +6,7 @@
 from jax.experimental import pallas as pl
 from jax.experimental.pallas import tpu as pltpu
 from jax.sharding import PartitionSpec as P
+
 
 OPPOSITE = (0, 2, 1, 4, 3, 6, 5)
 BRICKS = 4
@@ -33,19 +34,33 @@
     return pl.BlockSpec(memory_space=pltpu.SMEM)
 
 
-def call(body, scalars, arrays, outs, scratch=(), name=None):
+def hbm():
+    return pl.BlockSpec(memory_space=pltpu.HBM)
+
+
+LIMIT = 24 * 1024 * 1024
+
+
+def call(body, inputs, outs, scratch=(), aliases=None):
     return pl.pallas_call(
         body,
-        out_shape=[jax.ShapeDtypeStruct(shape, dtype) for shape, dtype in outs],
-        in_specs=[smem() for _ in scalars] + [vmem() for _ in arrays],
-        out_specs=[vmem() for _ in outs],
+        out_shape=[jax.ShapeDtypeStruct(shape, dtype) for _, shape, dtype in outs],
+        in_specs=[place() for place, _ in inputs],
+        out_specs=[place() for place, _, _ in outs],
         scratch_shapes=list(scratch),
+        input_output_aliases=aliases or {},
         compiler_params=pltpu.CompilerParams(vmem_limit_bytes=LIMIT),
-        name=name,
-    )(*scalars, *arrays)
-
-
-LIMIT = 24 * 1024 * 1024
+    )(*[value for _, value in inputs])
+
+
+def begin(sem, *pairs):
+    copies = [
+        pltpu.make_async_copy(source, target, sem.at[index])
+        for index, (source, target) in enumerate(pairs)
+    ]
+    for copy in copies:
+        copy.start()
+    return copies
 
 
 def nt_dot(left, right):
@@ -81,7 +96,7 @@
 
 
 def sent_face(ref, send_ref, edge, axis):
-    face = send_ref[0, 0, axis, 0]
+    face = send_ref[0, axis]
     brick = lax.div(face, 6)
     upper = lax.rem(face, 2)
     return face_value(ref, pl.multiple_of(brick * edge**3, edge**3), edge, axis, upper)
@@ -111,26 +126,34 @@
     return 1.0 / (1.0 + jnp.exp(-value))
 
 
-def feature_faces(send_ref, features, face_0, face_1, face_2, brick_ref):
+def feature_faces(
+    features, sides, sources, field, source_out, face_0, face_1, face_2, send_ref, brick_ref, sem
+):
+    copies = begin(sem, (sides, send_ref), (features, field), (sources, source_out))
+    for copy in copies:
+        copy.wait()
     for axis, out in enumerate((face_0, face_1, face_2)):
-        face = send_ref[0, 0, axis, 0]
+        face = send_ref[0, axis]
         base = pl.multiple_of(lax.div(face, 6) * 512, 512)
-        upper = lax.rem(face, 2)
-        brick_ref[axis] = features[pl.ds(base, 512), :].astype(F32)
-        out[...] = face_value(brick_ref.at[axis], 0, 8, axis, upper).astype(BF16)
+        brick_ref[axis] = field[pl.ds(base, 512), :].astype(F32)
+        out[...] = face_value(brick_ref.at[axis], 0, 8, axis, lax.rem(face, 2)).astype(BF16)
 
 
 def level_one(
-    source_ref, send_ref, features, got_0, got_1, got_2, weight, down,
-    taps, slope, patches, coarse, face_0, face_1, face_2,
-    field, shifted, hidden, cells,
+    source_ref, send_ref, features, got_0, got_1, got_2, conv, down_far, conv_next, cot_far,
+    taps, slope, patches, coarse, face_0, face_1, face_2, down, weight_next, cotangent,
+    field, shifted, hidden, cells, weight, sem,
 ):
+    copies = begin(
+        sem, (conv, weight), (down_far, down), (conv_next, weight_next), (cot_far, cotangent)
+    )
     field[...] = features[...].astype(F32)
     taps[:, 0:C1] = features[...]
     for side in range(6):
         tap = shifted.at[side]
         write_tap(tap, field, source_ref, (got_0, got_1, got_2), 8, side)
         taps[:, C1 * (side + 1) : C1 * (side + 2)] = tap[...].astype(BF16)
+    copies[0].wait()
     for brick in range(BRICKS):
         rows = pl.ds(512 * brick, 512)
         pre = jnp.dot(taps[rows, :], weight[...], preferred_element_type=F32)
@@ -148,6 +171,7 @@
             for q, value in enumerate((first, second)):
                 lane = ((a * 2 + q) * 2 + r) * C1
                 patches[:, lane : lane + C1] = value.reshape(256, C1).astype(BF16)
+    copies[1].wait()
     low_res = jnp.dot(patches[...], down[...], preferred_element_type=F32).astype(BF16)
     coarse[...] = low_res
     cells[0] = low_res[:, :C1].astype(F32)
@@ -157,6 +181,8 @@
             out[:, C1 * part : C1 * part + C1] = sent_face(
                 cells.at[part], send_ref, 4, axis
             ).astype(BF16)
+    for copy in copies[2:]:
+        copy.wait()
 
 
 def level_two_taps(source_ref, received, cells, shifted, taps):
@@ -173,7 +199,7 @@
 
 def level_two(
     source_ref, send_ref, coarse, got_0, got_1, got_2, weight, cotangent,
-    taps, encoded, delta, face_0, face_1, face_2,
+    taps, bent, delta, face_0, face_1, face_2,
     cells, shifted,
 ):
     low_res = coarse[...]
@@ -183,7 +209,7 @@
     level_two_taps(source_ref, (got_0, got_1, got_2), cells, shifted, taps)
     pre = jnp.dot(taps[...], weight[...], preferred_element_type=F32)
     gate = sigmoid(pre)
-    encoded[...] = (low_res.astype(F32) + pre * gate).astype(BF16)
+    bent[...] = pre * gate
     change = (cotangent[...].astype(F32) * (gate * (1.0 + pre * (1.0 - gate)))).astype(BF16)
     delta[...] = change
     cells[0] = change[:, :C1].astype(F32)
@@ -199,7 +225,8 @@
     return lax.rem(lax.axis_index("scene"), 2)
 
 
-def two_gradient(taps, delta, kept, sent, both):
+def two_gradient(taps, delta, coarse, bent, kept, sent, encoded, both):
+    encoded[...] = (coarse[...].astype(F32) + bent[...]).astype(BF16)
     change = delta[...]
     for tap in range(7):
         grad = tn_dot(taps[:, C2 * tap : C2 * tap + C2], change)
@@ -269,24 +296,25 @@
         out[index] = total
 
 
-def unpack(own, other, one, down, two):
-    def write(first, second):
-        one[pl.ds(0, ONE_ROWS), :] = first[pl.ds(0, ONE_ROWS), :].astype(F32)
-        one[pl.ds(ONE_ROWS, ONE_ROWS), :] = second[pl.ds(0, ONE_ROWS), :].astype(F32)
-        for half, source in enumerate((first, second)):
-            lanes = slice(C1 * half, C1 * half + C1)
-            down[:, lanes] = source[pl.ds(ONE_ROWS, DOWN_ROWS), :].astype(F32)
-            two[:, lanes] = source[pl.ds(EARLY, TWO_ROWS), :].astype(F32)
-
-    core = core_index()
-
-    @pl.when(core == 0)
-    def _():
-        write(own, other)
-
-    @pl.when(core == 1)
-    def _():
-        write(other, own)
+def unpack(turned, source, *refs):
+    one, down, two, stage, sem = refs[-5:]
+    half = core_index()
+    if turned:
+        half = 1 - half
+    lanes = pl.ds(pl.multiple_of(half * C1, C1), C1)
+    targets = (
+        (EARLY, TWO_ROWS, two.at[:, lanes]),
+        (ONE_ROWS, DOWN_ROWS, down.at[:, lanes]),
+        (0, ONE_ROWS, one.at[pl.ds(pl.multiple_of(half * ONE_ROWS, ONE_ROWS), ONE_ROWS), :]),
+    )
+    copies = []
+    for index, (start, size, target) in enumerate(targets):
+        rows = pl.ds(start, size)
+        stage[rows, :] = source[rows, :].astype(F32)
+        copies.append(pltpu.make_async_copy(stage.at[rows, :], target, sem.at[index]))
+        copies[-1].start()
+    for copy in copies:
+        copy.wait()
 
 
 def swapped(value, axis, bit):
@@ -296,46 +324,73 @@
 
 
 def exchanged(faces):
-    return [swapped(face, "kd", bit) for bit, face in enumerate(faces)]
-
-
-def on_device(features, send_faces, face_source, cotangent, conv_one, down_weight, conv_two):
-    field = features.reshape(2048, C1)
-    upstream = cotangent.reshape(256, C2)
+    got = []
+    for bit, face in enumerate(faces):
+        got.append(swapped(face, "kd", bit))
+    return got
+
+
+def step(features, send_faces, face_source, cotangent, conv_one, down_weight, conv_two):
+    sides = send_faces.reshape(1, 3)
     weight_one = conv_one.reshape(7 * C1, C1)
     weight_two = conv_two.reshape(7 * C2, C2)
-    sent = call(
-        feature_faces, (send_faces,), (field,), [((64, C1), BF16)] * 3,
-        [pltpu.VMEM((3, 512, C1), F32)], "feature_faces",
-    )
-    taps_one, slope, patches, coarse, *sent = call(
-        level_one, (face_source, send_faces), (field, *exchanged(sent), weight_one, down_weight),
-        [((2048, 7 * C1), BF16), ((2048, C1), F32), ((256, 8 * C1), BF16), ((256, C2), BF16)]
-        + [((16, C2), BF16)] * 3,
+    dma = pltpu.SemaphoreType.DMA
+    field, sources, *sent = call(
+        feature_faces,
+        [(hbm, features.reshape(2048, C1)), (hbm, sides), (hbm, face_source)],
+        [(vmem, (2048, C1), BF16), (vmem, (1, BRICKS, 6), jnp.int32)]
+        + [(vmem, (64, C1), BF16)] * 3,
+        [pltpu.SMEM((1, 3), jnp.int32), pltpu.VMEM((3, 512, C1), F32), dma((3,))],
+    )
+    received = exchanged(sent)
+    taps_one, slope, patches, coarse, face_0, face_1, face_2, down, weight, upstream = call(
+        level_one,
+        [(smem, sources), (smem, sides), (vmem, field)]
+        + [(vmem, got) for got in received]
+        + [(hbm, weight_one), (hbm, down_weight), (hbm, weight_two)]
+        + [(hbm, cotangent.reshape(256, C2))],
+        [
+            (vmem, (2048, 7 * C1), BF16),
+            (vmem, (2048, C1), F32),
+            (vmem, (256, 8 * C1), BF16),
+            (vmem, (256, C2), BF16),
+        ]
+        + [(vmem, (16, C2), BF16)] * 3
+        + [(vmem, (8 * C1, C2), BF16), (vmem, (7 * C2, C2), BF16), (vmem, (256, C2), BF16)],
         [
             pltpu.VMEM((2048, C1), F32),
             pltpu.VMEM((6, 2048, C1), F32),
             pltpu.VMEM((2048, C1), F32),
             pltpu.VMEM((2, 256, C1), F32),
+            pltpu.VMEM((7 * C1, C1), BF16),
+            dma((4,)),
         ],
-        "level_one",
-    )
-    taps_two, encoded, delta, *sent = call(
-        level_two, (face_source, send_faces), (coarse, *exchanged(sent), weight_two, upstream),
-        [((256, 7 * C2), BF16), ((256, C2), BF16), ((256, C2), BF16)] + [((16, C2), BF16)] * 3,
+    )
+    received = exchanged((face_0, face_1, face_2))
+    taps_two, bent, delta, *sent = call(
+        level_two,
+        [(smem, sources), (smem, sides), (vmem, coarse)]
+        + [(vmem, got) for got in received]
+        + [(vmem, weight), (vmem, upstream)],
+        [(vmem, (256, 7 * C2), BF16), (vmem, (256, C2), F32), (vmem, (256, C2), BF16)]
+        + [(vmem, (16, C2), BF16)] * 3,
         [pltpu.VMEM((2, 256, C1), F32), pltpu.VMEM((6, 2, 256, C1), F32)],
-        "level_two",
     )
     received = exchanged(sent)
-    kept_two, sent_two = call(
-        two_gradient, (), (taps_two, delta), [((TWO_ROWS, C1), F32), ((TWO_ROWS, C1), BF16)],
-        [pltpu.VMEM((2, TWO_ROWS, C1), F32)], "two_gradient",
+    kept_two, sent_two, encoded = call(
+        two_gradient,
+        [(vmem, taps_two), (vmem, delta), (vmem, coarse), (vmem, bent)],
+        [(vmem, (TWO_ROWS, C1), F32), (vmem, (TWO_ROWS, C1), BF16), (vmem, (256, C2), BF16)],
+        [pltpu.VMEM((2, TWO_ROWS, C1), F32)],
     )
     got_two = swapped(sent_two, "scene", 0)
     kept, sent = call(
-        backward, (face_source,),
-        (delta, *received, weight_two, upstream, down_weight, patches, slope, taps_one),
-        [((EARLY, C1), F32), ((EARLY, C1), BF16)],
+        backward,
+        [(smem, sources), (vmem, delta)]
+        + [(vmem, got) for got in received]
+        + [(vmem, weight), (vmem, upstream), (vmem, down), (vmem, patches), (vmem, slope)]
+        + [(vmem, taps_one)],
+        [(vmem, (EARLY, C1), F32), (vmem, (EARLY, C1), BF16)],
         [
             pltpu.VMEM((2, 256, C1), F32),
             pltpu.VMEM((6, 2, 256, C1), F32),
@@ -345,30 +400,37 @@
             pltpu.VMEM((2048, C1), BF16),
             pltpu.VMEM((2, EARLY, C1), F32),
         ],
-        "backward",
     )
     got = swapped(sent, "scene", 0)
     groups = [[2 * chip + core for chip in range(PLANE)] for core in range(2)]
     (packed,) = call(
-        pair_sum, (), (kept, got, kept_two, got_two), [((PLANE * CHUNK, C1), BF16)], (), "pair_sum"
+        pair_sum,
+        [(vmem, kept), (vmem, got), (vmem, kept_two), (vmem, got_two)],
+        [(vmem, (PLANE * CHUNK, C1), BF16)],
     )
     parts = lax.all_to_all(
         packed.reshape(PLANE, CHUNK, C1), "scene", 0, 0, axis_index_groups=groups
     )
-    (copies,) = call(group_sum, (), (parts,), [((DEPTH, CHUNK, C1), BF16)], (), "plane_sum")
+    (copies,) = call(group_sum, [(vmem, parts)], [(vmem, (DEPTH, CHUNK, C1), BF16)])
     parts = lax.all_to_all(copies, "kd", 0, 0)
-    (copies,) = call(group_sum, (), (parts,), [((PLANE, CHUNK, C1), BF16)], (), "depth_sum")
+    (copies,) = call(group_sum, [(vmem, parts)], [(vmem, (PLANE, CHUNK, C1), BF16)])
     own = lax.all_to_all(copies, "scene", 0, 0, axis_index_groups=groups)
     own = own.reshape(PLANE * CHUNK, C1)
     other = swapped(own, "scene", 0)
-    one, down, two = call(
-        unpack, (), (own, other),
-        [((7 * C1, C1), F32), ((8 * C1, C2), F32), ((7 * C2, C2), F32)], (), "unpack",
+    shapes = [(hbm, (7 * C1, C1), F32), (hbm, (8 * C1, C2), F32), (hbm, (7 * C2, C2), F32)]
+    scratch = [pltpu.VMEM((HALF, C1), F32), dma((3,))]
+    partial = call(functools.partial(unpack, False), [(vmem, own)], shapes, scratch)
+    one, low, two = call(
+        functools.partial(unpack, True),
+        [(vmem, other)] + [(hbm, value) for value in partial],
+        shapes,
+        scratch,
+        {1: 0, 2: 1, 3: 2},
     )
     return (
         encoded.reshape(1, BRICKS, 64, C2),
         one.reshape(7, C1, C1),
-        down,
+        low,
         two.reshape(7, C2, C2),
     )
 
@@ -384,7 +446,7 @@
         P(),
     )
     return jax.shard_map(
-        on_device,
+        step,
         mesh=mesh,
         in_specs=placed,
         out_specs=(P("scene", "kd", None, None), P(), P(), P()),

time: 116 us -> 116 us (level)
  Pallas kernels: 11.5 us -> 13.1 us
  waiting for transfers between devices: 9.15 us -> 7.91 us
    pallas_call x9 -> x10, Pallas kernels: 11.5 us -> 13.1 us  [call(): pl.pallas_call(body, out_shape=[jax.ShapeDtypeStruct(shape, dtype) for _,...]
    ppermute x12, waiting for transfers between devices: 9.15 us -> 7.91 us  [swapped(): return lax.ppermute(value, axis, pairs)]
    unnamed x17 -> x14, local copies, waits for them, and re-layouts: 6.62 us -> 6.43 us
  transfers between devices with their start and end apart: 12 -> 12, of which waited for: 5 -> 5; matrix products, arithmetic and copies ran while one was open for 0% -> 0% of each run, Pallas kernels for 3% -> 4%
where the time goes in v3:
time: 116 us; the launch traced here: 115 us
  blocking collectives  53.8 us (46%)
  starting transfers between devices  33.5 us (29%)
  Pallas kernels  13.1 us (11%)
  waiting for transfers between devices  7.91 us (7%)
  local copies, waits for them, and re-layouts  6.43 us (6%)
    ppermute x12, starting transfers between devices, swapped(): return lax.ppermute(value, axis, pairs)  33.5 us
    all_to_all x1, blocking collectives, step(): lax.all_to_all(packed.reshape(PLANE, CHUNK, C1), 'scene', 0, 0, axis_inde...  20.3 us
    all_to_all x1, blocking collectives, step(): parts = lax.all_to_all(copies, 'kd', 0, 0)  17.5 us
    all_to_all x1, blocking collectives, step(): own = lax.all_to_all(copies, 'scene', 0, 0, axis_index_groups=groups)  16 us
    pallas_call x10, Pallas kernels, call(): pl.pallas_call(body, out_shape=[jax.ShapeDtypeStruct(shape, dtype) for _,...  13.1 us
    ppermute x12, waiting for transfers between devices, swapped(): return lax.ppermute(value, axis, pairs)  7.91 us
    unnamed x14, local copies, waits for them, and re-layouts  6.43 us
  transfers between devices with their start and end apart: 12, of which 5 were waited for; matrix products, arithmetic and copies ran while one was open for 0% of the time, Pallas kernels for 4%

profile of v3, /device:TPU:1, one launch (start us, length us, event | category | flops | bytes accessed | tf_op | source)
XLA Modules:
  0.0 115.4 jit_solution(11709322332698054044)
XLA Ops:
  0.6 0.0 copy-start.1
  0.6 1.0 copy-done.1
  1.7 0.0 copy-start.5
  1.7 0.7 copy-done.5
  2.3 0.0 copy-start.6
  2.3 0.7 copy-done.6
  3.0 0.7 shard_map.102
  3.7 2.5 %collective-permute-start = (bf16[64,128]{1,0:T(8,128)(2,1)S(1)}, bf16[64,128]{1,0:T(8,128)(2,1)S(1)}, u32[]{:S(2)}, u32[]{:S(2)}) collective-permute-start(bf16[64,128]{1,0:T(8,128)(2,1)S(1)} %get-tuple-element.38), channel_id=1, source_target_pairs={{0,1},{1,0},{2,3},{3,2},{4,5},{5,4},{6,7},{7,6},{8,9},{9,8},{10,11... | collective-permute-start | bytes 49160 | tf_op jit(solution)/shard_map/ppermute | solution.py:323
  6.2 3.0 %collective-permute-start.1 = (bf16[64,128]{1,0:T(8,128)(2,1)S(1)}, bf16[64,128]{1,0:T(8,128)(2,1)S(1)}, u32[]{:S(2)}, u32[]{:S(2)}) collective-permute-start(bf16[64,128]{1,0:T(8,128)(2,1)S(1)} %get-tuple-element.39), channel_id=1, source_target_pairs={{0,2},{1,3},{2,0},{3,1},{4,6},{5,7},{6,4},{7,5},{8,10},{9,11},{10,... | collective-permute-start | bytes 49160 | tf_op jit(solution)/shard_map/ppermute | solution.py:323
  9.2 4.2 %collective-permute-start.2 = (bf16[64,128]{1,0:T(8,128)(2,1)S(1)}, bf16[64,128]{1,0:T(8,128)(2,1)S(1)}, u32[]{:S(2)}, u32[]{:S(2)}) collective-permute-start(bf16[64,128]{1,0:T(8,128)(2,1)S(1)} %get-tuple-element.40), channel_id=1, source_target_pairs={{0,4},{1,5},{2,6},{3,7},{4,0},{5,1},{6,2},{7,3},{8,12},{9,13},{10,... | collective-permute-start | bytes 49160 | tf_op jit(solution)/shard_map/ppermute | solution.py:323
  13.4 0.0 collective-permute-done.got_0
  13.4 0.0 collective-permute-done.1.got_1
  13.4 2.3 %collective-permute-done.2.got_2 = bf16[64,128]{1,0:T(8,128)(2,1)S(1)} collective-permute-done((bf16[64,128]{1,0:T(8,128)(2,1)S(1)}, bf16[64,128]{1,0:T(8,128)(2,1)S(1)}, u32[]{:S(2)}, u32[]{:S(2)}) %collective-permute-start.2) | collective-permute-done | bytes 16416 | tf_op jit(solution)/shard_map/ppermute | solution.py:323
  15.7 0.0 copy-start
  15.7 1.2 %copy-done = bf16[7,256,256]{2,1,0:T(8,128)(2,1)S(1)} copy-done((bf16[7,256,256]{2,1,0:T(8,128)(2,1)S(1)}, bf16[7,256,256]{2,1,0:T(8,128)(2,1)}, u32[]{:S(2)}) %copy-start) | copy-done | bytes 917528
  16.9 1.0 copy-done.2
  17.9 0.9 copy-done.3
  18.9 0.9 copy-done.4
  19.8 4.0 %shard_map.103 = (bf16[2048,896]{1,0:T(8,128)(2,1)S(1)}, f32[2048,128]{1,0:T(8,128)S(1)}, bf16[256,1024]{1,0:T(8,128)(2,1)S(1)}, bf16[256,256]{1,0:T(8,128)(2,1)...) custom-call(s32[1,4,6]{2,1,0:T(4,128)S(1)} %get-tuple-element.36.sou, ...), custom_call_target="tpu_custom_call" | custom-call | tf_op jit(solution)/shard_map/pallas_call | solution.py:45
  23.8 0.3 collective-permute-start.3
  24.0 0.9 collective-permute-start.4
  24.9 5.1 %collective-permute-start.5 = (bf16[16,256]{1,0:T(8,128)(2,1)S(1)}, bf16[16,256]{1,0:T(8,128)(2,1)S(1)}, u32[]{:S(2)}, u32[]{:S(2)}) collective-permute-start(bf16[16,256]{1,0:T(8,128)(2,1)S(1)} %get-tuple-element.44), channel_id=1, source_target_pairs={{0,4},{1,5},{2,6},{3,7},{4,0},{5,1},{6,2},{7,3},{8,12},{9,13},{10,... | collective-permute-start | bytes 24584 | tf_op jit(solution)/shard_map/ppermute | solution.py:323
  30.0 0.0 collective-permute-done.3.got_0
  30.0 0.0 collective-permute-done.4.got_1
  30.0 1.3 %collective-permute-done.5.got_2 = bf16[16,256]{1,0:T(8,128)(2,1)S(1)} collective-permute-done((bf16[16,256]{1,0:T(8,128)(2,1)S(1)}, bf16[16,256]{1,0:T(8,128)(2,1)S(1)}, u32[]{:S(2)}, u32[]{:S(2)}) %collective-permute-start.5) | collective-permute-done | bytes 8224 | tf_op jit(solution)/shard_map/ppermute | solution.py:323
  31.3 1.2 %shard_map.104 = (bf16[256,1792]{1,0:T(8,128)(2,1)S(1)}, f32[256,256]{1,0:T(8,128)S(1)}, bf16[256,256]{1,0:T(8,128)(2,1)S(1)}, bf16[16,256]{1,0:T(8,128)(2,1)S(1...) custom-call(s32[1,4,6]{2,1,0:T(4,128)S(1)} %get-tuple-element.36.source_ref, s32[1,3]{1,0:T(1,128)S(1)} %bitcast.19, ...), custom_call_target="tpu_custom_call" | custom-call | tf_op jit(solution)/shard_map/pallas_call | solution.py:45
  32.5 1.4 %shard_map.105 = (f32[1792,128]{1,0:T(8,128)S(1)}, bf16[1792,128]{1,0:T(8,128)(2,1)S(1)}, bf16[256,256]{1,0:T(8,128)(2,1)}) custom-call(bf16[256,1792]{1,0:T(8,128)(2,1)S(1)} %get-tuple-element.47.taps, bf16[256,256]{1,0:T(8,128)(2,1)S(1)} %get-tuple-element.48.delta, bf16[256,256]{1,0:T(8,128)(2,1)S(1)} %get-tuple-element.41.coarse, ...), custom_call_target="tpu_custom_call" | custom-call | tf_op jit(solution)/shard_map/pallas_call | solution.py:45
  33.9 3.9 %collective-permute-start.10 = (bf16[1792,128]{1,0:T(8,128)(2,1)S(1)}, bf16[1792,128]{1,0:T(8,128)(2,1)S(1)}, u32[]{:S(2)}, u32[]{:S(2)}) collective-permute-start(bf16[1792,128]{1,0:T(8,128)(2,1)S(1)} %get-tuple-element.61), channel_id=1, source_target_pairs={{0,8},{8,0},{16,24},{24,16},{32,40},{40,32},{48,56},{56,48},{64,72... | collective-permute-start | bytes 1376264 | tf_op jit(solution)/shard_map/ppermute | solution.py:323
  37.8 0.3 collective-permute-start.6
  38.1 2.6 %collective-permute-start.7 = (bf16[16,256]{1,0:T(8,128)(2,1)S(1)}, bf16[16,256]{1,0:T(8,128)(2,1)S(1)}, u32[]{:S(2)}, u32[]{:S(2)}) collective-permute-start(bf16[16,256]{1,0:T(8,128)(2,1)S(1)} %get-tuple-element.52), channel_id=1, source_target_pairs={{0,2},{1,3},{2,0},{3,1},{4,6},{5,7},{6,4},{7,5},{8,10},{9,11},{10,... | collective-permute-start | bytes 24584 | tf_op jit(solution)/shard_map/ppermute | solution.py:323
  40.8 4.2 %collective-permute-start.8 = (bf16[16,256]{1,0:T(8,128)(2,1)S(1)}, bf16[16,256]{1,0:T(8,128)(2,1)S(1)}, u32[]{:S(2)}, u32[]{:S(2)}) collective-permute-start(bf16[16,256]{1,0:T(8,128)(2,1)S(1)} %get-tuple-element.53), channel_id=1, source_target_pairs={{0,4},{1,5},{2,6},{3,7},{4,0},{5,1},{6,2},{7,3},{8,12},{9,13},{10,... | collective-permute-start | bytes 24584 | tf_op jit(solution)/shard_map/ppermute | solution.py:323
  45.0 0.0 collective-permute-done.6.got_0
  45.0 0.0 collective-permute-done.7.got_1
  45.0 2.2 %collective-permute-done.8.got_2 = bf16[16,256]{1,0:T(8,128)(2,1)S(1)} collective-permute-done((bf16[16,256]{1,0:T(8,128)(2,1)S(1)}, bf16[16,256]{1,0:T(8,128)(2,1)S(1)}, u32[]{:S(2)}, u32[]{:S(2)}) %collective-permute-start.8) | collective-permute-done | bytes 8224 | tf_op jit(solution)/shard_map/ppermute | solution.py:323
  47.2 3.0 %shard_map.106 = (f32[1472,128]{1,0:T(8,128)S(1)}, bf16[1472,128]{1,0:T(8,128)(2,1)S(1)}) custom-call(s32[1,4,6]{2,1,0:T(4,128)S(1)} %get-tuple-element.36.source_ref, bf16[256,256]{1,0:T(8,128)(2,1)S(1)} %get-tuple-element.48.delta, bf16[16,256]{1,0:T(8,128)(2,1)S(1)} %collective-permute-done.6.got_0, bf16[16,256]{1,0:T(8,128)(2,1)S(1)} %collective-permute-done.7.got_1, ...), custom_call_target="tpu_custom_call" | custom-call | tf_op jit(solution)/shard_map/pallas_call | solution.py:45
  50.2 1.8 %collective-permute-start.9 = (bf16[1472,128]{1,0:T(8,128)(2,1)S(1)}, bf16[1472,128]{1,0:T(8,128)(2,1)S(1)}, u32[]{:S(2)}, u32[]{:S(2)}) collective-permute-start(bf16[1472,128]{1,0:T(8,128)(2,1)S(1)} %get-tuple-element.59), channel_id=1, source_target_pairs={{0,8},{8,0},{16,24},{24,16},{32,40},{40,32},{48,56},{56,48},{64,72... | collective-permute-start | bytes 1130504 | tf_op jit(solution)/shard_map/ppermute | solution.py:323
  52.0 1.3 %collective-permute-done.9.got_a = bf16[1472,128]{1,0:T(8,128)(2,1)S(1)} collective-permute-done((bf16[1472,128]{1,0:T(8,128)(2,1)S(1)}, bf16[1472,128]{1,0:T(8,128)(2,1)S(1)}, u32[]{:S(2)}, u32[]{:S(2)}) %collective-permute-start.9) | collective-permute-done | bytes 376864 | tf_op jit(solution)/shard_map/ppermute | solution.py:323
  53.3 0.0 collective-permute-done.10.got_b
  53.3 0.2 shard_map.107
  53.5 20.3 %all_to_all.15.parts = bf16[16,208,128]{2,1,0:T(8,128)(2,1)S(1)} all-to-all(bf16[16,208,128]{2,1,0:T(8,128)(2,1)S(1)} %bitcast.12), channel_id=1, replica_groups={{0,16,32,48,64,80,96,112,128,144,160,176,192,208,224,240},{8,24,40,56,7..., dimensions={0} | all-to-all | bytes 1703936 | tf_op jit(solution)/shard_map/all_to_all | solution.py:411
  73.8 0.1 shard_map.108
  73.9 17.5 %all_to_all.16.parts = bf16[8,208,128]{2,1,0:T(8,128)(2,1)S(1)} all-to-all(bf16[8,208,128]{2,1,0:T(8,128)(2,1)S(1)} %shard_map.108), channel_id=1, replica_groups=mesh['scene'=32,'kd'=8] {'kd'}, dimensions={0} | all-to-all | bytes 851968 | tf_op jit(solution)/shard_map/all_to_all | solution.py:415
  91.4 0.1 shard_map.109
  91.4 16.0 %all_to_all.17 = bf16[16,208,128]{2,1,0:T(8,128)(2,1)S(1)} all-to-all(bf16[16,208,128]{2,1,0:T(8,128)(2,1)S(1)} %shard_map.109), channel_id=1, replica_groups={{0,16,32,48,64,80,96,112,128,144,160,176,192,208,224,240},{8,24,40,56,7..., dimensions={0} | all-to-all | bytes 1703936 | tf_op jit(solution)/shard_map/all_to_all | solution.py:417
  107.5 4.7 %collective-permute-start.11 = (bf16[3328,128]{1,0:T(8,128)(2,1)S(1)}, bf16[3328,128]{1,0:T(8,128)(2,1)S(1)}, u32[]{:S(2)}, u32[]{:S(2)}) collective-permute-start(bf16[3328,128]{1,0:T(8,128)(2,1)S(1)} %bitcast.10), channel_id=1, source_target_pairs={{0,8},{8,0},{16,24},{24,16},{32,40},{40,32},{48,56},{56,48},{64,72... | collective-permute-start | bytes 2555912 | tf_op jit(solution)/shard_map/ppermute | solution.py:323
  112.1 1.2 %shard_map.110 = (f32[896,128]{1,0:T(8,128)}, f32[1024,256]{1,0:T(8,128)}, f32[1792,256]{1,0:T(8,128)}) custom-call(bf16[3328,128]{1,0:T(8,128)(2,1)S(1)} %bitcast.11), custom_call_target="tpu_custom_call" | custom-call | tf_op jit(solution)/shard_map/pallas_call | solution.py:45
  113.4 0.8 collective-permute-done.11.source
  114.1 1.2 %shard_map.111 = (f32[896,128]{1,0:T(8,128)}, f32[1024,256]{1,0:T(8,128)}, f32[1792,256]{1,0:T(8,128)}) custom-call(bf16[3328,128]{1,0:T(8,128)(2,1)S(1)} %collective-permute-done.11.source, f32[896,128]{1,0:T(8,128)} %get-tuple-element.62.refs_0_, ...), custom_call_target="tpu_custom_call", output_to_operand_aliasing={{0}: (1, {}), {1}: (2, {}), {2}: (3, {})} | custom-call | tf_op jit(solution)/shard_map/pallas_call | solution.py:45
  (3 shorter events, 0.0 us)
Async XLA Ops:
  0.6 1.0 copy-start.1
  1.7 0.7 copy-start.5
  2.3 0.7 copy-start.6
  3.7 9.7 %collective-permute-start = (bf16[64,128]{1,0:T(8,128)(2,1)S(1)}, bf16[64,128]{1,0:T(8,128)(2,1)S(1)}, u32[]{:S(2)}, u32[]{:S(2)}) collective-permute-start(bf16[64,128]{1,0:T(8,128)(2,1)S(1)} %get-tuple-element.38), channel_id=1, source_target_pairs={{0,1},{1,0},{2,3},{3,2},{4,5},{5,4},{6,7},{7,6},{8,9},{9,8},{10,11... | collective-permute-start | bytes 49160 | tf_op jit(solution)/shard_map/ppermute | solution.py:323
  6.2 7.2 %collective-permute-start.1 = (bf16[64,128]{1,0:T(8,128)(2,1)S(1)}, bf16[64,128]{1,0:T(8,128)(2,1)S(1)}, u32[]{:S(2)}, u32[]{:S(2)}) collective-permute-start(bf16[64,128]{1,0:T(8,128)(2,1)S(1)} %get-tuple-element.39), channel_id=1, source_target_pairs={{0,2},{1,3},{2,0},{3,1},{4,6},{5,7},{6,4},{7,5},{8,10},{9,11},{10,... | collective-permute-start | bytes 49160 | tf_op jit(solution)/shard_map/ppermute | solution.py:323
  9.2 6.5 %collective-permute-start.2 = (bf16[64,128]{1,0:T(8,128)(2,1)S(1)}, bf16[64,128]{1,0:T(8,128)(2,1)S(1)}, u32[]{:S(2)}, u32[]{:S(2)}) collective-permute-start(bf16[64,128]{1,0:T(8,128)(2,1)S(1)} %get-tuple-element.40), channel_id=1, source_target_pairs={{0,4},{1,5},{2,6},{3,7},{4,0},{5,1},{6,2},{7,3},{8,12},{9,13},{10,... | collective-permute-start | bytes 49160 | tf_op jit(solution)/shard_map/ppermute | solution.py:323
  15.7 1.2 %copy-start = (bf16[7,256,256]{2,1,0:T(8,128)(2,1)S(1)}, bf16[7,256,256]{2,1,0:T(8,128)(2,1)}, u32[]{:S(2)}) copy-start(bf16[7,256,256]{2,1,0:T(8,128)(2,1)} %param.13) | copy-start | bytes 2752516
  16.9 1.0 copy-start.2
  17.9 0.9 copy-start.3
  18.9 0.9 copy-start.4
  23.8 6.2 %collective-permute-start.3 = (bf16[16,256]{1,0:T(8,128)(2,1)S(1)}, bf16[16,256]{1,0:T(8,128)(2,1)S(1)}, u32[]{:S(2)}, u32[]{:S(2)}) collective-permute-start(bf16[16,256]{1,0:T(8,128)(2,1)S(1)} %get-tuple-element.42), channel_id=1, source_target_pairs={{0,1},{1,0},{2,3},{3,2},{4,5},{5,4},{6,7},{7,6},{8,9},{9,8},{10,11... | collective-permute-start | bytes 24584 | tf_op jit(solution)/shard_map/ppermute | solution.py:323
  24.0 5.9 %collective-permute-start.4 = (bf16[16,256]{1,0:T(8,128)(2,1)S(1)}, bf16[16,256]{1,0:T(8,128)(2,1)S(1)}, u32[]{:S(2)}, u32[]{:S(2)}) collective-permute-start(bf16[16,256]{1,0:T(8,128)(2,1)S(1)} %get-tuple-element.43), channel_id=1, source_target_pairs={{0,2},{1,3},{2,0},{3,1},{4,6},{5,7},{6,4},{7,5},{8,10},{9,11},{10,... | collective-permute-start | bytes 24584 | tf_op jit(solution)/shard_map/ppermute | solution.py:323
  24.9 6.4 %collective-permute-start.5 = (bf16[16,256]{1,0:T(8,128)(2,1)S(1)}, bf16[16,256]{1,0:T(8,128)(2,1)S(1)}, u32[]{:S(2)}, u32[]{:S(2)}) collective-permute-start(bf16[16,256]{1,0:T(8,128)(2,1)S(1)} %get-tuple-element.44), channel_id=1, source_target_pairs={{0,4},{1,5},{2,6},{3,7},{4,0},{5,1},{6,2},{7,3},{8,12},{9,13},{10,... | collective-permute-start | bytes 24584 | tf_op jit(solution)/shard_map/ppermute | solution.py:323
  33.9 19.4 %collective-permute-start.10 = (bf16[1792,128]{1,0:T(8,128)(2,1)S(1)}, bf16[1792,128]{1,0:T(8,128)(2,1)S(1)}, u32[]{:S(2)}, u32[]{:S(2)}) collective-permute-start(bf16[1792,128]{1,0:T(8,128)(2,1)S(1)} %get-tuple-element.61), channel_id=1, source_target_pairs={{0,8},{8,0},{16,24},{24,16},{32,40},{40,32},{48,56},{56,48},{64,72... | collective-permute-start | bytes 1376264 | tf_op jit(solution)/shard_map/ppermute | solution.py:323
  37.8 7.1 %collective-permute-start.6 = (bf16[16,256]{1,0:T(8,128)(2,1)S(1)}, bf16[16,256]{1,0:T(8,128)(2,1)S(1)}, u32[]{:S(2)}, u32[]{:S(2)}) collective-permute-start(bf16[16,256]{1,0:T(8,128)(2,1)S(1)} %get-tuple-element.51), channel_id=1, source_target_pairs={{0,1},{1,0},{2,3},{3,2},{4,5},{5,4},{6,7},{7,6},{8,9},{9,8},{10,11... | collective-permute-start | bytes 24584 | tf_op jit(solution)/shard_map/ppermute | solution.py:323
  38.1 6.8 %collective-permute-start.7 = (bf16[16,256]{1,0:T(8,128)(2,1)S(1)}, bf16[16,256]{1,0:T(8,128)(2,1)S(1)}, u32[]{:S(2)}, u32[]{:S(2)}) collective-permute-start(bf16[16,256]{1,0:T(8,128)(2,1)S(1)} %get-tuple-element.52), channel_id=1, source_target_pairs={{0,2},{1,3},{2,0},{3,1},{4,6},{5,7},{6,4},{7,5},{8,10},{9,11},{10,... | collective-permute-start | bytes 24584 | tf_op jit(solution)/shard_map/ppermute | solution.py:323
  40.8 6.4 %collective-permute-start.8 = (bf16[16,256]{1,0:T(8,128)(2,1)S(1)}, bf16[16,256]{1,0:T(8,128)(2,1)S(1)}, u32[]{:S(2)}, u32[]{:S(2)}) collective-permute-start(bf16[16,256]{1,0:T(8,128)(2,1)S(1)} %get-tuple-element.53), channel_id=1, source_target_pairs={{0,4},{1,5},{2,6},{3,7},{4,0},{5,1},{6,2},{7,3},{8,12},{9,13},{10,... | collective-permute-start | bytes 24584 | tf_op jit(solution)/shard_map/ppermute | solution.py:323
  50.2 3.1 %collective-permute-start.9 = (bf16[1472,128]{1,0:T(8,128)(2,1)S(1)}, bf16[1472,128]{1,0:T(8,128)(2,1)S(1)}, u32[]{:S(2)}, u32[]{:S(2)}) collective-permute-start(bf16[1472,128]{1,0:T(8,128)(2,1)S(1)} %get-tuple-element.59), channel_id=1, source_target_pairs={{0,8},{8,0},{16,24},{24,16},{32,40},{40,32},{48,56},{56,48},{64,72... | collective-permute-start | bytes 1130504 | tf_op jit(solution)/shard_map/ppermute | solution.py:323
  107.5 6.7 %collective-permute-start.11 = (bf16[3328,128]{1,0:T(8,128)(2,1)S(1)}, bf16[3328,128]{1,0:T(8,128)(2,1)S(1)}, u32[]{:S(2)}, u32[]{:S(2)}) collective-permute-start(bf16[3328,128]{1,0:T(8,128)(2,1)S(1)} %bitcast.10), channel_id=1, source_target_pairs={{0,8},{8,0},{16,24},{24,16},{32,40},{40,32},{48,56},{56,48},{64,72... | collective-permute-start | bytes 2555912 | tf_op jit(solution)/shard_map/ppermute | solution.py:323

commit v4 on v3

--- a/solution.py
+++ b/solution.py
@@ -13,7 +13,6 @@
 C1 = 128
 C2 = 256
 LOCAL = 6 * BRICKS
-EMPTY = LOCAL + 3
 PLANE = 16
 DEPTH = 8
 CHUNK = 208
@@ -41,6 +40,10 @@
 LIMIT = 24 * 1024 * 1024
 
 
+def far(value):
+    return pltpu.with_memory_space_constraint(value, pltpu.HBM)
+
+
 def call(body, inputs, outs, scratch=(), aliases=None):
     return pl.pallas_call(
         body,
@@ -50,7 +53,7 @@
         scratch_shapes=list(scratch),
         input_output_aliases=aliases or {},
         compiler_params=pltpu.CompilerParams(vmem_limit_bytes=LIMIT),
-    )(*[value for _, value in inputs])
+    )(*[far(value) if place is hbm else value for place, value in inputs])
 
 
 def begin(sem, *pairs):
@@ -96,13 +99,13 @@
 
 
 def sent_face(ref, send_ref, edge, axis):
-    face = send_ref[0, axis]
+    face = jnp.bitwise_and(send_ref[0, axis], 31)
     brick = lax.div(face, 6)
     upper = lax.rem(face, 2)
     return face_value(ref, pl.multiple_of(brick * edge**3, edge**3), edge, axis, upper)
 
 
-def write_tap(out, field, source_ref, received, edge, side):
+def write_tap(out, field, source_ref, edge, side):
     volume = edge**3
     total = BRICKS * volume
     axis, upper = side // 2, side % 2
@@ -111,15 +114,26 @@
         out[pl.ds(0, total - step), :] = field[pl.ds(step, total - step), :]
     else:
         out[pl.ds(step, total - step), :] = field[pl.ds(0, total - step), :]
-    border = received[axis][...].astype(F32)
     for brick in range(BRICKS):
         source = source_ref[0, brick, side]
         near = lax.div(jnp.minimum(source, LOCAL - 1), 6)
         slab = face_value(field, pl.multiple_of(near * volume, volume), edge, axis, 1 - upper)
-        rim = jnp.where(
-            source < LOCAL, slab, jnp.where(source < EMPTY, border, jnp.zeros_like(border))
-        )
+        rim = jnp.where(source < LOCAL, slab, jnp.zeros_like(slab))
         write_face(out, brick * volume, edge, axis, upper, rim)
+
+
+def far_rims(info_ref, edge, received):
+    volume = edge**3
+    for axis in range(3):
+        info = info_ref[0, axis]
+        face = jnp.bitwise_and(info, 31)
+        base = pl.multiple_of(lax.div(face, 6) * volume, volume)
+        rim = received[axis][...]
+        yield axis, lax.rem(face, 2), base, jnp.where(info >= 32, rim, jnp.zeros_like(rim))
+
+
+def add_face(ref, base, edge, axis, upper, value):
+    write_face(ref, base, edge, axis, upper, face_value(ref, base, edge, axis, upper) + value)
 
 
 def sigmoid(value):
@@ -127,39 +141,61 @@
 
 
 def feature_faces(
-    features, sides, sources, field, source_out, face_0, face_1, face_2, send_ref, brick_ref, sem
+    features, sides, sources, field, source_out, info_out, face_0, face_1, face_2,
+    send_ref, source_ref, brick_ref, sem,
 ):
-    copies = begin(sem, (sides, send_ref), (features, field), (sources, source_out))
+    copies = begin(
+        sem, (sides, send_ref), (features, field), (sources, source_out), (sources, source_ref)
+    )
     for copy in copies:
         copy.wait()
+    place = lax.broadcasted_iota(jnp.int32, (1, C1), 1)
+    infos = jnp.zeros((1, C1), jnp.int32)
     for axis, out in enumerate((face_0, face_1, face_2)):
         face = send_ref[0, axis]
-        base = pl.multiple_of(lax.div(face, 6) * 512, 512)
+        brick = lax.div(face, 6)
+        linked = source_ref[0, brick, lax.rem(face, 6)] == LOCAL + axis
+        infos = jnp.where(place == axis, face + jnp.where(linked, 32, 0), infos)
+        base = pl.multiple_of(brick * 512, 512)
         brick_ref[axis] = field[pl.ds(base, 512), :].astype(F32)
         out[...] = face_value(brick_ref.at[axis], 0, 8, axis, lax.rem(face, 2)).astype(BF16)
-
-
-def level_one(
-    source_ref, send_ref, features, got_0, got_1, got_2, conv, down_far, conv_next, cot_far,
-    taps, slope, patches, coarse, face_0, face_1, face_2, down, weight_next, cotangent,
-    field, shifted, hidden, cells, weight, sem,
+    info_out[...] = infos
+
+
+def ready_one(
+    source_ref, field_near, conv, down_far, taps, pre, weight, down, field, shifted, sem
 ):
-    copies = begin(
-        sem, (conv, weight), (down_far, down), (conv_next, weight_next), (cot_far, cotangent)
-    )
-    field[...] = features[...].astype(F32)
-    taps[:, 0:C1] = features[...]
+    copies = begin(sem, (conv, weight), (down_far, down))
+    field[...] = field_near[...].astype(F32)
+    taps[:, 0:C1] = field_near[...]
     for side in range(6):
         tap = shifted.at[side]
-        write_tap(tap, field, source_ref, (got_0, got_1, got_2), 8, side)
+        write_tap(tap, field, source_ref, 8, side)
         taps[:, C1 * (side + 1) : C1 * (side + 2)] = tap[...].astype(BF16)
     copies[0].wait()
     for brick in range(BRICKS):
         rows = pl.ds(512 * brick, 512)
-        pre = jnp.dot(taps[rows, :], weight[...], preferred_element_type=F32)
-        gate = sigmoid(pre)
-        slope[rows, :] = gate * (1.0 + pre * (1.0 - gate))
-        hidden[rows, :] = field[rows, :] + pre * gate
+        pre[rows, :] = jnp.dot(taps[rows, :], weight[...], preferred_element_type=F32)
+    copies[1].wait()
+
+
+def level_one(
+    info_ref, field, got_0, got_1, got_2, weight, down, pre_near, conv_next, cot_far,
+    slope, patches, coarse, face_0, face_1, face_2, weight_next, cotangent,
+    pre, hidden, cells, sem,
+):
+    copies = begin(sem, (conv_next, weight_next), (cot_far, cotangent))
+    pre[...] = pre_near[...]
+    for axis, upper, base, rim in far_rims(info_ref, 8, (got_0, got_1, got_2)):
+        rows = pl.ds(pl.multiple_of(C1 * (2 * axis + upper + 1), C1), C1)
+        add = jnp.dot(rim, weight[rows, :], preferred_element_type=F32)
+        add_face(pre, base, 8, axis, upper, add)
+    for brick in range(BRICKS):
+        rows = pl.ds(512 * brick, 512)
+        value = pre[rows, :]
+        gate = sigmoid(value)
+        slope[rows, :] = gate * (1.0 + value * (1.0 - gate))
+        hidden[rows, :] = field[rows, :].astype(F32) + value * gate
     low = lax.broadcasted_iota(jnp.int32, (1, 8, C1), 1) < 4
     for r in range(2):
         rows = hidden[pl.ds(r, 1024, stride=2), :].reshape(BRICKS * 4, 2, 2, 2, 8, C1)
@@ -171,88 +207,111 @@
             for q, value in enumerate((first, second)):
                 lane = ((a * 2 + q) * 2 + r) * C1
                 patches[:, lane : lane + C1] = value.reshape(256, C1).astype(BF16)
-    copies[1].wait()
     low_res = jnp.dot(patches[...], down[...], preferred_element_type=F32).astype(BF16)
     coarse[...] = low_res
-    cells[0] = low_res[:, :C1].astype(F32)
-    cells[1] = low_res[:, C1:].astype(F32)
-    for axis, out in enumerate((face_0, face_1, face_2)):
+    send_faces_of(low_res, info_ref, cells, (face_0, face_1, face_2))
+    for copy in copies:
+        copy.wait()
+
+
+def split(value, cells):
+    cells[0] = value[:, :C1].astype(F32)
+    cells[1] = value[:, C1:].astype(F32)
+
+
+def send_faces_of(value, send_ref, cells, outs):
+    split(value, cells)
+    for axis, out in enumerate(outs):
         for part in range(2):
             out[:, C1 * part : C1 * part + C1] = sent_face(
                 cells.at[part], send_ref, 4, axis
             ).astype(BF16)
-    for copy in copies[2:]:
-        copy.wait()
-
-
-def level_two_taps(source_ref, received, cells, shifted, taps):
+
+
+def add_cells(ref, base, axis, upper, value):
+    for part in range(2):
+        add_face(ref.at[part], base, 4, axis, upper, value[:, C1 * part : C1 * part + C1])
+
+
+def level_two_taps(source_ref, cells, shifted, taps):
     for side in range(6):
         for part in range(2):
             tap = shifted.at[side, part]
-            lanes = pl.ds(C1 * part, C1)
-            write_tap(
-                tap, cells.at[part], source_ref, tuple(got.at[:, lanes] for got in received), 4, side
-            )
+            write_tap(tap, cells.at[part], source_ref, 4, side)
             start = C2 * (side + 1) + C1 * part
             taps[:, start : start + C1] = tap[...].astype(BF16)
 
 
+def ready_two(source_ref, coarse, weight, taps, pre, cells, shifted):
+    low_res = coarse[...]
+    split(low_res, cells)
+    taps[:, 0:C2] = low_res
+    level_two_taps(source_ref, cells, shifted, taps)
+    split(jnp.dot(taps[...], weight[...], preferred_element_type=F32), pre)
+
+
 def level_two(
-    source_ref, send_ref, coarse, got_0, got_1, got_2, weight, cotangent,
-    taps, bent, delta, face_0, face_1, face_2,
-    cells, shifted,
+    info_ref, got_0, got_1, got_2, weight, cotangent, pre_near,
+    pre, delta, face_0, face_1, face_2,
+    cells,
 ):
-    low_res = coarse[...]
-    cells[0] = low_res[:, :C1].astype(F32)
-    cells[1] = low_res[:, C1:].astype(F32)
-    taps[:, 0:C2] = low_res
-    level_two_taps(source_ref, (got_0, got_1, got_2), cells, shifted, taps)
-    pre = jnp.dot(taps[...], weight[...], preferred_element_type=F32)
-    gate = sigmoid(pre)
-    bent[...] = pre * gate
-    change = (cotangent[...].astype(F32) * (gate * (1.0 + pre * (1.0 - gate)))).astype(BF16)
+    pre[...] = pre_near[...]
+    for axis, upper, base, rim in far_rims(info_ref, 4, (got_0, got_1, got_2)):
+        rows = pl.ds(pl.multiple_of(C2 * (2 * axis + upper + 1), C2), C2)
+        add = jnp.dot(rim, weight[rows, :], preferred_element_type=F32)
+        add_cells(pre, base, axis, upper, add)
+    value = jnp.concatenate([pre[0], pre[1]], axis=1)
+    gate = sigmoid(value)
+    change = (cotangent[...].astype(F32) * (gate * (1.0 + value * (1.0 - gate)))).astype(BF16)
     delta[...] = change
-    cells[0] = change[:, :C1].astype(F32)
-    cells[1] = change[:, C1:].astype(F32)
-    for axis, out in enumerate((face_0, face_1, face_2)):
-        for part in range(2):
-            out[:, C1 * part : C1 * part + C1] = sent_face(
-                cells.at[part], send_ref, 4, axis
-            ).astype(BF16)
+    send_faces_of(change, info_ref, cells, (face_0, face_1, face_2))
 
 
 def core_index():
     return lax.rem(lax.axis_index("scene"), 2)
 
 
-def two_gradient(taps, delta, coarse, bent, kept, sent, encoded, both):
-    encoded[...] = (coarse[...].astype(F32) + bent[...]).astype(BF16)
+def ready_back(
+    source_ref, info_ref, delta, weight, cotangent, coarse, pre, taps_two, got_0, got_1, got_2,
+    kept, sent, encoded, total,
+    cells, shifted, taps, both,
+):
     change = delta[...]
+    split(change, cells)
+    taps[:, 0:C2] = change
+    level_two_taps(source_ref, cells, shifted, taps)
+    value = cotangent[...].astype(F32)
     for tap in range(7):
-        grad = tn_dot(taps[:, C2 * tap : C2 * tap + C2], change)
+        lane = C2 * OPPOSITE[tap]
+        value = value + nt_dot(taps[:, lane : lane + C2], weight[pl.ds(C2 * tap, C2), :])
+    split(value, total)
+    value = jnp.concatenate([pre[0], pre[1]], axis=1)
+    encoded[...] = (coarse[...].astype(F32) + value * sigmoid(value)).astype(BF16)
+    for tap in range(7):
+        grad = tn_dot(taps_two[:, C2 * tap : C2 * tap + C2], change)
         rows = pl.ds(C2 * tap, C2)
         both[0, rows, :] = grad[:, :C1]
         both[1, rows, :] = grad[:, C1:]
+    for axis, upper, base, rim in far_rims(info_ref, 4, (got_0, got_1, got_2)):
+        rows = pl.ds(pl.multiple_of(C2 * (2 * axis + upper + 1), C2), C2)
+        for part in range(2):
+            here = face_value(cells.at[part], base, 4, axis, upper).astype(BF16)
+            both[part, rows, :] = both[part, rows, :] + tn_dot(rim, here)
     core = core_index()
     kept[...] = both[core]
     sent[...] = both[1 - core].astype(BF16)
 
 
 def backward(
-    source_ref, delta, got_0, got_1, got_2, weight, cotangent, down, patches, slope, taps_one,
-    kept, sent,
-    cells, shifted, taps, patch_grad, spread, delta_one, both,
+    info_ref, got_0, got_1, got_2, rim_0, rim_1, rim_2, weight, down, patches, slope,
+    taps_one, total_near, kept, sent,
+    total, patch_grad, spread, delta_one, both,
 ):
-    change = delta[...]
-    cells[0] = change[:, :C1].astype(F32)
-    cells[1] = change[:, C1:].astype(F32)
-    taps[:, 0:C2] = change
-    level_two_taps(source_ref, (got_0, got_1, got_2), cells, shifted, taps)
-    total = cotangent[...].astype(F32)
-    for tap in range(7):
-        lane = C2 * OPPOSITE[tap]
-        total = total + nt_dot(taps[:, lane : lane + C2], weight[pl.ds(C2 * tap, C2), :])
-    upstream = total.astype(BF16)
+    total[...] = total_near[...]
+    for axis, upper, base, rim in far_rims(info_ref, 4, (got_0, got_1, got_2)):
+        rows = pl.ds(pl.multiple_of(C2 * (2 * axis + 2 - upper), C2), C2)
+        add_cells(total, base, axis, upper, nt_dot(rim, weight[rows, :]))
+    upstream = jnp.concatenate([total[0], total[1]], axis=1).astype(BF16)
     grad_down = tn_dot(patches[...], upstream)
     both[0, pl.ds(ONE_ROWS, DOWN_ROWS), :] = grad_down[:, :C1]
     both[1, pl.ds(ONE_ROWS, DOWN_ROWS), :] = grad_down[:, C1:]
@@ -269,13 +328,22 @@
             right = jnp.where(low, pltpu.roll(first, 4, 1), second)
             halves.append(jnp.stack([left, right], axis=1).reshape(BRICKS * 4, 4, 8, C1))
         spread[pl.ds(r, 1024, stride=2), :] = jnp.stack(halves, axis=1).reshape(1024, C1)
-    delta_one[...] = (spread[...] * slope[...]).astype(BF16)
+    change = (spread[...] * slope[...]).astype(BF16)
+    delta_one[...] = change
+    spread[...] = change.astype(F32)
     grad_one = tn_dot(delta_one[...], taps_one[...])
     for tap in range(7):
         block = grad_one[:, C1 * tap : C1 * tap + C1].T
         for start in range(0, C1, 64):
             row = C1 * tap + start
             both[row // ONE_ROWS, pl.ds(row % ONE_ROWS, 64), :] = block[start : start + 64]
+    for axis, upper, base, rim in far_rims(info_ref, 8, (rim_0, rim_1, rim_2)):
+        add = tn_dot(rim, face_value(spread, base, 8, axis, upper).astype(BF16))
+        for start in range(0, C1, 64):
+            row = C1 * (2 * axis + upper + 1) + start
+            half = lax.div(row, ONE_ROWS)
+            rows = pl.ds(pl.multiple_of(row - half * ONE_ROWS, 64), 64)
+            both[half, rows, :] = both[half, rows, :] + add[start : start + 64]
     core = core_index()
     kept[...] = both[core]
     sent[...] = both[1 - core].astype(BF16)
@@ -335,66 +403,89 @@
     weight_one = conv_one.reshape(7 * C1, C1)
     weight_two = conv_two.reshape(7 * C2, C2)
     dma = pltpu.SemaphoreType.DMA
-    field, sources, *sent = call(
+    field, sources, info, *sent = call(
         feature_faces,
         [(hbm, features.reshape(2048, C1)), (hbm, sides), (hbm, face_source)],
         [(vmem, (2048, C1), BF16), (vmem, (1, BRICKS, 6), jnp.int32)]
+        + [(vmem, (1, C1), jnp.int32)]
         + [(vmem, (64, C1), BF16)] * 3,
-        [pltpu.SMEM((1, 3), jnp.int32), pltpu.VMEM((3, 512, C1), F32), dma((3,))],
-    )
-    received = exchanged(sent)
-    taps_one, slope, patches, coarse, face_0, face_1, face_2, down, weight, upstream = call(
-        level_one,
-        [(smem, sources), (smem, sides), (vmem, field)]
-        + [(vmem, got) for got in received]
-        + [(hbm, weight_one), (hbm, down_weight), (hbm, weight_two)]
-        + [(hbm, cotangent.reshape(256, C2))],
+        [
+            pltpu.SMEM((1, 3), jnp.int32),
+            pltpu.SMEM((1, BRICKS, 6), jnp.int32),
+            pltpu.VMEM((3, 512, C1), F32),
+            dma((4,)),
+        ],
+    )
+    got_field = [(vmem, face) for face in exchanged(sent)]
+    taps_one, pre_one, near_one, down = call(
+        ready_one,
+        [(smem, sources), (vmem, field)]
+        + [(hbm, weight_one), (hbm, down_weight)],
         [
             (vmem, (2048, 7 * C1), BF16),
             (vmem, (2048, C1), F32),
-            (vmem, (256, 8 * C1), BF16),
-            (vmem, (256, C2), BF16),
-        ]
+            (vmem, (7 * C1, C1), BF16),
+            (vmem, (8 * C1, C2), BF16),
+        ],
+        [pltpu.VMEM((2048, C1), F32), pltpu.VMEM((6, 2048, C1), F32), dma((2,))],
+    )
+    slope, patches, coarse, face_0, face_1, face_2, weight, upstream = call(
+        level_one,
+        [(smem, info), (vmem, field)]
+        + got_field
+        + [(vmem, near_one), (vmem, down), (vmem, pre_one)]
+        + [(hbm, weight_two), (hbm, cotangent.reshape(256, C2))],
+        [(vmem, (2048, C1), F32), (vmem, (256, 8 * C1), BF16), (vmem, (256, C2), BF16)]
         + [(vmem, (16, C2), BF16)] * 3
-        + [(vmem, (8 * C1, C2), BF16), (vmem, (7 * C2, C2), BF16), (vmem, (256, C2), BF16)],
+        + [(vmem, (7 * C2, C2), BF16), (vmem, (256, C2), BF16)],
         [
             pltpu.VMEM((2048, C1), F32),
-            pltpu.VMEM((6, 2048, C1), F32),
             pltpu.VMEM((2048, C1), F32),
             pltpu.VMEM((2, 256, C1), F32),
-            pltpu.VMEM((7 * C1, C1), BF16),
-            dma((4,)),
+            dma((2,)),
         ],
     )
-    received = exchanged((face_0, face_1, face_2))
-    taps_two, bent, delta, *sent = call(
+    got_coarse = [(vmem, face) for face in exchanged((face_0, face_1, face_2))]
+    taps_two, pre_two = call(
+        ready_two,
+        [(smem, sources), (vmem, coarse), (vmem, weight)],
+        [(vmem, (256, 7 * C2), BF16), (vmem, (2, 256, C1), F32)],
+        [pltpu.VMEM((2, 256, C1), F32), pltpu.VMEM((6, 2, 256, C1), F32)],
+    )
+    pre_two, delta, *sent = call(
         level_two,
-        [(smem, sources), (smem, sides), (vmem, coarse)]
-        + [(vmem, got) for got in received]
-        + [(vmem, weight), (vmem, upstream)],
-        [(vmem, (256, 7 * C2), BF16), (vmem, (256, C2), F32), (vmem, (256, C2), BF16)]
-        + [(vmem, (16, C2), BF16)] * 3,
-        [pltpu.VMEM((2, 256, C1), F32), pltpu.VMEM((6, 2, 256, C1), F32)],
-    )
-    received = exchanged(sent)
-    kept_two, sent_two, encoded = call(
-        two_gradient,
-        [(vmem, taps_two), (vmem, delta), (vmem, coarse), (vmem, bent)],
-        [(vmem, (TWO_ROWS, C1), F32), (vmem, (TWO_ROWS, C1), BF16), (vmem, (256, C2), BF16)],
-        [pltpu.VMEM((2, TWO_ROWS, C1), F32)],
-    )
-    got_two = swapped(sent_two, "scene", 0)
-    kept, sent = call(
-        backward,
-        [(smem, sources), (vmem, delta)]
-        + [(vmem, got) for got in received]
-        + [(vmem, weight), (vmem, upstream), (vmem, down), (vmem, patches), (vmem, slope)]
-        + [(vmem, taps_one)],
-        [(vmem, (EARLY, C1), F32), (vmem, (EARLY, C1), BF16)],
+        [(smem, info)]
+        + got_coarse
+        + [(vmem, weight), (vmem, upstream), (vmem, pre_two)],
+        [(vmem, (2, 256, C1), F32), (vmem, (256, C2), BF16)] + [(vmem, (16, C2), BF16)] * 3,
+        [pltpu.VMEM((2, 256, C1), F32)],
+    )
+    got = [(vmem, face) for face in exchanged(sent)]
+    kept_two, sent_two, encoded, total = call(
+        ready_back,
+        [(smem, sources), (smem, info), (vmem, delta), (vmem, weight), (vmem, upstream)]
+        + [(vmem, coarse), (vmem, pre_two), (vmem, taps_two)]
+        + got_coarse,
+        [(vmem, (TWO_ROWS, C1), F32), (vmem, (TWO_ROWS, C1), BF16), (vmem, (256, C2), BF16)]
+        + [(vmem, (2, 256, C1), F32)],
         [
             pltpu.VMEM((2, 256, C1), F32),
             pltpu.VMEM((6, 2, 256, C1), F32),
             pltpu.VMEM((256, 7 * C2), BF16),
+            pltpu.VMEM((2, TWO_ROWS, C1), F32),
+        ],
+    )
+    got_two = swapped(sent_two, "scene", 0)
+    kept, sent = call(
+        backward,
+        [(smem, info)]
+        + got
+        + got_field
+        + [(vmem, weight), (vmem, down), (vmem, patches), (vmem, slope), (vmem, taps_one)]
+        + [(vmem, total)],
+        [(vmem, (EARLY, C1), F32), (vmem, (EARLY, C1), BF16)],
+        [
+            pltpu.VMEM((2, 256, C1), F32),
             pltpu.VMEM((256, 8 * C1), F32),
             pltpu.VMEM((2048, C1), F32),
             pltpu.VMEM((2048, C1), BF16),

time: 116 us -> 108 us (0.931)
  local copies, waits for them, and re-layouts: 6.43 us -> 0 us
  Pallas kernels: 13.1 us -> 15.3 us
  waiting for transfers between devices: 7.91 us -> 5.78 us
  starting transfers between devices: 33.5 us -> 31.8 us
    unnamed x14 -> x0, local copies, waits for them, and re-layouts: 6.43 us -> none
    pallas_call x10 -> x12, Pallas kernels: 13.1 us -> 15.3 us  [call(): pl.pallas_call(body, out_shape=[jax.ShapeDtypeStruct(shape, dtype) for _,...]
    ppermute x12, waiting for transfers between devices: 7.91 us -> 5.78 us  [swapped(): return lax.ppermute(value, axis, pairs)]
    ppermute x12, starting transfers between devices: 33.5 us -> 31.8 us  [swapped(): return lax.ppermute(value, axis, pairs)]
  transfers between devices with their start and end apart: 12 -> 12, of which waited for: 5 -> 4; matrix products, arithmetic and copies ran while one was open for 0% -> 0% of each run, Pallas kernels for 4% -> 7%
where the time goes in v4:
time: 108 us; the launch traced here: 107 us
  blocking collectives  53.7 us (50%)
  starting transfers between devices  31.8 us (29%)
  Pallas kernels  15.3 us (14%)
  waiting for transfers between devices  5.78 us (5%)
    ppermute x12, starting transfers between devices, swapped(): return lax.ppermute(value, axis, pairs)  31.8 us
    all_to_all x1, blocking collectives, step(): lax.all_to_all(packed.reshape(PLANE, CHUNK, C1), 'scene', 0, 0, axis_inde...  20.3 us
    all_to_all x1, blocking collectives, step(): parts = lax.all_to_all(copies, 'kd', 0, 0)  17.5 us
    all_to_all x1, blocking collectives, step(): own = lax.all_to_all(copies, 'scene', 0, 0, axis_index_groups=groups)  16 us
    pallas_call x12, Pallas kernels, call(): pl.pallas_call(body, out_shape=[jax.ShapeDtypeStruct(shape, dtype) for _,...  15.3 us
    ppermute x12, waiting for transfers between devices, swapped(): return lax.ppermute(value, axis, pairs)  5.78 us
  transfers between devices with their start and end apart: 12, of which 4 were waited for; matrix products, arithmetic and copies ran while one was open for 0% of the time, Pallas kernels for 7%

profile of v4, /device:TPU:1, one launch (start us, length us, event | category | flops | bytes accessed | tf_op | source)
XLA Modules:
  0.0 107.4 jit_solution(1741417636789205262)
XLA Ops:
  0.6 1.2 %shard_map.102 = (bf16[2048,128]{1,0:T(8,128)(2,1)S(1)}, s32[1,4,6]{2,1,0:T(4,128)S(1)}, s32[1,128]{1,0:T(1,128)S(1)}, bf16[64,128]{1,0:T(8,128)(2,1)S(1)}, bf16...) custom-call(bf16[2048,128]{1,0:T(8,128)(2,1)} %bitcast.15, s32[1,3]{1,0:T(1,128)} %bitcast.19, s32[1,4,6]{2,1,0:T(4,128)} %sources.1), custom_call_target="tpu_custom_call" | custom-call | tf_op jit(solution)/shard_map/pallas_call | solution.py:48
  1.8 2.5 %collective-permute-start = (bf16[64,128]{1,0:T(8,128)(2,1)S(1)}, bf16[64,128]{1,0:T(8,128)(2,1)S(1)}, u32[]{:S(2)}, u32[]{:S(2)}) collective-permute-start(bf16[64,128]{1,0:T(8,128)(2,1)S(1)} %get-tuple-element.44), channel_id=1, source_target_pairs={{0,1},{1,0},{2,3},{3,2},{4,5},{5,4},{6,7},{7,6},{8,9},{9,8},{10,11... | collective-permute-start | bytes 49160 | tf_op jit(solution)/shard_map/ppermute | solution.py:391
  4.4 3.0 %collective-permute-start.1 = (bf16[64,128]{1,0:T(8,128)(2,1)S(1)}, bf16[64,128]{1,0:T(8,128)(2,1)S(1)}, u32[]{:S(2)}, u32[]{:S(2)}) collective-permute-start(bf16[64,128]{1,0:T(8,128)(2,1)S(1)} %get-tuple-element.45), channel_id=1, source_target_pairs={{0,2},{1,3},{2,0},{3,1},{4,6},{5,7},{6,4},{7,5},{8,10},{9,11},{10,... | collective-permute-start | bytes 49160 | tf_op jit(solution)/shard_map/ppermute | solution.py:391
  7.4 4.2 %collective-permute-start.2 = (bf16[64,128]{1,0:T(8,128)(2,1)S(1)}, bf16[64,128]{1,0:T(8,128)(2,1)S(1)}, u32[]{:S(2)}, u32[]{:S(2)}) collective-permute-start(bf16[64,128]{1,0:T(8,128)(2,1)S(1)} %get-tuple-element.46), channel_id=1, source_target_pairs={{0,4},{1,5},{2,6},{3,7},{4,0},{5,1},{6,2},{7,3},{8,12},{9,13},{10,... | collective-permute-start | bytes 49160 | tf_op jit(solution)/shard_map/ppermute | solution.py:391
  11.6 2.6 %shard_map.103 = (bf16[2048,896]{1,0:T(8,128)(2,1)S(1)}, f32[2048,128]{1,0:T(8,128)S(1)}, bf16[896,128]{1,0:T(8,128)(2,1)S(1)}, bf16[1024,256]{1,0:T(8,128)(2,1)S(1)}) custom-call(s32[1,4,6]{2,1,0:T(4,128)S(1)} %get-tuple-element.41.source_ref, bf16[2048,128]{1,0:T(8,128)(2,1)S(1)} %get-tuple-element.43.field_near.field, bf16[896,128]{1,0:T(8,128)(2,1)} %bitcast.17, ...), custom_call_target="tpu_custom_call" | custom-call | tf_op jit(solution)/shard_map/pallas_call | solution.py:48
  14.2 0.0 collective-permute-done.got_0.rim_0
  14.2 0.0 collective-permute-done.1.got_1.rim_1
  14.2 0.0 collective-permute-done.2.got_2.rim_2
  14.2 1.9 %shard_map.104 = (f32[2048,128]{1,0:T(8,128)S(1)}, bf16[256,1024]{1,0:T(8,128)(2,1)S(1)}, bf16[256,256]{1,0:T(8,128)(2,1)S(1)}, bf16[16,256]{1,0:T(8,128)(2,1)S(...) custom-call(s32[1,128]{1,0:T(1,128)S(1)} %get-tuple-element.42.info_, ...), custom_call_target="tpu_custom_call" | custom-call | tf_op jit(solution)/shard_map/pallas_call | solution.py:48
  16.2 0.8 collective-permute-start.3
  17.0 1.2 %collective-permute-start.4 = (bf16[16,256]{1,0:T(8,128)(2,1)S(1)}, bf16[16,256]{1,0:T(8,128)(2,1)S(1)}, u32[]{:S(2)}, u32[]{:S(2)}) collective-permute-start(bf16[16,256]{1,0:T(8,128)(2,1)S(1)} %get-tuple-element.51), channel_id=1, source_target_pairs={{0,2},{1,3},{2,0},{3,1},{4,6},{5,7},{6,4},{7,5},{8,10},{9,11},{10,... | collective-permute-start | bytes 24584 | tf_op jit(solution)/shard_map/ppermute | solution.py:391
  18.1 3.8 %collective-permute-start.5 = (bf16[16,256]{1,0:T(8,128)(2,1)S(1)}, bf16[16,256]{1,0:T(8,128)(2,1)S(1)}, u32[]{:S(2)}, u32[]{:S(2)}) collective-permute-start(bf16[16,256]{1,0:T(8,128)(2,1)S(1)} %get-tuple-element.52), channel_id=1, source_target_pairs={{0,4},{1,5},{2,6},{3,7},{4,0},{5,1},{6,2},{7,3},{8,12},{9,13},{10,... | collective-permute-start | bytes 24584 | tf_op jit(solution)/shard_map/ppermute | solution.py:391
  21.9 1.1 %shard_map.105 = (bf16[256,1792]{1,0:T(8,128)(2,1)S(1)}, f32[2,256,128]{2,1,0:T(8,128)S(1)}) custom-call(s32[1,4,6]{2,1,0:T(4,128)S(1)} %get-tuple-element.41.source_ref, bf16[256,256]{1,0:T(8,128)(2,1)S(1)} %get-tuple-element.55.coarse, bf16[1792,256]{1,0:T(8,128)(2,1)S(1)} %get-tuple-element.53.weight), custom_call_target="tpu_custom_call" | custom-call | tf_op jit(solution)/shard_map/pallas_call | solution.py:48
  23.0 0.0 collective-permute-done.3.got_0
  23.1 0.0 collective-permute-done.4.got_1
  23.1 1.5 %collective-permute-done.5.got_2 = bf16[16,256]{1,0:T(8,128)(2,1)S(1)} collective-permute-done((bf16[16,256]{1,0:T(8,128)(2,1)S(1)}, bf16[16,256]{1,0:T(8,128)(2,1)S(1)}, u32[]{:S(2)}, u32[]{:S(2)}) %collective-permute-start.5) | collective-permute-done | bytes 8224 | tf_op jit(solution)/shard_map/ppermute | solution.py:391
  24.6 0.9 shard_map.106
  25.5 2.4 %shard_map.107 = (f32[1792,128]{1,0:T(8,128)S(1)}, bf16[1792,128]{1,0:T(8,128)(2,1)S(1)}, bf16[256,256]{1,0:T(8,128)(2,1)}, f32[2,256,128]{2,1,0:T(8,128)S(1)}) custom-call(s32[1,4,6]{2,1,0:T(4,128)S(1)} %get-tuple-element.41.source_ref, s32[1,128]{1,0:T(1,128)S(1)} %get-tuple-element.42.info_ref, bf16[256,256]{1,0:T(8,128)(2,1)S(1)} %get-tuple-element.57.delta, ...), custom_call_target="tpu_custom_call" | custom-call | tf_op jit(solution)/shard_map/pallas_call | solution.py:48
  27.9 3.2 %collective-permute-start.10 = (bf16[1792,128]{1,0:T(8,128)(2,1)S(1)}, bf16[1792,128]{1,0:T(8,128)(2,1)S(1)}, u32[]{:S(2)}, u32[]{:S(2)}) collective-permute-start(bf16[1792,128]{1,0:T(8,128)(2,1)S(1)} %get-tuple-element.71), channel_id=1, source_target_pairs={{0,8},{8,0},{16,24},{24,16},{32,40},{40,32},{48,56},{56,48},{64,72... | collective-permute-start | bytes 1376264 | tf_op jit(solution)/shard_map/ppermute | solution.py:391
  31.1 0.7 collective-permute-start.6
  31.8 1.7 %collective-permute-start.7 = (bf16[16,256]{1,0:T(8,128)(2,1)S(1)}, bf16[16,256]{1,0:T(8,128)(2,1)S(1)}, u32[]{:S(2)}, u32[]{:S(2)}) collective-permute-start(bf16[16,256]{1,0:T(8,128)(2,1)S(1)} %get-tuple-element.62), channel_id=1, source_target_pairs={{0,2},{1,3},{2,0},{3,1},{4,6},{5,7},{6,4},{7,5},{8,10},{9,11},{10,... | collective-permute-start | bytes 24584 | tf_op jit(solution)/shard_map/ppermute | solution.py:391
  33.5 4.2 %collective-permute-start.8 = (bf16[16,256]{1,0:T(8,128)(2,1)S(1)}, bf16[16,256]{1,0:T(8,128)(2,1)S(1)}, u32[]{:S(2)}, u32[]{:S(2)}) collective-permute-start(bf16[16,256]{1,0:T(8,128)(2,1)S(1)} %get-tuple-element.63), channel_id=1, source_target_pairs={{0,4},{1,5},{2,6},{3,7},{4,0},{5,1},{6,2},{7,3},{8,12},{9,13},{10,... | collective-permute-start | bytes 24584 | tf_op jit(solution)/shard_map/ppermute | solution.py:391
  37.7 0.0 collective-permute-done.6.got_0
  37.7 0.0 collective-permute-done.7.got_1
  37.7 2.2 %collective-permute-done.8.got_2 = bf16[16,256]{1,0:T(8,128)(2,1)S(1)} collective-permute-done((bf16[16,256]{1,0:T(8,128)(2,1)S(1)}, bf16[16,256]{1,0:T(8,128)(2,1)S(1)}, u32[]{:S(2)}, u32[]{:S(2)}) %collective-permute-start.8) | collective-permute-done | bytes 8224 | tf_op jit(solution)/shard_map/ppermute | solution.py:391
  39.9 2.3 %shard_map.108 = (f32[1472,128]{1,0:T(8,128)S(1)}, bf16[1472,128]{1,0:T(8,128)(2,1)S(1)}) custom-call(s32[1,128]{1,0:T(1,128)S(1)} %get-tuple-element.42.info_ref, bf16[16,256]{1,0:T(8,128)(2,1)S(1)} %collective-permute-done.6.got_0, bf16[16,256]{1,0:T(8,128)(2,1)S(1)} %collective-permute-done.7.got_1, bf16[16,256]{1,0:T(8,128)(2,1)S(1)} %collective-permute-done.8.got_2, ...), custom_call_target="tpu_custom_call" | custom-call | tf_op jit(solution)/shard_map/pallas_call | solution.py:48
  42.2 1.8 %collective-permute-start.9 = (bf16[1472,128]{1,0:T(8,128)(2,1)S(1)}, bf16[1472,128]{1,0:T(8,128)(2,1)S(1)}, u32[]{:S(2)}, u32[]{:S(2)}) collective-permute-start(bf16[1472,128]{1,0:T(8,128)(2,1)S(1)} %get-tuple-element.69), channel_id=1, source_target_pairs={{0,8},{8,0},{16,24},{24,16},{32,40},{40,32},{48,56},{56,48},{64,72... | collective-permute-start | bytes 1130504 | tf_op jit(solution)/shard_map/ppermute | solution.py:391
  44.0 1.3 %collective-permute-done.9.got_a = bf16[1472,128]{1,0:T(8,128)(2,1)S(1)} collective-permute-done((bf16[1472,128]{1,0:T(8,128)(2,1)S(1)}, bf16[1472,128]{1,0:T(8,128)(2,1)S(1)}, u32[]{:S(2)}, u32[]{:S(2)}) %collective-permute-start.9) | collective-permute-done | bytes 376864 | tf_op jit(solution)/shard_map/ppermute | solution.py:391
  45.3 0.0 collective-permute-done.10.got_b
  45.4 0.2 shard_map.109
  45.5 20.3 %all_to_all.15.parts = bf16[16,208,128]{2,1,0:T(8,128)(2,1)S(1)} all-to-all(bf16[16,208,128]{2,1,0:T(8,128)(2,1)S(1)} %bitcast.12), channel_id=1, replica_groups={{0,16,32,48,64,80,96,112,128,144,160,176,192,208,224,240},{8,24,40,56,7..., dimensions={0} | all-to-all | bytes 1703936 | tf_op jit(solution)/shard_map/all_to_all | solution.py:502
  65.8 0.1 shard_map.110
  65.9 17.5 %all_to_all.16.parts = bf16[8,208,128]{2,1,0:T(8,128)(2,1)S(1)} all-to-all(bf16[8,208,128]{2,1,0:T(8,128)(2,1)S(1)} %shard_map.110), channel_id=1, replica_groups=mesh['scene'=32,'kd'=8] {'kd'}, dimensions={0} | all-to-all | bytes 851968 | tf_op jit(solution)/shard_map/all_to_all | solution.py:506
  83.4 0.1 shard_map.111
  83.4 16.0 %all_to_all.17 = bf16[16,208,128]{2,1,0:T(8,128)(2,1)S(1)} all-to-all(bf16[16,208,128]{2,1,0:T(8,128)(2,1)S(1)} %shard_map.111), channel_id=1, replica_groups={{0,16,32,48,64,80,96,112,128,144,160,176,192,208,224,240},{8,24,40,56,7..., dimensions={0} | all-to-all | bytes 1703936 | tf_op jit(solution)/shard_map/all_to_all | solution.py:508
  99.5 4.7 %collective-permute-start.11 = (bf16[3328,128]{1,0:T(8,128)(2,1)S(1)}, bf16[3328,128]{1,0:T(8,128)(2,1)S(1)}, u32[]{:S(2)}, u32[]{:S(2)}) collective-permute-start(bf16[3328,128]{1,0:T(8,128)(2,1)S(1)} %bitcast.10), channel_id=1, source_target_pairs={{0,8},{8,0},{16,24},{24,16},{32,40},{40,32},{48,56},{56,48},{64,72... | collective-permute-start | bytes 2555912 | tf_op jit(solution)/shard_map/ppermute | solution.py:391
  104.2 1.2 %shard_map.112 = (f32[896,128]{1,0:T(8,128)}, f32[1024,256]{1,0:T(8,128)}, f32[1792,256]{1,0:T(8,128)}) custom-call(bf16[3328,128]{1,0:T(8,128)(2,1)S(1)} %bitcast.11), custom_call_target="tpu_custom_call" | custom-call | tf_op jit(solution)/shard_map/pallas_call | solution.py:48
  105.4 0.8 collective-permute-done.11.source
  106.2 1.2 %shard_map.113 = (f32[896,128]{1,0:T(8,128)}, f32[1024,256]{1,0:T(8,128)}, f32[1792,256]{1,0:T(8,128)}) custom-call(bf16[3328,128]{1,0:T(8,128)(2,1)S(1)} %collective-permute-done.11.source, f32[896,128]{1,0:T(8,128)} %get-tuple-element.72.refs_0_, ...), custom_call_target="tpu_custom_call", output_to_operand_aliasing={{0}: (1, {}), {1}: (2, {}), {2}: (3, {})} | custom-call | tf_op jit(solution)/shard_map/pallas_call | solution.py:48
Async XLA Ops:
  1.8 12.4 %collective-permute-start = (bf16[64,128]{1,0:T(8,128)(2,1)S(1)}, bf16[64,128]{1,0:T(8,128)(2,1)S(1)}, u32[]{:S(2)}, u32[]{:S(2)}) collective-permute-start(bf16[64,128]{1,0:T(8,128)(2,1)S(1)} %get-tuple-element.44), channel_id=1, source_target_pairs={{0,1},{1,0},{2,3},{3,2},{4,5},{5,4},{6,7},{7,6},{8,9},{9,8},{10,11... | collective-permute-start | bytes 49160 | tf_op jit(solution)/shard_map/ppermute | solution.py:391
  4.4 9.9 %collective-permute-start.1 = (bf16[64,128]{1,0:T(8,128)(2,1)S(1)}, bf16[64,128]{1,0:T(8,128)(2,1)S(1)}, u32[]{:S(2)}, u32[]{:S(2)}) collective-permute-start(bf16[64,128]{1,0:T(8,128)(2,1)S(1)} %get-tuple-element.45), channel_id=1, source_target_pairs={{0,2},{1,3},{2,0},{3,1},{4,6},{5,7},{6,4},{7,5},{8,10},{9,11},{10,... | collective-permute-start | bytes 49160 | tf_op jit(solution)/shard_map/ppermute | solution.py:391
  7.4 6.9 %collective-permute-start.2 = (bf16[64,128]{1,0:T(8,128)(2,1)S(1)}, bf16[64,128]{1,0:T(8,128)(2,1)S(1)}, u32[]{:S(2)}, u32[]{:S(2)}) collective-permute-start(bf16[64,128]{1,0:T(8,128)(2,1)S(1)} %get-tuple-element.46), channel_id=1, source_target_pairs={{0,4},{1,5},{2,6},{3,7},{4,0},{5,1},{6,2},{7,3},{8,12},{9,13},{10,... | collective-permute-start | bytes 49160 | tf_op jit(solution)/shard_map/ppermute | solution.py:391
  16.2 6.9 %collective-permute-start.3 = (bf16[16,256]{1,0:T(8,128)(2,1)S(1)}, bf16[16,256]{1,0:T(8,128)(2,1)S(1)}, u32[]{:S(2)}, u32[]{:S(2)}) collective-permute-start(bf16[16,256]{1,0:T(8,128)(2,1)S(1)} %get-tuple-element.50), channel_id=1, source_target_pairs={{0,1},{1,0},{2,3},{3,2},{4,5},{5,4},{6,7},{7,6},{8,9},{9,8},{10,11... | collective-permute-start | bytes 24584 | tf_op jit(solution)/shard_map/ppermute | solution.py:391
  17.0 6.1 %collective-permute-start.4 = (bf16[16,256]{1,0:T(8,128)(2,1)S(1)}, bf16[16,256]{1,0:T(8,128)(2,1)S(1)}, u32[]{:S(2)}, u32[]{:S(2)}) collective-permute-start(bf16[16,256]{1,0:T(8,128)(2,1)S(1)} %get-tuple-element.51), channel_id=1, source_target_pairs={{0,2},{1,3},{2,0},{3,1},{4,6},{5,7},{6,4},{7,5},{8,10},{9,11},{10,... | collective-permute-start | bytes 24584 | tf_op jit(solution)/shard_map/ppermute | solution.py:391
  18.1 6.4 %collective-permute-start.5 = (bf16[16,256]{1,0:T(8,128)(2,1)S(1)}, bf16[16,256]{1,0:T(8,128)(2,1)S(1)}, u32[]{:S(2)}, u32[]{:S(2)}) collective-permute-start(bf16[16,256]{1,0:T(8,128)(2,1)S(1)} %get-tuple-element.52), channel_id=1, source_target_pairs={{0,4},{1,5},{2,6},{3,7},{4,0},{5,1},{6,2},{7,3},{8,12},{9,13},{10,... | collective-permute-start | bytes 24584 | tf_op jit(solution)/shard_map/ppermute | solution.py:391
  27.9 17.5 %collective-permute-start.10 = (bf16[1792,128]{1,0:T(8,128)(2,1)S(1)}, bf16[1792,128]{1,0:T(8,128)(2,1)S(1)}, u32[]{:S(2)}, u32[]{:S(2)}) collective-permute-start(bf16[1792,128]{1,0:T(8,128)(2,1)S(1)} %get-tuple-element.71), channel_id=1, source_target_pairs={{0,8},{8,0},{16,24},{24,16},{32,40},{40,32},{48,56},{56,48},{64,72... | collective-permute-start | bytes 1376264 | tf_op jit(solution)/shard_map/ppermute | solution.py:391
  31.1 6.6 %collective-permute-start.6 = (bf16[16,256]{1,0:T(8,128)(2,1)S(1)}, bf16[16,256]{1,0:T(8,128)(2,1)S(1)}, u32[]{:S(2)}, u32[]{:S(2)}) collective-permute-start(bf16[16,256]{1,0:T(8,128)(2,1)S(1)} %get-tuple-element.61), channel_id=1, source_target_pairs={{0,1},{1,0},{2,3},{3,2},{4,5},{5,4},{6,7},{7,6},{8,9},{9,8},{10,11... | collective-permute-start | bytes 24584 | tf_op jit(solution)/shard_map/ppermute | solution.py:391
  31.8 5.9 %collective-permute-start.7 = (bf16[16,256]{1,0:T(8,128)(2,1)S(1)}, bf16[16,256]{1,0:T(8,128)(2,1)S(1)}, u32[]{:S(2)}, u32[]{:S(2)}) collective-permute-start(bf16[16,256]{1,0:T(8,128)(2,1)S(1)} %get-tuple-element.62), channel_id=1, source_target_pairs={{0,2},{1,3},{2,0},{3,1},{4,6},{5,7},{6,4},{7,5},{8,10},{9,11},{10,... | collective-permute-start | bytes 24584 | tf_op jit(solution)/shard_map/ppermute | solution.py:391
  33.5 6.4 %collective-permute-start.8 = (bf16[16,256]{1,0:T(8,128)(2,1)S(1)}, bf16[16,256]{1,0:T(8,128)(2,1)S(1)}, u32[]{:S(2)}, u32[]{:S(2)}) collective-permute-start(bf16[16,256]{1,0:T(8,128)(2,1)S(1)} %get-tuple-element.63), channel_id=1, source_target_pairs={{0,4},{1,5},{2,6},{3,7},{4,0},{5,1},{6,2},{7,3},{8,12},{9,13},{10,... | collective-permute-start | bytes 24584 | tf_op jit(solution)/shard_map/ppermute | solution.py:391
  42.2 3.1 %collective-permute-start.9 = (bf16[1472,128]{1,0:T(8,128)(2,1)S(1)}, bf16[1472,128]{1,0:T(8,128)(2,1)S(1)}, u32[]{:S(2)}, u32[]{:S(2)}) collective-permute-start(bf16[1472,128]{1,0:T(8,128)(2,1)S(1)} %get-tuple-element.69), channel_id=1, source_target_pairs={{0,8},{8,0},{16,24},{24,16},{32,40},{40,32},{48,56},{56,48},{64,72... | collective-permute-start | bytes 1130504 | tf_op jit(solution)/shard_map/ppermute | solution.py:391
  99.5 6.7 %collective-permute-start.11 = (bf16[3328,128]{1,0:T(8,128)(2,1)S(1)}, bf16[3328,128]{1,0:T(8,128)(2,1)S(1)}, u32[]{:S(2)}, u32[]{:S(2)}) collective-permute-start(bf16[3328,128]{1,0:T(8,128)(2,1)S(1)} %bitcast.10), channel_id=1, source_target_pairs={{0,8},{8,0},{16,24},{24,16},{32,40},{40,32},{48,56},{56,48},{64,72... | collective-permute-start | bytes 2555912 | tf_op jit(solution)/shard_map/ppermute | solution.py:391

commit v5 on v4

--- a/solution.py
+++ b/solution.py
@@ -15,6 +15,7 @@
 LOCAL = 6 * BRICKS
 PLANE = 16
 DEPTH = 8
+STEPS = (3, 2, 1)
 CHUNK = 208
 ONE_ROWS = 448
 DOWN_ROWS = 1024
@@ -105,6 +106,15 @@
     return face_value(ref, pl.multiple_of(brick * edge**3, edge**3), edge, axis, upper)
 
 
+def local_rim(field, source_ref, edge, side, brick):
+    volume = edge**3
+    source = source_ref[0, brick, side]
+    near = lax.div(jnp.minimum(source, LOCAL - 1), 6)
+    base = pl.multiple_of(near * volume, volume)
+    slab = face_value(field, base, edge, side // 2, 1 - side % 2)
+    return jnp.where(source < LOCAL, slab, jnp.zeros_like(slab))
+
+
 def write_tap(out, field, source_ref, edge, side):
     volume = edge**3
     total = BRICKS * volume
@@ -115,10 +125,7 @@
     else:
         out[pl.ds(step, total - step), :] = field[pl.ds(0, total - step), :]
     for brick in range(BRICKS):
-        source = source_ref[0, brick, side]
-        near = lax.div(jnp.minimum(source, LOCAL - 1), 6)
-        slab = face_value(field, pl.multiple_of(near * volume, volume), edge, axis, 1 - upper)
-        rim = jnp.where(source < LOCAL, slab, jnp.zeros_like(slab))
+        rim = local_rim(field, source_ref, edge, side, brick)
         write_face(out, brick * volume, edge, axis, upper, rim)
 
 
@@ -137,7 +144,7 @@
 
 
 def sigmoid(value):
-    return 1.0 / (1.0 + jnp.exp(-value))
+    return 0.5 * jnp.tanh(0.5 * value) + 0.5
 
 
 def feature_faces(
@@ -169,9 +176,25 @@
     field[...] = field_near[...].astype(F32)
     taps[:, 0:C1] = field_near[...]
     for side in range(6):
-        tap = shifted.at[side]
-        write_tap(tap, field, source_ref, 8, side)
-        taps[:, C1 * (side + 1) : C1 * (side + 2)] = tap[...].astype(BF16)
+        lanes = slice(C1 * (side + 1), C1 * (side + 2))
+        upper = side % 2
+        if side < 2:
+            to, start = (0, 64) if upper else (64, 0)
+            taps[pl.ds(to, 1984), lanes] = field_near[pl.ds(start, 1984), :]
+            for brick in range(BRICKS):
+                rim = local_rim(field_near, source_ref, 8, side, brick)
+                taps[pl.ds(512 * brick + 448 * upper, 64), lanes] = rim
+        elif side < 4:
+            for brick in range(BRICKS):
+                here = field[pl.ds(512 * brick, 512), :].reshape(8, 64, C1)
+                rim = local_rim(field, source_ref, 8, side, brick).reshape(8, 8, C1)
+                pair = (here[:, 8:], rim) if upper else (rim, here[:, :56])
+                tap = jnp.concatenate(pair, axis=1).reshape(512, C1)
+                taps[pl.ds(512 * brick, 512), lanes] = tap.astype(BF16)
+        else:
+            tap = shifted.at[upper]
+            write_tap(tap, field, source_ref, 8, side)
+            taps[:, lanes] = tap[...].astype(BF16)
     copies[0].wait()
     for brick in range(BRICKS):
         rows = pl.ds(512 * brick, 512)
@@ -181,8 +204,8 @@
 
 def level_one(
     info_ref, field, got_0, got_1, got_2, weight, down, pre_near, conv_next, cot_far,
-    slope, patches, coarse, face_0, face_1, face_2, weight_next, cotangent,
-    pre, hidden, cells, sem,
+    pre, patches, coarse, face_0, face_1, face_2, weight_next, cotangent,
+    hidden, cells, sem,
 ):
     copies = begin(sem, (conv_next, weight_next), (cot_far, cotangent))
     pre[...] = pre_near[...]
@@ -193,9 +216,7 @@
     for brick in range(BRICKS):
         rows = pl.ds(512 * brick, 512)
         value = pre[rows, :]
-        gate = sigmoid(value)
-        slope[rows, :] = gate * (1.0 + value * (1.0 - gate))
-        hidden[rows, :] = field[rows, :].astype(F32) + value * gate
+        hidden[rows, :] = field[rows, :].astype(F32) + value * sigmoid(value)
     low = lax.broadcasted_iota(jnp.int32, (1, 8, C1), 1) < 4
     for r in range(2):
         rows = hidden[pl.ds(r, 1024, stride=2), :].reshape(BRICKS * 4, 2, 2, 2, 8, C1)
@@ -242,12 +263,17 @@
             taps[:, start : start + C1] = tap[...].astype(BF16)
 
 
-def ready_two(source_ref, coarse, weight, taps, pre, cells, shifted):
+def ready_two(source_ref, coarse, weight, pre_one, taps, pre, slope, cells, shifted):
     low_res = coarse[...]
     split(low_res, cells)
     taps[:, 0:C2] = low_res
     level_two_taps(source_ref, cells, shifted, taps)
     split(jnp.dot(taps[...], weight[...], preferred_element_type=F32), pre)
+    for brick in range(BRICKS):
+        rows = pl.ds(512 * brick, 512)
+        value = pre_one[rows, :]
+        gate = sigmoid(value)
+        slope[rows, :] = gate * (1.0 + value * (1.0 - gate))
 
 
 def level_two(
@@ -274,7 +300,7 @@
 def ready_back(
     source_ref, info_ref, delta, weight, cotangent, coarse, pre, taps_two, got_0, got_1, got_2,
     kept, sent, encoded, total,
-    cells, shifted, taps, both,
+    cells, shifted, taps,
 ):
     change = delta[...]
     split(change, cells)
@@ -287,24 +313,29 @@
     split(value, total)
     value = jnp.concatenate([pre[0], pre[1]], axis=1)
     encoded[...] = (coarse[...].astype(F32) + value * sigmoid(value)).astype(BF16)
+    far = {}
+    for axis, upper, base, rim in far_rims(info_ref, 4, (got_0, got_1, got_2)):
+        here = [face_value(cells.at[part], base, 4, axis, upper) for part in range(2)]
+        add = tn_dot(rim, jnp.concatenate(here, axis=1).astype(BF16))
+        for side in range(2):
+            far[2 * axis + side + 1] = jnp.where(upper == side, add, jnp.zeros_like(add))
+    first = core_index() == 0
     for tap in range(7):
         grad = tn_dot(taps_two[:, C2 * tap : C2 * tap + C2], change)
-        rows = pl.ds(C2 * tap, C2)
-        both[0, rows, :] = grad[:, :C1]
-        both[1, rows, :] = grad[:, C1:]
-    for axis, upper, base, rim in far_rims(info_ref, 4, (got_0, got_1, got_2)):
-        rows = pl.ds(pl.multiple_of(C2 * (2 * axis + upper + 1), C2), C2)
-        for part in range(2):
-            here = face_value(cells.at[part], base, 4, axis, upper).astype(BF16)
-            both[part, rows, :] = both[part, rows, :] + tn_dot(rim, here)
-    core = core_index()
-    kept[...] = both[core]
-    sent[...] = both[1 - core].astype(BF16)
+        if tap:
+            grad = grad + far[tap]
+        keep_half(first, grad, kept, sent, pl.ds(C2 * tap, C2))
+
+
+def keep_half(first, grad, kept, sent, rows):
+    low, high = grad[:, :C1], grad[:, C1:]
+    kept[rows, :] = jnp.where(first, low, high)
+    sent[rows, :] = jnp.where(first, high, low).astype(BF16)
 
 
 def backward(
     info_ref, got_0, got_1, got_2, rim_0, rim_1, rim_2, weight, down, patches, slope,
-    taps_one, total_near, kept, sent,
+    taps_one, total_near, sent_two, kept, sent,
     total, patch_grad, spread, delta_one, both,
 ):
     total[...] = total_near[...]
@@ -312,9 +343,11 @@
         rows = pl.ds(pl.multiple_of(C2 * (2 * axis + 2 - upper), C2), C2)
         add_cells(total, base, axis, upper, nt_dot(rim, weight[rows, :]))
     upstream = jnp.concatenate([total[0], total[1]], axis=1).astype(BF16)
-    grad_down = tn_dot(patches[...], upstream)
-    both[0, pl.ds(ONE_ROWS, DOWN_ROWS), :] = grad_down[:, :C1]
-    both[1, pl.ds(ONE_ROWS, DOWN_ROWS), :] = grad_down[:, C1:]
+    core = core_index()
+    for start in range(0, DOWN_ROWS, C2):
+        grad = tn_dot(patches[:, start : start + C2], upstream)
+        keep_half(core == 0, grad, kept, sent, pl.ds(ONE_ROWS + start, C2))
+    sent[pl.ds(EARLY, TWO_ROWS), :] = sent_two[...]
     patch_grad[...] = nt_dot(upstream, down[...])
     low = lax.broadcasted_iota(jnp.int32, (1, 8, C1), 1) < 4
     for r in range(2):
@@ -344,14 +377,14 @@
             half = lax.div(row, ONE_ROWS)
             rows = pl.ds(pl.multiple_of(row - half * ONE_ROWS, 64), 64)
             both[half, rows, :] = both[half, rows, :] + add[start : start + 64]
-    core = core_index()
-    kept[...] = both[core]
-    sent[...] = both[1 - core].astype(BF16)
-
-
-def pair_sum(kept_a, got_a, kept_b, got_b, out):
-    out[pl.ds(0, EARLY), :] = (kept_a[...] + got_a[...].astype(F32)).astype(BF16)
-    out[pl.ds(EARLY, TWO_ROWS), :] = (kept_b[...] + got_b[...].astype(F32)).astype(BF16)
+    kept[pl.ds(0, ONE_ROWS), :] = both[core]
+    sent[pl.ds(0, ONE_ROWS), :] = both[1 - core].astype(BF16)
+
+
+def pair_sum(kept_a, kept_b, got, out):
+    early, late = pl.ds(0, EARLY), pl.ds(EARLY, TWO_ROWS)
+    out[early, :] = (kept_a[...] + got[early, :].astype(F32)).astype(BF16)
+    out[late, :] = (kept_b[...] + got[late, :].astype(F32)).astype(BF16)
     out[pl.ds(HALF, PLANE * CHUNK - HALF), :] = jnp.zeros((PLANE * CHUNK - HALF, C1), BF16)
 
 
@@ -364,17 +397,34 @@
         out[index] = total
 
 
+def depth_pair(own, got, out):
+    out[...] = (own[...].astype(F32) + got[...].astype(F32)).astype(BF16)
+
+
+def depth_sum(own, got_3, got_2, got_1, out, parts):
+    here = lax.axis_index("kd")
+    pair, odd = lax.div(here, 2), lax.rem(here, 2)
+    parts[pair] = own[0]
+    parts[lax.rem(pair + 2, 4)] = got_3[0]
+    parts[lax.rem(pair + 1 + 2 * odd, 4)] = got_2[0]
+    parts[lax.rem(pair + 3 - 2 * odd, 4)] = got_1[0]
+    group_sum(parts, out)
+
+
 def unpack(turned, source, *refs):
     one, down, two, stage, sem = refs[-5:]
     half = core_index()
     if turned:
         half = 1 - half
     lanes = pl.ds(pl.multiple_of(half * C1, C1), C1)
-    targets = (
-        (EARLY, TWO_ROWS, two.at[:, lanes]),
-        (ONE_ROWS, DOWN_ROWS, down.at[:, lanes]),
-        (0, ONE_ROWS, one.at[pl.ds(pl.multiple_of(half * ONE_ROWS, ONE_ROWS), ONE_ROWS), :]),
-    )
+    place = pl.multiple_of(half * ONE_ROWS, ONE_ROWS)
+    targets = [
+        (EARLY + row, 448, two.at[pl.ds(row, 448), lanes]) for row in range(0, TWO_ROWS, 448)
+    ]
+    targets += [
+        (ONE_ROWS + row, 512, down.at[pl.ds(row, 512), lanes]) for row in range(0, DOWN_ROWS, 512)
+    ]
+    targets.append((0, ONE_ROWS, one.at[pl.ds(place, ONE_ROWS), :]))
     copies = []
     for index, (start, size, target) in enumerate(targets):
         rows = pl.ds(start, size)
@@ -427,9 +477,9 @@
             (vmem, (7 * C1, C1), BF16),
             (vmem, (8 * C1, C2), BF16),
         ],
-        [pltpu.VMEM((2048, C1), F32), pltpu.VMEM((6, 2048, C1), F32), dma((2,))],
-    )
-    slope, patches, coarse, face_0, face_1, face_2, weight, upstream = call(
+        [pltpu.VMEM((2048, C1), F32), pltpu.VMEM((2, 2048, C1), F32), dma((2,))],
+    )
+    pre_one, patches, coarse, face_0, face_1, face_2, weight, upstream = call(
         level_one,
         [(smem, info), (vmem, field)]
         + got_field
@@ -438,18 +488,13 @@
         [(vmem, (2048, C1), F32), (vmem, (256, 8 * C1), BF16), (vmem, (256, C2), BF16)]
         + [(vmem, (16, C2), BF16)] * 3
         + [(vmem, (7 * C2, C2), BF16), (vmem, (256, C2), BF16)],
-        [
-            pltpu.VMEM((2048, C1), F32),
-            pltpu.VMEM((2048, C1), F32),
-            pltpu.VMEM((2, 256, C1), F32),
-            dma((2,)),
-        ],
+        [pltpu.VMEM((2048, C1), F32), pltpu.VMEM((2, 256, C1), F32), dma((2,))],
     )
     got_coarse = [(vmem, face) for face in exchanged((face_0, face_1, face_2))]
-    taps_two, pre_two = call(
+    taps_two, pre_two, slope = call(
         ready_two,
-        [(smem, sources), (vmem, coarse), (vmem, weight)],
-        [(vmem, (256, 7 * C2), BF16), (vmem, (2, 256, C1), F32)],
+        [(smem, sources), (vmem, coarse), (vmem, weight), (vmem, pre_one)],
+        [(vmem, (256, 7 * C2), BF16), (vmem, (2, 256, C1), F32), (vmem, (2048, C1), F32)],
         [pltpu.VMEM((2, 256, C1), F32), pltpu.VMEM((6, 2, 256, C1), F32)],
     )
     pre_two, delta, *sent = call(
@@ -472,44 +517,54 @@
             pltpu.VMEM((2, 256, C1), F32),
             pltpu.VMEM((6, 2, 256, C1), F32),
             pltpu.VMEM((256, 7 * C2), BF16),
-            pltpu.VMEM((2, TWO_ROWS, C1), F32),
         ],
     )
-    got_two = swapped(sent_two, "scene", 0)
     kept, sent = call(
         backward,
         [(smem, info)]
         + got
         + got_field
         + [(vmem, weight), (vmem, down), (vmem, patches), (vmem, slope), (vmem, taps_one)]
-        + [(vmem, total)],
-        [(vmem, (EARLY, C1), F32), (vmem, (EARLY, C1), BF16)],
+        + [(vmem, total), (vmem, sent_two)],
+        [(vmem, (EARLY, C1), F32), (vmem, (HALF, C1), BF16)],
         [
             pltpu.VMEM((2, 256, C1), F32),
             pltpu.VMEM((256, 8 * C1), F32),
             pltpu.VMEM((2048, C1), F32),
             pltpu.VMEM((2048, C1), BF16),
-            pltpu.VMEM((2, EARLY, C1), F32),
+            pltpu.VMEM((2, ONE_ROWS, C1), F32),
         ],
     )
     got = swapped(sent, "scene", 0)
     groups = [[2 * chip + core for chip in range(PLANE)] for core in range(2)]
     (packed,) = call(
-        pair_sum,
-        [(vmem, kept), (vmem, got), (vmem, kept_two), (vmem, got_two)],
-        [(vmem, (PLANE * CHUNK, C1), BF16)],
+        pair_sum, [(vmem, kept), (vmem, kept_two), (vmem, got)], [(vmem, (PLANE * CHUNK, C1), BF16)]
     )
     parts = lax.all_to_all(
         packed.reshape(PLANE, CHUNK, C1), "scene", 0, 0, axis_index_groups=groups
     )
-    (copies,) = call(group_sum, [(vmem, parts)], [(vmem, (DEPTH, CHUNK, C1), BF16)])
-    parts = lax.all_to_all(copies, "kd", 0, 0)
-    (copies,) = call(group_sum, [(vmem, parts)], [(vmem, (PLANE, CHUNK, C1), BF16)])
+    (piece,) = call(group_sum, [(vmem, parts)], [(vmem, (1, CHUNK, C1), BF16)])
+    (piece,) = call(
+        depth_pair, [(vmem, piece), (vmem, swapped(piece, "kd", 0))], [(vmem, (1, CHUNK, C1), BF16)]
+    )
+    pieces = [piece]
+    for step in STEPS:
+        pairs = [
+            (source, (source + (2 * (source % 2) - 1) * step) % DEPTH)
+            for source in range(DEPTH)
+        ]
+        pieces.append(lax.ppermute(piece, "kd", pairs))
+    (copies,) = call(
+        depth_sum,
+        [(vmem, value) for value in pieces],
+        [(vmem, (PLANE, CHUNK, C1), BF16)],
+        [pltpu.VMEM((4, CHUNK, C1), BF16)],
+    )
     own = lax.all_to_all(copies, "scene", 0, 0, axis_index_groups=groups)
     own = own.reshape(PLANE * CHUNK, C1)
     other = swapped(own, "scene", 0)
     shapes = [(hbm, (7 * C1, C1), F32), (hbm, (8 * C1, C2), F32), (hbm, (7 * C2, C2), F32)]
-    scratch = [pltpu.VMEM((HALF, C1), F32), dma((3,))]
+    scratch = [pltpu.VMEM((HALF, C1), F32), dma((7,))]
     partial = call(functools.partial(unpack, False), [(vmem, own)], shapes, scratch)
     one, low, two = call(
         functools.partial(unpack, True),

time: 108 us -> 102 us (0.944)
  blocking collectives: 53.7 us -> 34.1 us
  waiting for transfers between devices: 5.78 us -> 13.2 us
  starting transfers between devices: 31.8 us -> 38 us
    all_to_all x1 -> x0, blocking collectives: 17.5 us -> none  [step(): parts = lax.all_to_all(copies, 'kd', 0, 0)]
    ppermute x0 -> x3, waiting for transfers between devices: none -> 6.15 us  [step(): pieces.append(lax.ppermute(piece, 'kd', pairs))]
    ppermute x0 -> x3, starting transfers between devices: none -> 5.1 us  [step(): pieces.append(lax.ppermute(piece, 'kd', pairs))]
    all_to_all x1, blocking collectives: 16 us -> 13.9 us  [step(): own = lax.all_to_all(copies, 'scene', 0, 0, axis_index_groups=groups)]
    ppermute x12, waiting for transfers between devices: 5.78 us -> 7.06 us  [swapped(): return lax.ppermute(value, axis, pairs)]
    pallas_call x12 -> x13, Pallas kernels: 15.3 us -> 15.2 us  [call(): pl.pallas_call(body, out_shape=[jax.ShapeDtypeStruct(shape, dtype) for _,...]
  transfers between devices with their start and end apart: 12 -> 15, of which waited for: 4 -> 7; matrix products, arithmetic and copies ran while one was open for 0% -> 0% of each run, Pallas kernels for 7% -> 7%
where the time goes in v5:
time: 102 us; the launch traced here: 101 us
  starting transfers between devices  38 us (37%)
  blocking collectives  34.1 us (33%)
  Pallas kernels  15.2 us (15%)
  waiting for transfers between devices  13.2 us (13%)
    ppermute x12, starting transfers between devices, swapped(): return lax.ppermute(value, axis, pairs)  32.9 us
    all_to_all x1, blocking collectives, step(): lax.all_to_all(packed.reshape(PLANE, CHUNK, C1), 'scene', 0, 0, axis_inde...  20.3 us
    pallas_call x13, Pallas kernels, call(): pl.pallas_call(body, out_shape=[jax.ShapeDtypeStruct(shape, dtype) for _,...  15.2 us
    all_to_all x1, blocking collectives, step(): own = lax.all_to_all(copies, 'scene', 0, 0, axis_index_groups=groups)  13.9 us
    ppermute x12, waiting for transfers between devices, swapped(): return lax.ppermute(value, axis, pairs)  7.06 us
    ppermute x3, waiting for transfers between devices, step(): pieces.append(lax.ppermute(piece, 'kd', pairs))  6.15 us
    ppermute x3, starting transfers between devices, step(): pieces.append(lax.ppermute(piece, 'kd', pairs))  5.1 us
  transfers between devices with their start and end apart: 15, of which 7 were waited for; matrix products, arithmetic and copies ran while one was open for 0% of the time, Pallas kernels for 7%

profile of v5, /device:TPU:1, one launch (start us, length us, event | category | flops | bytes accessed | tf_op | source)
XLA Modules:
  0.0 101.4 jit_solution(8713465498821137392)
XLA Ops:
  0.6 1.2 %shard_map.102 = (bf16[2048,128]{1,0:T(8,128)(2,1)S(1)}, s32[1,4,6]{2,1,0:T(4,128)S(1)}, s32[1,128]{1,0:T(1,128)S(1)}, bf16[64,128]{1,0:T(8,128)(2,1)S(1)}, bf16...) custom-call(bf16[2048,128]{1,0:T(8,128)(2,1)} %bitcast.15, s32[1,3]{1,0:T(1,128)} %bitcast.19, s32[1,4,6]{2,1,0:T(4,128)} %sources.1), custom_call_target="tpu_custom_call" | custom-call | tf_op jit(solution)/shard_map/pallas_call | solution.py:49
  1.8 2.5 %collective-permute-start = (bf16[64,128]{1,0:T(8,128)(2,1)S(1)}, bf16[64,128]{1,0:T(8,128)(2,1)S(1)}, u32[]{:S(2)}, u32[]{:S(2)}) collective-permute-start(bf16[64,128]{1,0:T(8,128)(2,1)S(1)} %get-tuple-element.45), channel_id=1, source_target_pairs={{0,1},{1,0},{2,3},{3,2},{4,5},{5,4},{6,7},{7,6},{8,9},{9,8},{10,11... | collective-permute-start | bytes 49160 | tf_op jit(solution)/shard_map/ppermute | solution.py:441
  4.4 3.0 %collective-permute-start.1 = (bf16[64,128]{1,0:T(8,128)(2,1)S(1)}, bf16[64,128]{1,0:T(8,128)(2,1)S(1)}, u32[]{:S(2)}, u32[]{:S(2)}) collective-permute-start(bf16[64,128]{1,0:T(8,128)(2,1)S(1)} %get-tuple-element.46), channel_id=1, source_target_pairs={{0,2},{1,3},{2,0},{3,1},{4,6},{5,7},{6,4},{7,5},{8,10},{9,11},{10,... | collective-permute-start | bytes 49160 | tf_op jit(solution)/shard_map/ppermute | solution.py:441
  7.4 4.2 %collective-permute-start.2 = (bf16[64,128]{1,0:T(8,128)(2,1)S(1)}, bf16[64,128]{1,0:T(8,128)(2,1)S(1)}, u32[]{:S(2)}, u32[]{:S(2)}) collective-permute-start(bf16[64,128]{1,0:T(8,128)(2,1)S(1)} %get-tuple-element.47), channel_id=1, source_target_pairs={{0,4},{1,5},{2,6},{3,7},{4,0},{5,1},{6,2},{7,3},{8,12},{9,13},{10,... | collective-permute-start | bytes 49160 | tf_op jit(solution)/shard_map/ppermute | solution.py:441
  11.6 2.6 %shard_map.103 = (bf16[2048,896]{1,0:T(8,128)(2,1)S(1)}, f32[2048,128]{1,0:T(8,128)S(1)}, bf16[896,128]{1,0:T(8,128)(2,1)S(1)}, bf16[1024,256]{1,0:T(8,128)(2,1)S(1)}) custom-call(s32[1,4,6]{2,1,0:T(4,128)S(1)} %get-tuple-element.42.source_ref, bf16[2048,128]{1,0:T(8,128)(2,1)S(1)} %get-tuple-element.44.field_near.field, bf16[896,128]{1,0:T(8,128)(2,1)} %bitcast.17, ...), custom_call_target="tpu_custom_call" | custom-call | tf_op jit(solution)/shard_map/pallas_call | solution.py:49
  14.2 0.0 collective-permute-done.got_0.rim_0
  14.2 0.0 collective-permute-done.1.got_1.rim_1
  14.2 0.0 collective-permute-done.2.got_2.rim_2
  14.3 1.8 %shard_map.104 = (f32[2048,128]{1,0:T(8,128)S(1)}, bf16[256,1024]{1,0:T(8,128)(2,1)S(1)}, bf16[256,256]{1,0:T(8,128)(2,1)S(1)}, bf16[16,256]{1,0:T(8,128)(2,1)S(...) custom-call(s32[1,128]{1,0:T(1,128)S(1)} %get-tuple-element.43.info_, ...), custom_call_target="tpu_custom_call" | custom-call | tf_op jit(solution)/shard_map/pallas_call | solution.py:49
  16.0 0.8 collective-permute-start.3
  16.8 1.2 %collective-permute-start.4 = (bf16[16,256]{1,0:T(8,128)(2,1)S(1)}, bf16[16,256]{1,0:T(8,128)(2,1)S(1)}, u32[]{:S(2)}, u32[]{:S(2)}) collective-permute-start(bf16[16,256]{1,0:T(8,128)(2,1)S(1)} %get-tuple-element.52), channel_id=1, source_target_pairs={{0,2},{1,3},{2,0},{3,1},{4,6},{5,7},{6,4},{7,5},{8,10},{9,11},{10,... | collective-permute-start | bytes 24584 | tf_op jit(solution)/shard_map/ppermute | solution.py:441
  18.0 3.8 %collective-permute-start.5 = (bf16[16,256]{1,0:T(8,128)(2,1)S(1)}, bf16[16,256]{1,0:T(8,128)(2,1)S(1)}, u32[]{:S(2)}, u32[]{:S(2)}) collective-permute-start(bf16[16,256]{1,0:T(8,128)(2,1)S(1)} %get-tuple-element.53), channel_id=1, source_target_pairs={{0,4},{1,5},{2,6},{3,7},{4,0},{5,1},{6,2},{7,3},{8,12},{9,13},{10,... | collective-permute-start | bytes 24584 | tf_op jit(solution)/shard_map/ppermute | solution.py:441
  21.8 1.4 %shard_map.105 = (bf16[256,1792]{1,0:T(8,128)(2,1)S(1)}, f32[2,256,128]{2,1,0:T(8,128)S(1)}, f32[2048,128]{1,0:T(8,128)S(1)}) custom-call(s32[1,4,6]{2,1,0:T(4,128)S(1)} %get-tuple-element.42.source_ref, bf16[256,256]{1,0:T(8,128)(2,1)S(1)} %get-tuple-element.56.coarse, bf16[1792,256]{1,0:T(8,128)(2,1)S(1)} %get-tuple-element.54.weight, ...), custom_call_target="tpu_custom_call" | custom-call | tf_op jit(solution)/shard_map/pallas_call | solution.py:49
  23.2 0.0 collective-permute-done.3.got_0
  23.2 0.0 collective-permute-done.4.got_1
  23.2 1.2 %collective-permute-done.5.got_2 = bf16[16,256]{1,0:T(8,128)(2,1)S(1)} collective-permute-done((bf16[16,256]{1,0:T(8,128)(2,1)S(1)}, bf16[16,256]{1,0:T(8,128)(2,1)S(1)}, u32[]{:S(2)}, u32[]{:S(2)}) %collective-permute-start.5) | collective-permute-done | bytes 8224 | tf_op jit(solution)/shard_map/ppermute | solution.py:441
  24.4 0.9 shard_map.106
  25.3 0.8 collective-permute-start.6
  26.2 1.2 %collective-permute-start.7 = (bf16[16,256]{1,0:T(8,128)(2,1)S(1)}, bf16[16,256]{1,0:T(8,128)(2,1)S(1)}, u32[]{:S(2)}, u32[]{:S(2)}) collective-permute-start(bf16[16,256]{1,0:T(8,128)(2,1)S(1)} %get-tuple-element.64), channel_id=1, source_target_pairs={{0,2},{1,3},{2,0},{3,1},{4,6},{5,7},{6,4},{7,5},{8,10},{9,11},{10,... | collective-permute-start | bytes 24584 | tf_op jit(solution)/shard_map/ppermute | solution.py:441
  27.4 3.8 %collective-permute-start.8 = (bf16[16,256]{1,0:T(8,128)(2,1)S(1)}, bf16[16,256]{1,0:T(8,128)(2,1)S(1)}, u32[]{:S(2)}, u32[]{:S(2)}) collective-permute-start(bf16[16,256]{1,0:T(8,128)(2,1)S(1)} %get-tuple-element.65), channel_id=1, source_target_pairs={{0,4},{1,5},{2,6},{3,7},{4,0},{5,1},{6,2},{7,3},{8,12},{9,13},{10,... | collective-permute-start | bytes 24584 | tf_op jit(solution)/shard_map/ppermute | solution.py:441
  31.1 2.2 %shard_map.107 = (f32[1792,128]{1,0:T(8,128)S(1)}, bf16[1792,128]{1,0:T(8,128)(2,1)S(1)}, bf16[256,256]{1,0:T(8,128)(2,1)}, f32[2,256,128]{2,1,0:T(8,128)S(1)}) custom-call(s32[1,4,6]{2,1,0:T(4,128)S(1)} %get-tuple-element.42.source_ref, s32[1,128]{1,0:T(1,128)S(1)} %get-tuple-element.43.info_ref, bf16[256,256]{1,0:T(8,128)(2,1)S(1)} %get-tuple-element.59.delta, ...), custom_call_target="tpu_custom_call" | custom-call | tf_op jit(solution)/shard_map/pallas_call | solution.py:49
  33.4 0.0 collective-permute-done.6.got_0
  33.4 0.0 collective-permute-done.7.got_1
  33.4 0.4 collective-permute-done.8.got_2
  33.8 2.2 %shard_map.108 = (f32[1472,128]{1,0:T(8,128)S(1)}, bf16[3264,128]{1,0:T(8,128)(2,1)S(1)}) custom-call(s32[1,128]{1,0:T(1,128)S(1)} %get-tuple-element.43.info_ref, bf16[16,256]{1,0:T(8,128)(2,1)S(1)} %collective-permute-done.6.got_0, bf16[16,256]{1,0:T(8,128)(2,1)S(1)} %collective-permute-done.7.got_1, bf16[16,256]{1,0:T(8,128)(2,1)S(1)} %collective-permute-done.8.got_2, ...), custom_call_target="tpu_custom_call" | custom-call | tf_op jit(solution)/shard_map/pallas_call | solution.py:49
  36.0 5.5 %collective-permute-start.9 = (bf16[3264,128]{1,0:T(8,128)(2,1)S(1)}, bf16[3264,128]{1,0:T(8,128)(2,1)S(1)}, u32[]{:S(2)}, u32[]{:S(2)}) collective-permute-start(bf16[3264,128]{1,0:T(8,128)(2,1)S(1)} %get-tuple-element.73), channel_id=1, source_target_pairs={{0,8},{8,0},{16,24},{24,16},{32,40},{40,32},{48,56},{56,48},{64,72... | collective-permute-start | bytes 2506760 | tf_op jit(solution)/shard_map/ppermute | solution.py:441
  41.4 2.0 %collective-permute-done.9.got = bf16[3264,128]{1,0:T(8,128)(2,1)S(1)} collective-permute-done((bf16[3264,128]{1,0:T(8,128)(2,1)S(1)}, bf16[3264,128]{1,0:T(8,128)(2,1)S(1)}, u32[]{:S(2)}, u32[]{:S(2)}) %collective-permute-start.9) | collective-permute-done | bytes 835616 | tf_op jit(solution)/shard_map/ppermute | solution.py:441
  43.4 0.2 shard_map.109
  43.6 20.3 %all_to_all.10.parts = bf16[16,208,128]{2,1,0:T(8,128)(2,1)S(1)} all-to-all(bf16[16,208,128]{2,1,0:T(8,128)(2,1)S(1)} %bitcast.12), channel_id=1, replica_groups={{0,16,32,48,64,80,96,112,128,144,160,176,192,208,224,240},{8,24,40,56,7..., dimensions={0} | all-to-all | bytes 1703936 | tf_op jit(solution)/shard_map/all_to_all | solution.py:543
  63.9 0.1 shard_map.110.own
  64.0 0.5 collective-permute-start.10
  64.5 2.7 %collective-permute-done.10.got = bf16[1,208,128]{2,1,0:T(8,128)(2,1)S(1)} collective-permute-done((bf16[1,208,128]{2,1,0:T(8,128)(2,1)S(1)}, bf16[1,208,128]{2,1,0:T(8,128)(2,1)S(1)}, u32[]{:S(2)}, u32[]{:S(2)}) %collective-permute-start.10) | collective-permute-done | bytes 53280 | tf_op jit(solution)/shard_map/ppermute | solution.py:441
  67.3 2.9 %collective-permute-start.13 = (bf16[1,208,128]{2,1,0:T(8,128)(2,1)S(1)}, bf16[1,208,128]{2,1,0:T(8,128)(2,1)S(1)}, u32[]{:S(2)}, u32[]{:S(2)}) collective-permute-start(bf16[1,208,128]{2,1,0:T(8,128)(2,1)S(1)} %shard_map.111.own), channel_id=1, source_target_pairs={{0,7},{1,2},{2,1},{3,4},{4,3},{5,6},{6,5},{7,0},{8,15},{9,10},{10,... | collective-permute-start | bytes 159752 | tf_op jit(solution)/shard_map/ppermute | solution.py:556
  70.2 1.2 %collective-permute-start.12 = (bf16[1,208,128]{2,1,0:T(8,128)(2,1)S(1)}, bf16[1,208,128]{2,1,0:T(8,128)(2,1)S(1)}, u32[]{:S(2)}, u32[]{:S(2)}) collective-permute-start(bf16[1,208,128]{2,1,0:T(8,128)(2,1)S(1)} %shard_map.111.own), channel_id=1, source_target_pairs={{0,6},{1,3},{2,0},{3,5},{4,2},{5,7},{6,4},{7,1},{8,14},{9,11},{10,... | collective-permute-start | bytes 159752 | tf_op jit(solution)/shard_map/ppermute | solution.py:556
  71.4 1.0 collective-permute-start.11
  72.4 0.0 collective-permute-done.13.got_1
  72.4 2.2 %collective-permute-done.12.got_2 = bf16[1,208,128]{2,1,0:T(8,128)(2,1)S(1)} collective-permute-done((bf16[1,208,128]{2,1,0:T(8,128)(2,1)S(1)}, bf16[1,208,128]{2,1,0:T(8,128)(2,1)S(1)}, u32[]{:S(2)}, u32[]{:S(2)}) %collective-permute-start.12) | collective-permute-done | bytes 53280 | tf_op jit(solution)/shard_map/ppermute | solution.py:556
  74.5 4.0 %collective-permute-done.11.got_3 = bf16[1,208,128]{2,1,0:T(8,128)(2,1)S(1)} collective-permute-done((bf16[1,208,128]{2,1,0:T(8,128)(2,1)S(1)}, bf16[1,208,128]{2,1,0:T(8,128)(2,1)S(1)}, u32[]{:S(2)}, u32[]{:S(2)}) %collective-permute-start.11) | collective-permute-done | bytes 53280 | tf_op jit(solution)/shard_map/ppermute | solution.py:556
  78.5 0.1 shard_map.112
  78.6 13.9 %all_to_all.11 = bf16[16,208,128]{2,1,0:T(8,128)(2,1)S(1)} all-to-all(bf16[16,208,128]{2,1,0:T(8,128)(2,1)S(1)} %shard_map.112), channel_id=1, replica_groups={{0,16,32,48,64,80,96,112,128,144,160,176,192,208,224,240},{8,24,40,56,7..., dimensions={0} | all-to-all | bytes 1703936 | tf_op jit(solution)/shard_map/all_to_all | solution.py:563
  92.5 5.6 %collective-permute-start.14 = (bf16[3328,128]{1,0:T(8,128)(2,1)S(1)}, bf16[3328,128]{1,0:T(8,128)(2,1)S(1)}, u32[]{:S(2)}, u32[]{:S(2)}) collective-permute-start(bf16[3328,128]{1,0:T(8,128)(2,1)S(1)} %bitcast.10), channel_id=1, source_target_pairs={{0,8},{8,0},{16,24},{24,16},{32,40},{40,32},{48,56},{56,48},{64,72... | collective-permute-start | bytes 2555912 | tf_op jit(solution)/shard_map/ppermute | solution.py:441
  98.0 1.2 %shard_map.113 = (f32[896,128]{1,0:T(8,128)}, f32[1024,256]{1,0:T(8,128)}, f32[1792,256]{1,0:T(8,128)}) custom-call(bf16[3328,128]{1,0:T(8,128)(2,1)S(1)} %bitcast.11), custom_call_target="tpu_custom_call" | custom-call | tf_op jit(solution)/shard_map/pallas_call | solution.py:49
  99.3 0.8 collective-permute-done.14.source
  100.0 1.2 %shard_map.114 = (f32[896,128]{1,0:T(8,128)}, f32[1024,256]{1,0:T(8,128)}, f32[1792,256]{1,0:T(8,128)}) custom-call(bf16[3328,128]{1,0:T(8,128)(2,1)S(1)} %collective-permute-done.14.source, f32[896,128]{1,0:T(8,128)} %get-tuple-element.74.refs_0_, ...), custom_call_target="tpu_custom_call", output_to_operand_aliasing={{0}: (1, {}), {1}: (2, {}), {2}: (3, {})} | custom-call | tf_op jit(solution)/shard_map/pallas_call | solution.py:49
  (1 shorter events, 0.0 us)
Async XLA Ops:
  1.8 12.4 %collective-permute-start = (bf16[64,128]{1,0:T(8,128)(2,1)S(1)}, bf16[64,128]{1,0:T(8,128)(2,1)S(1)}, u32[]{:S(2)}, u32[]{:S(2)}) collective-permute-start(bf16[64,128]{1,0:T(8,128)(2,1)S(1)} %get-tuple-element.45), channel_id=1, source_target_pairs={{0,1},{1,0},{2,3},{3,2},{4,5},{5,4},{6,7},{7,6},{8,9},{9,8},{10,11... | collective-permute-start | bytes 49160 | tf_op jit(solution)/shard_map/ppermute | solution.py:441
  4.4 9.9 %collective-permute-start.1 = (bf16[64,128]{1,0:T(8,128)(2,1)S(1)}, bf16[64,128]{1,0:T(8,128)(2,1)S(1)}, u32[]{:S(2)}, u32[]{:S(2)}) collective-permute-start(bf16[64,128]{1,0:T(8,128)(2,1)S(1)} %get-tuple-element.46), channel_id=1, source_target_pairs={{0,2},{1,3},{2,0},{3,1},{4,6},{5,7},{6,4},{7,5},{8,10},{9,11},{10,... | collective-permute-start | bytes 49160 | tf_op jit(solution)/shard_map/ppermute | solution.py:441
  7.4 6.9 %collective-permute-start.2 = (bf16[64,128]{1,0:T(8,128)(2,1)S(1)}, bf16[64,128]{1,0:T(8,128)(2,1)S(1)}, u32[]{:S(2)}, u32[]{:S(2)}) collective-permute-start(bf16[64,128]{1,0:T(8,128)(2,1)S(1)} %get-tuple-element.47), channel_id=1, source_target_pairs={{0,4},{1,5},{2,6},{3,7},{4,0},{5,1},{6,2},{7,3},{8,12},{9,13},{10,... | collective-permute-start | bytes 49160 | tf_op jit(solution)/shard_map/ppermute | solution.py:441
  16.0 7.2 %collective-permute-start.3 = (bf16[16,256]{1,0:T(8,128)(2,1)S(1)}, bf16[16,256]{1,0:T(8,128)(2,1)S(1)}, u32[]{:S(2)}, u32[]{:S(2)}) collective-permute-start(bf16[16,256]{1,0:T(8,128)(2,1)S(1)} %get-tuple-element.51), channel_id=1, source_target_pairs={{0,1},{1,0},{2,3},{3,2},{4,5},{5,4},{6,7},{7,6},{8,9},{9,8},{10,11... | collective-permute-start | bytes 24584 | tf_op jit(solution)/shard_map/ppermute | solution.py:441
  16.8 6.4 %collective-permute-start.4 = (bf16[16,256]{1,0:T(8,128)(2,1)S(1)}, bf16[16,256]{1,0:T(8,128)(2,1)S(1)}, u32[]{:S(2)}, u32[]{:S(2)}) collective-permute-start(bf16[16,256]{1,0:T(8,128)(2,1)S(1)} %get-tuple-element.52), channel_id=1, source_target_pairs={{0,2},{1,3},{2,0},{3,1},{4,6},{5,7},{6,4},{7,5},{8,10},{9,11},{10,... | collective-permute-start | bytes 24584 | tf_op jit(solution)/shard_map/ppermute | solution.py:441
  18.0 6.4 %collective-permute-start.5 = (bf16[16,256]{1,0:T(8,128)(2,1)S(1)}, bf16[16,256]{1,0:T(8,128)(2,1)S(1)}, u32[]{:S(2)}, u32[]{:S(2)}) collective-permute-start(bf16[16,256]{1,0:T(8,128)(2,1)S(1)} %get-tuple-element.53), channel_id=1, source_target_pairs={{0,4},{1,5},{2,6},{3,7},{4,0},{5,1},{6,2},{7,3},{8,12},{9,13},{10,... | collective-permute-start | bytes 24584 | tf_op jit(solution)/shard_map/ppermute | solution.py:441
  25.3 8.1 %collective-permute-start.6 = (bf16[16,256]{1,0:T(8,128)(2,1)S(1)}, bf16[16,256]{1,0:T(8,128)(2,1)S(1)}, u32[]{:S(2)}, u32[]{:S(2)}) collective-permute-start(bf16[16,256]{1,0:T(8,128)(2,1)S(1)} %get-tuple-element.63), channel_id=1, source_target_pairs={{0,1},{1,0},{2,3},{3,2},{4,5},{5,4},{6,7},{7,6},{8,9},{9,8},{10,11... | collective-permute-start | bytes 24584 | tf_op jit(solution)/shard_map/ppermute | solution.py:441
  26.2 7.2 %collective-permute-start.7 = (bf16[16,256]{1,0:T(8,128)(2,1)S(1)}, bf16[16,256]{1,0:T(8,128)(2,1)S(1)}, u32[]{:S(2)}, u32[]{:S(2)}) collective-permute-start(bf16[16,256]{1,0:T(8,128)(2,1)S(1)} %get-tuple-element.64), channel_id=1, source_target_pairs={{0,2},{1,3},{2,0},{3,1},{4,6},{5,7},{6,4},{7,5},{8,10},{9,11},{10,... | collective-permute-start | bytes 24584 | tf_op jit(solution)/shard_map/ppermute | solution.py:441
  27.4 6.4 %collective-permute-start.8 = (bf16[16,256]{1,0:T(8,128)(2,1)S(1)}, bf16[16,256]{1,0:T(8,128)(2,1)S(1)}, u32[]{:S(2)}, u32[]{:S(2)}) collective-permute-start(bf16[16,256]{1,0:T(8,128)(2,1)S(1)} %get-tuple-element.65), channel_id=1, source_target_pairs={{0,4},{1,5},{2,6},{3,7},{4,0},{5,1},{6,2},{7,3},{8,12},{9,13},{10,... | collective-permute-start | bytes 24584 | tf_op jit(solution)/shard_map/ppermute | solution.py:441
  36.0 7.4 %collective-permute-start.9 = (bf16[3264,128]{1,0:T(8,128)(2,1)S(1)}, bf16[3264,128]{1,0:T(8,128)(2,1)S(1)}, u32[]{:S(2)}, u32[]{:S(2)}) collective-permute-start(bf16[3264,128]{1,0:T(8,128)(2,1)S(1)} %get-tuple-element.73), channel_id=1, source_target_pairs={{0,8},{8,0},{16,24},{24,16},{32,40},{40,32},{48,56},{56,48},{64,72... | collective-permute-start | bytes 2506760 | tf_op jit(solution)/shard_map/ppermute | solution.py:441
  64.0 3.3 %collective-permute-start.10 = (bf16[1,208,128]{2,1,0:T(8,128)(2,1)S(1)}, bf16[1,208,128]{2,1,0:T(8,128)(2,1)S(1)}, u32[]{:S(2)}, u32[]{:S(2)}) collective-permute-start(bf16[1,208,128]{2,1,0:T(8,128)(2,1)S(1)} %shard_map.110.own), channel_id=1, source_target_pairs={{0,1},{1,0},{2,3},{3,2},{4,5},{5,4},{6,7},{7,6},{8,9},{9,8},{10,11... | collective-permute-start | bytes 159752 | tf_op jit(solution)/shard_map/ppermute | solution.py:441
  67.3 5.1 %collective-permute-start.13 = (bf16[1,208,128]{2,1,0:T(8,128)(2,1)S(1)}, bf16[1,208,128]{2,1,0:T(8,128)(2,1)S(1)}, u32[]{:S(2)}, u32[]{:S(2)}) collective-permute-start(bf16[1,208,128]{2,1,0:T(8,128)(2,1)S(1)} %shard_map.111.own), channel_id=1, source_target_pairs={{0,7},{1,2},{2,1},{3,4},{4,3},{5,6},{6,5},{7,0},{8,15},{9,10},{10,... | collective-permute-start | bytes 159752 | tf_op jit(solution)/shard_map/ppermute | solution.py:556
  70.2 4.3 %collective-permute-start.12 = (bf16[1,208,128]{2,1,0:T(8,128)(2,1)S(1)}, bf16[1,208,128]{2,1,0:T(8,128)(2,1)S(1)}, u32[]{:S(2)}, u32[]{:S(2)}) collective-permute-start(bf16[1,208,128]{2,1,0:T(8,128)(2,1)S(1)} %shard_map.111.own), channel_id=1, source_target_pairs={{0,6},{1,3},{2,0},{3,5},{4,2},{5,7},{6,4},{7,1},{8,14},{9,11},{10,... | collective-permute-start | bytes 159752 | tf_op jit(solution)/shard_map/ppermute | solution.py:556
  71.4 7.1 %collective-permute-start.11 = (bf16[1,208,128]{2,1,0:T(8,128)(2,1)S(1)}, bf16[1,208,128]{2,1,0:T(8,128)(2,1)S(1)}, u32[]{:S(2)}, u32[]{:S(2)}) collective-permute-start(bf16[1,208,128]{2,1,0:T(8,128)(2,1)S(1)} %shard_map.111.own), channel_id=1, source_target_pairs={{0,5},{1,4},{2,7},{3,6},{4,1},{5,0},{6,3},{7,2},{8,13},{9,12},{10,... | collective-permute-start | bytes 159752 | tf_op jit(solution)/shard_map/ppermute | solution.py:556
  92.5 7.6 %collective-permute-start.14 = (bf16[3328,128]{1,0:T(8,128)(2,1)S(1)}, bf16[3328,128]{1,0:T(8,128)(2,1)S(1)}, u32[]{:S(2)}, u32[]{:S(2)}) collective-permute-start(bf16[3328,128]{1,0:T(8,128)(2,1)S(1)} %bitcast.10), channel_id=1, source_target_pairs={{0,8},{8,0},{16,24},{24,16},{32,40},{40,32},{48,56},{56,48},{64,72... | collective-permute-start | bytes 2555912 | tf_op jit(solution)/shard_map/ppermute | solution.py:441
